TPU v7x, 128 devices: a whole 4x4x4 slice. The times are simulated.
128 devices in a mesh: stream: 16 (over y, x), span: 8 (over z, core).
Axes of the slice: x: 4, y: 4, z: 4, core: 2. Of those that a mesh axis runs over, the one named last changes fastest.
Arguments:
- fluid_pos: float32 [128, 64, 3, 128], P('stream', 'span'), may hold values from 0 to 1
- fluid_vel: float32 [128, 64, 3, 128], P('stream', 'span'), may hold values from -6 to 6
- fluid_mass: float32 [128, 64, 128], P('stream', 'span'), may hold values from 0.5 to 2
- fluid_count: int32 [128, 64], P('stream', 'span'), may hold values from 64 to 128
- clump_center: float32 [65536, 3], P(('stream', 'span')), may hold values from 0 to 1
- clump_vel: float32 [65536, 3], P(('stream', 'span')), may hold values from -6 to 6
- clump_arm: float32 [65536, 3, 128], P(('stream', 'span')), may hold values from -1.8 to 1.8
- margin_device: int32 [65536, 2], P(('stream', 'span')), may hold values from 0 to 127, all different within a row; in each aligned block of 512 rows (0 to 511, 512 to 1023, ...) at most 16 rows name the same one
- margin_block: int32 [65536, 2], P(('stream', 'span')), may hold values from 0 to 63
- margin_offset: float32 [65536, 2, 3], P(('stream', 'span')), may hold values from 0 to 1
- contact_partner: int32 [65536], P(('stream', 'span')), may hold values from 0 to 1023
Outputs:
- fluid_density: float32 [128, 64, 128], P('stream', 'span')
- clump_load: float32 [6, 65536], P(None, ('stream', 'span'))
Inputs may be any that keep to these rules, and one draw needn't show every extreme that they name: `margin_device`: among the 1024 margins of one device's clumps, at most 16 name any one device, and some device is named exactly 16 times; the two margins of a clump name different devices.
All inputs are finite; a program needn't handle non-finite values.
Results may differ from a plain program's by a relative error of at most 0.0001.
Values sent between devices are 32-bit elements; how exact they have to be, the bound alone decides.
No kernel may reach another device: no remote copies, remote signals or barrier semaphores. Data moves between devices by JAX's collectives and lax.ppermute only.
A program may use at most 128 MiB of HBM per device.

v0:
```python
import functools
import math

import jax
import jax.numpy as jnp
from jax import lax
from jax.experimental import pallas as pl
from jax.experimental.pallas import tpu as pltpu
from jax.sharding import PartitionSpec as P

H_SQ = 0.25
SIG_SQ = 0.5
DENS = 0.03125
DRAG = 0.002
STIFF = 0.005
LOG2E = math.log2(math.e)
C_FLUID = LOG2E / H_SQ
C_CONTACT = LOG2E / SIG_SQ
AXES = ("stream", "span")
W = 128
FEATS = 32
DEAD = -30000.0
BF = jnp.bfloat16
F32 = jnp.float32


def split3(v):
    hi = v.astype(BF).astype(F32)
    rest = v - hi
    mid = rest.astype(BF).astype(F32)
    return hi, mid, rest - mid


def norm_of(x, y, z, coef):
    return (x * x + y * y + z * z) * (-coef)


def left_rows(xs, ys, zs, norm):
    h, m, low = ([c[i] for c in (xs, ys, zs)] for i in range(3))
    one = jnp.ones_like(h[0])
    return h + h + h + m + m + low + list(split3(norm)) + [one, one, one]


def right_rows(xs, ys, zs, norm):
    h, m, low = ([c[i] for c in (xs, ys, zs)] for i in range(3))
    one = jnp.ones_like(h[0])
    return h + m + low + h + m + h + [one, one, one] + list(split3(norm))


def put_rows(ref, rows, base=0):
    for i, row in enumerate(rows):
        ref[base + 8 * i : base + 8 * i + 8, :] = row


def zero_tail(ref, base=0):
    zero = jnp.zeros((8, W), F32)
    for i in range(24, FEATS):
        ref[base + 8 * i : base + 8 * i + 8, :] = zero


def take_rows(ref, j, base=0):
    return ref[pl.ds(base + j, FEATS, stride=8), :]


def gauss(left, right):
    return jnp.exp2(jnp.dot(left, right, preferred_element_type=F32))


def two_halves(kernel):
    hi = kernel.astype(BF)
    lo = (kernel - hi.astype(F32)).astype(BF)
    return jnp.concatenate([hi, lo], axis=0)


def lane_sum(v):
    return jnp.sum(v, axis=1, keepdims=True)


def prep_kernel(dev_ref, blk_ref, dev_s, off_s, arm_ref, first_ref, second_ref, ids_ref, rank_ref,
                buf, rank_s, sems):
    entries = dev_ref.shape[1]
    parts = entries // W
    dev = dev_ref[...]
    row = lax.broadcasted_iota(jnp.int32, (W, entries), 0)
    hot = (row == dev).astype(F32)
    hot_b = hot.astype(BF)
    up = lax.broadcasted_iota(jnp.int32, (W, 2 * W), 0)
    lane = lax.broadcasted_iota(jnp.int32, (W, 2 * W), 1)
    tri = jnp.where(lane >= W, 1.0, jnp.where(up < lane, 1.0, 0.0)).astype(BF)
    carry = jnp.zeros((W, W), F32)
    ranks = []
    for part in range(parts):
        piece = slice(part * W, part * W + W)
        both = jnp.dot(hot_b[:, piece], tri, preferred_element_type=F32)
        ranks.append(jnp.sum(hot[:, piece] * (both[:, :W] + carry), axis=0, keepdims=True))
        carry = carry + both[:, W:]
    rank = jnp.concatenate(ranks, axis=1).astype(jnp.int32)
    rank_ref[...] = rank
    move = pltpu.make_async_copy(rank_ref, rank_s, sems.at[0])
    move.start()
    named = jnp.where(row == rank, blk_ref[...] + 1, 0).astype(F32).astype(BF)
    ids = lax.dot_general(hot_b, named, (((1,), (1,)), ((), ())), preferred_element_type=F32)
    ids_ref[...] = ids.astype(jnp.int32) - 1
    move.wait()

    clumps = entries // 2

    def step(i, carry):
        for k in range(2):
            for j in range(8):
                c = i * 8 + j
                e = k * clumps + c
                d = dev_s[0, e]
                r = rank_s[0, e]
                base = ((r >> 3) * W + d) * 24 + (r & 7)
                for q in range(3):
                    buf[pl.ds(base + 8 * q, 1), :] = (
                        arm_ref[q, pl.ds(c, 1), :] + off_s[q, e]
                    )
        return carry

    lax.fori_loop(0, clumps // 8, step, 0)
    half = W * 24
    one = pltpu.make_async_copy(buf.at[pl.ds(0, half)], first_ref, sems.at[0])
    two = pltpu.make_async_copy(buf.at[pl.ds(half, half)], second_ref, sems.at[1])
    one.start()
    two.start()
    one.wait()
    two.wait()


def prep(dev, blk, off, arms):
    entries = dev.shape[1]
    vm = pl.BlockSpec(memory_space=pltpu.VMEM)
    sm = pl.BlockSpec(memory_space=pltpu.SMEM)
    hbm = pl.BlockSpec(memory_space=pl.ANY)
    send = jax.ShapeDtypeStruct((W * 24, W), F32)
    return pl.pallas_call(
        prep_kernel,
        out_shape=(
            send,
            send,
            jax.ShapeDtypeStruct((W, W), jnp.int32),
            jax.ShapeDtypeStruct((1, entries), jnp.int32),
        ),
        in_specs=[vm, vm, sm, sm, vm],
        out_specs=(hbm, hbm, vm, vm),
        scratch_shapes=[
            pltpu.VMEM((2 * W * 24, W), F32),
            pltpu.SMEM((1, entries), jnp.int32),
            pltpu.SemaphoreType.DMA((2,)),
        ],
        compiler_params=pltpu.CompilerParams(vmem_limit_bytes=24 << 20),
        name="prep",
    )(dev, blk, dev, off, arms)


def density_kernel(ext_ref, own_ref, mass_ref, vel_ref, dens_ref, table_ref, amp_ref,
                   feat, right, sums, left, wide):
    rows_y = 8
    zero_tail(feat)
    for s in range(9):
        zero_tail(right, s * FEATS * 8)

    def coords(ref, at):
        return [ref[q, pl.ds(at, 8), :] - 0.5 for q in range(3)]

    def ext_group(g, carry):
        at = pl.multiple_of(g * 8, 8)
        x, y, z = coords(ext_ref, at)
        m = ext_ref[3, pl.ds(at, 8), :]
        logm = jnp.where(m > 0.0, jnp.log2(jnp.where(m > 0.0, m, 1.0)), DEAD)
        norm = norm_of(x, y, z, C_FLUID) + logm
        put_rows(feat, left_rows(split3(x), split3(y), split3(z), norm))
        for j in range(8):
            left[at + j] = jnp.transpose(take_rows(feat, j)).astype(BF)
        return carry

    lax.fori_loop(0, ext_ref.shape[1] // 8, ext_group, 0)

    def own_row(a, carry):
        at = pl.multiple_of(a * 8, 8)
        x, y, z = coords(own_ref, at)
        xs = [x + 1.0, x, x - 1.0]
        ys = [y + 1.0, y, y - 1.0]
        scale = 2.0 * C_FLUID
        xsplit = [split3(v * scale) for v in xs]
        ysplit = [split3(v * scale) for v in ys]
        zsplit = split3(z * scale)
        for ix in range(3):
            for iy in range(3):
                norm = norm_of(xs[ix], ys[iy], z, C_FLUID)
                put_rows(right, right_rows(xsplit[ix], ysplit[iy], zsplit, norm),
                         (ix * 3 + iy) * FEATS * 8)

        def block(b, inner):
            total = jnp.zeros((8, W), F32)
            for ix in range(3):
                for iy in range(3):
                    rhs = take_rows(right, b, (ix * 3 + iy) * FEATS * 8).astype(BF)
                    lhs = left[(a + ix) * 10 + b + iy]
                    total = total + jnp.sum(gauss(lhs, rhs).reshape(16, 8, W), axis=0)
            sums[pl.ds(b, 1), :] = jnp.sum(total, axis=0, keepdims=True)
            return inner

        lax.fori_loop(0, rows_y, block, 0)
        density = DENS * (mass_ref[pl.ds(at, 8), :] + sums[...])
        dens_ref[pl.ds(at, 8), :] = density
        weight = own_ref[3, pl.ds(at, 8), :] / density
        parts = [vel_ref[q, pl.ds(at, 8), :] * weight for q in range(3)] + [weight]
        zero = jnp.zeros((8, W), F32)
        for q, v in enumerate(parts):
            hi = v.astype(BF).astype(F32)
            wide[8 * q : 8 * q + 8, :] = hi
            wide[8 * (q + 8) : 8 * (q + 8) + 8, :] = v - hi
        for q in (4, 5, 6, 7, 12, 13, 14, 15):
            wide[8 * q : 8 * q + 8, :] = zero
        norm = norm_of(x, y, z, C_FLUID)
        put_rows(feat, left_rows(split3(x), split3(y), split3(z), norm))
        upper = lax.broadcasted_iota(jnp.int32, (16, W), 0) < 8
        for j in range(8):
            table_ref[at + j] = jnp.transpose(take_rows(feat, j)).astype(BF)
            a16 = wide[pl.ds(j, 16, stride=8), :]
            amp_ref[at + j, :, 0:W] = a16.astype(BF)
            amp_ref[at + j, :, W : 2 * W] = jnp.where(upper, a16, 0.0).astype(BF)
        return carry

    lax.fori_loop(0, 8, own_row, 0)


def density(ext, own, mass, vel):
    blocks = mass.shape[0]
    vm = pl.BlockSpec(memory_space=pltpu.VMEM)
    return pl.pallas_call(
        density_kernel,
        out_shape=(
            jax.ShapeDtypeStruct((blocks, W), F32),
            jax.ShapeDtypeStruct((blocks, W, FEATS), BF),
            jax.ShapeDtypeStruct((blocks, 16, 2 * W), BF),
        ),
        in_specs=[vm] * 4,
        out_specs=(vm, vm, vm),
        scratch_shapes=[
            pltpu.VMEM((FEATS * 8, W), F32),
            pltpu.VMEM((9 * FEATS * 8, W), F32),
            pltpu.VMEM((8, W), F32),
            pltpu.VMEM((ext.shape[1], W, FEATS), BF),
            pltpu.VMEM((W, W), F32),
        ],
        compiler_params=pltpu.CompilerParams(vmem_limit_bytes=24 << 20),
        name="density",
    )(ext, own, mass, vel)


def columns_to_lanes(cols):
    lane = lax.broadcasted_iota(jnp.int32, (8, W), 1)
    out = jnp.zeros((8, W), F32)
    for q, col in enumerate(cols):
        out = jnp.where(lane == q, col, out)
    return out


def contact_kernel(partner_s, arm_ref, world_ref, next_ref, out_ref, cand, gat, feat, right, lead, acc):
    clumps = arm_ref.shape[1]
    cand[:, 0:clumps, :] = world_ref[...]
    cand[:, clumps : 2 * clumps, :] = next_ref[...]
    zero_tail(feat)
    zero_tail(right)
    zero = jnp.zeros((8, W), F32)
    for q in (4, 5, 6, 7, 12, 13, 14, 15):
        lead[8 * q : 8 * q + 8, :] = zero
    upper = lax.broadcasted_iota(jnp.int32, (16, W), 0) < 8

    def group(g, carry):
        at = pl.multiple_of(g * 8, 8)
        for j in range(8):
            p = partner_s[0, at + j]
            for q in range(3):
                gat[8 * q + j : 8 * q + j + 1, :] = cand[q, pl.ds(p, 1), :]
        zb = [gat[8 * q : 8 * q + 8, :] - 0.5 for q in range(3)]
        za = [world_ref[q, pl.ds(at, 8), :] - 0.5 for q in range(3)]
        put_rows(feat, left_rows(*[split3(v) for v in zb], norm_of(*zb, C_CONTACT)))
        scaled = [split3(v * (2.0 * C_CONTACT)) for v in za]
        put_rows(right, right_rows(*scaled, norm_of(*za, C_CONTACT)))
        for q, v in enumerate(zb + [jnp.ones((8, W), F32)]):
            hi = v.astype(BF).astype(F32)
            lead[8 * q : 8 * q + 8, :] = hi
            lead[8 * (q + 8) : 8 * (q + 8) + 8, :] = v - hi
        for j in range(8):
            lhs = jnp.transpose(take_rows(feat, j)).astype(BF)
            kernel = gauss(lhs, take_rows(right, j).astype(BF))
            l16 = lead[pl.ds(j, 16, stride=8), :]
            both = jnp.concatenate([l16, jnp.where(upper, l16, 0.0)], axis=1).astype(BF)
            res = jnp.dot(both, two_halves(kernel), preferred_element_type=F32)
            acc[8 * j : 8 * j + 8, :] = res[0:8] + res[8:16]
        s = [acc[pl.ds(q, 8, stride=8), :] for q in range(4)]
        f = [STIFF * (za[q] * s[3] - s[q]) for q in range(3)]
        arm = [arm_ref[q, pl.ds(at, 8), :] for q in range(3)]
        t = [arm[1] * f[2] - arm[2] * f[1], arm[2] * f[0] - arm[0] * f[2],
             arm[0] * f[1] - arm[1] * f[0]]
        out_ref[pl.ds(at, 8), :] = columns_to_lanes([lane_sum(v) for v in f + t])
        return carry

    lax.fori_loop(0, clumps // 8, group, 0)


def contact(partner, arms, world, following):
    clumps = arms.shape[1]
    vm = pl.BlockSpec(memory_space=pltpu.VMEM)
    sm = pl.BlockSpec(memory_space=pltpu.SMEM)
    return pl.pallas_call(
        contact_kernel,
        out_shape=jax.ShapeDtypeStruct((clumps, W), F32),
        in_specs=[sm, vm, vm, vm],
        out_specs=vm,
        scratch_shapes=[
            pltpu.VMEM((3, 2 * clumps, W), F32),
            pltpu.VMEM((24, W), F32),
            pltpu.VMEM((FEATS * 8, W), F32),
            pltpu.VMEM((FEATS * 8, W), F32),
            pltpu.VMEM((W, W), F32),
            pltpu.VMEM((64, W), F32),
        ],
        compiler_params=pltpu.CompilerParams(vmem_limit_bytes=24 << 20),
        name="contact",
    )(partner, arms, world, following)


def fluid_kernel(first, ids_s, y_ref, table_ref, amp_ref, out_ref, right, acc):
    zero_tail(right)
    lane = lax.broadcasted_iota(jnp.int32, (8, W), 1)
    mine = (lane >> 4) == lax.broadcasted_iota(jnp.int32, (8, W), 0)
    place = lane & 15

    def group(g, carry):
        at = pl.multiple_of(g * 24, 8)
        y = [y_ref[pl.ds(at + 8 * q, 8), :] for q in range(3)]
        u = [v - 0.5 for v in y]
        scaled = [split3(v * (2.0 * C_FLUID)) for v in u]
        put_rows(right, right_rows(*scaled, norm_of(*u, C_FLUID)))
        valid = jnp.zeros((1, W), jnp.int32)
        for j in range(8):
            name = ids_s[g, first + j]
            valid = jnp.where((lane[0:1] >> 4) == j, name, valid)
            b = jnp.maximum(name, 0)
            kernel = gauss(table_ref[b], take_rows(right, j).astype(BF))
            res = jnp.dot(amp_ref[b], two_halves(kernel), preferred_element_type=F32)
            acc[8 * j : 8 * j + 8, :] = res[0:8] + res[8:16]
        s = [acc[pl.ds(q, 8, stride=8), :] for q in range(4)]
        cross = [y[1] * s[2] - y[2] * s[1], y[2] * s[0] - y[0] * s[2], y[0] * s[1] - y[1] * s[0]]
        moment = [y[q] * s[3] for q in range(3)]
        out = jnp.zeros((8, W), F32)
        for q, v in enumerate(s + cross + moment):
            out = jnp.where(place == q, lane_sum(v), out)
        row = jnp.sum(jnp.where(mine, out, 0.0), axis=0, keepdims=True)
        out_ref[pl.ds(g, 1), :] = jnp.where(valid >= 0, row, 0.0)
        return carry

    lax.fori_loop(0, out_ref.shape[0], group, 0)


def fluid(first, ids, spots, table, amp):
    vm = pl.BlockSpec(memory_space=pltpu.VMEM)
    sm = pl.BlockSpec(memory_space=pltpu.SMEM)
    return pl.pallas_call(
        functools.partial(fluid_kernel, first),
        out_shape=jax.ShapeDtypeStruct((W, W), F32),
        in_specs=[sm, vm, vm, vm],
        out_specs=vm,
        scratch_shapes=[pltpu.VMEM((FEATS * 8, W), F32), pltpu.VMEM((64, W), F32)],
        compiler_params=pltpu.CompilerParams(vmem_limit_bytes=24 << 20),
        name="fluid",
    )(ids, spots, table, amp)


def combine_kernel(dev_ref, rank_ref, off_ref, vel_ref, one_ref, two_ref, contact_ref, out_ref):
    entries = dev_ref.shape[1]
    clumps = entries // 2
    row = lax.broadcasted_iota(jnp.int32, (W, entries), 0)
    hot = (row == dev_ref[...]).astype(BF)
    rank = rank_ref[...]
    picked = jnp.zeros((16, entries), F32)
    for chunk, ref in enumerate((one_ref, two_ref)):
        spread = jnp.zeros((W, entries), F32)
        for part in split3(jnp.transpose(ref[...])):
            spread = spread + jnp.dot(part.astype(BF), hot, preferred_element_type=F32)
        spread = jnp.where((row >> 4) + 8 * chunk == rank, spread, 0.0)
        picked = picked + jnp.sum(spread.reshape(8, 16, entries), axis=0)
    touch = jnp.transpose(contact_ref[...])
    total = [touch[q : q + 1, :] for q in range(6)]
    v = [vel_ref[q : q + 1, :] for q in range(3)]
    for k in range(2):
        part = slice(k * clumps, k * clumps + clumps)
        g = [picked[q : q + 1, part] for q in range(10)]
        off = [off_ref[q : q + 1, part] for q in range(3)]
        f = [g[q] - v[q] * g[3] for q in range(3)]
        m = g[7:10]
        for q in range(3):
            a, b = (q + 1) % 3, (q + 2) % 3
            t = g[4 + q] - (m[a] * v[b] - m[b] * v[a]) - (off[a] * f[b] - off[b] * f[a])
            total[q] = total[q] + DRAG * f[q]
            total[3 + q] = total[3 + q] + DRAG * t
    for q in range(6):
        out_ref[q : q + 1, :] = total[q]


def combine(dev, rank, off, vel, one, two, touch):
    vm = pl.BlockSpec(memory_space=pltpu.VMEM)
    return pl.pallas_call(
        combine_kernel,
        out_shape=jax.ShapeDtypeStruct((6, vel.shape[1]), F32),
        in_specs=[vm] * 7,
        out_specs=vm,
        compiler_params=pltpu.CompilerParams(vmem_limit_bytes=24 << 20),
        name="combine",
    )(dev, rank, off, vel, one, two, touch)


def extended(cells, sides):
    for axis, dim in sides:
        count = lax.axis_size(axis)
        ends = count - 1
        head = lax.slice_in_dim(cells, 0, 1, axis=dim)
        tail = lax.slice_in_dim(cells, cells.shape[dim] - 1, cells.shape[dim], axis=dim)
        cells = jnp.concatenate(
            [
                lax.ppermute(tail, axis, [(i, (i + 1) % count) for i in range(ends)]),
                cells,
                lax.ppermute(head, axis, [((i + 1) % count, i) for i in range(ends)]),
            ],
            axis=dim,
        )
    return cells


def swap_all(array):
    return lax.all_to_all(array, AXES, split_axis=0, concat_axis=0, tiled=True)


def body(
    fluid_pos,
    fluid_vel,
    fluid_mass,
    fluid_count,
    clump_center,
    clump_vel,
    clump_arm,
    margin_device,
    margin_block,
    margin_offset,
    contact_partner,
):
    rows_x, rows_y, width = fluid_mass.shape
    blocks = rows_x * rows_y
    clumps = clump_arm.shape[0]
    entries = 2 * clumps
    devices = lax.axis_size(AXES)
    arms = jnp.transpose(clump_arm, (1, 0, 2))
    dev = margin_device.T.reshape(1, entries)
    blk = margin_block.T.reshape(1, entries)
    off = jnp.transpose(margin_offset, (2, 1, 0)).reshape(3, entries)
    vel = clump_vel.T
    first, second, ids, rank = prep(dev, blk, off, arms)
    names = swap_all(ids)
    got_first = swap_all(first.reshape(devices, 24, width))
    got_second = swap_all(second.reshape(devices, 24, width))
    world = arms + clump_center.T[:, :, None]
    following = lax.ppermute(world, AXES, [(i, (i + devices - 1) % devices) for i in range(devices)])
    touch = contact(contact_partner.reshape(1, clumps), arms, world, following)
    lanes = jnp.arange(width, dtype=jnp.int32)
    live = jnp.where(lanes[None, None, :] < fluid_count[..., None], fluid_mass, 0.0)
    planes = jnp.concatenate([jnp.moveaxis(fluid_pos, 2, 0), live[None]], axis=0)
    ext = extended(planes, (("stream", 1), ("span", 2)))
    ext = ext.reshape(4, (rows_x + 2) * (rows_y + 2), width)
    ext = jnp.pad(ext, ((0, 0), (0, 4), (0, 0)))
    own = planes.reshape(4, blocks, width)
    speed = jnp.moveaxis(fluid_vel, 2, 0).reshape(3, blocks, width)
    dens, table, amp = density(ext, own, fluid_mass.reshape(blocks, width), speed)
    one = swap_all(fluid(0, names, got_first.reshape(devices * 24, width), table, amp))
    two = swap_all(fluid(8, names, got_second.reshape(devices * 24, width), table, amp))
    loads = combine(dev, rank, off, vel, one, two, touch)
    return (dens.reshape(rows_x, rows_y, width), loads)


def solution(mesh):
    in_specs = (
        P("stream", "span", None, None),
        P("stream", "span", None, None),
        P("stream", "span", None),
        P("stream", "span"),
        P(("stream", "span"), None),
        P(("stream", "span"), None),
        P(("stream", "span"), None, None),
        P(("stream", "span"), None),
        P(("stream", "span"), None),
        P(("stream", "span"), None, None),
        P(("stream", "span")),
    )
    out_specs = (P("stream", "span", None), P(None, ("stream", "span")))
    return jax.shard_map(body, mesh=mesh, in_specs=in_specs, out_specs=out_specs, check_vma=False)
```

profile of v0, /device:TPU:1, one launch (start us, length us, event | category | flops | bytes accessed | tf_op | source)
XLA Modules:
  0.0 314.2 jit_solution(4273590708776932527)
XLA Ops:
  0.6 0.0 copy-start
  0.6 0.7 copy.32
  1.4 0.7 copy.30
  2.1 0.7 copy.31
  2.8 1.1 copy-done.1
  3.9 10.0 %prep.1 = (f32[3072,128]{1,0:T(8,128)}, f32[3072,128]{1,0:T(8,128)S(1)}, s32[128,128]{1,0:T(8,128)S(1)}, s32[1,1024]{1,0:T(1,128)S(1)}) custom-call(s32[1,1024]{1,0:T(1,128)S(1)} %bitcast.63, s32[1,1024]{1,0:T(1,128)S(1)} %bitcast.67, s32[1,1024]{1,0:T(1,128)S(1)} %bitcast.64, f32[3,1024]{1,0:T(4,128)S(1)} %bitcast.60, f32[3,512,128]{2,1,0:T(8,128)S(1)} %bitcast.51), custom_call_target="tpu_custom_call" | custom-call | tf_op jit(solution)/shard_map/prep/pallas_call | solution.py:138
  14.0 21.1 %all_to_all.43 = s32[128,1,128]{2,1,0:T(1,128)} all-to-all(s32[128,1,128]{2,1,0:T(1,128)S(1)} %bitcast.66), channel_id=1, replica_groups=mesh['stream'=16,'span'=8] {'stream','span'}, dimensions={0} | all-to-all | bytes 131072 | tf_op jit(solution)/shard_map/all_to_all | solution.py:437
  35.0 29.4 %all_to_all.44 = f32[128,24,128]{2,1,0:T(8,128)} all-to-all(f32[128,24,128]{2,1,0:T(8,128)S(1)} %bitcast.54), channel_id=1, replica_groups=mesh['stream'=16,'span'=8] {'stream','span'}, dimensions={0} | all-to-all | bytes 3145728 | tf_op jit(solution)/shard_map/all_to_all | solution.py:437
  64.5 0.0 copy-done.9
  64.5 0.0 copy-start.15
  64.5 0.0 copy-start.2
  64.5 0.0 copy-start.16
  64.5 5.8 %all-to-all-start.1 = ((f32[128,24,128]{2,1,0:T(8,128)}), f32[128,24,128]{2,1,0:T(8,128)}, u32[]{:S(2)}, u32[]{:S(2)}) async-start(f32[128,24,128]{2,1,0:T(8,128)} %bitcast.18), calls=%async_computation.1 | async-start | bytes 3145728 | tf_op jit(solution)/shard_map/all_to_all | solution.py:437
  70.4 0.0 copy-done.8
  70.4 0.0 copy-done.17
  70.4 0.1 fusion.1
  70.5 3.3 %collective-permute-start = (f32[4,1,8,128]{3,2,0,1:T(8,128)S(1)}, f32[4,1,8,128]{3,2,0,1:T(8,128)S(1)}, u32[]{:S(2)}, u32[]{:S(2)}) collective-permute-start(f32[4,1,8,128]{3,2,0,1:T(8,128)S(1)} %get-tuple-element.18), channel_id=1, source_target_pairs={{0,8},{8,16},{16,24},{24,32},{32,40},{40,48},{48,56},{56,64},{64,7... | collective-permute-start | bytes 49160 | tf_op jit(solution)/shard_map/ppermute | solution.py:427
  73.8 1.3 collective-permute-start.1
  75.1 0.0 copy-done.2
  75.1 0.0 copy-done.16
  75.1 1.2 broadcast_add_fusion.world_ref
  76.3 0.6 collective-permute-start.4
  76.9 0.0 copy-done
  77.0 8.7 %collective-permute-done = f32[4,1,8,128]{3,2,0,1:T(8,128)S(1)} collective-permute-done((f32[4,1,8,128]{3,2,0,1:T(8,128)S(1)}, f32[4,1,8,128]{3,2,0,1:T(8,128)S(1)}, u32[]{:S(2)}, u32[]{:S(2)}) %collective-permute-start) | collective-permute-done | bytes 16416 | tf_op jit(solution)/shard_map/ppermute | solution.py:427
  85.7 3.1 collective-permute-done.1
  88.8 4.0 %collective-permute-start.2 = (f32[4,10,1,128]{3,2,0,1:T(1,128)S(1)}, f32[4,10,1,128]{3,2,0,1:T(1,128)S(1)}, u32[]{:S(2)}, u32[]{:S(2)}) collective-permute-start(f32[4,10,1,128]{3,2,0,1:T(1,128)S(1)} %get-tuple-element.16), channel_id=1, source_target_pairs={{0,1},{1,2},{2,3},{3,4},{4,5},{5,6},{6,7},{8,9},{9,10},{10,11},{11... | collective-permute-start | bytes 61448 | tf_op jit(solution)/shard_map/ppermute | solution.py:427
  92.8 1.9 collective-permute-start.3
  94.8 0.0 collective-permute-done.2
  94.8 4.2 %collective-permute-done.3 = f32[4,10,1,128]{3,2,0,1:T(1,128)S(1)} collective-permute-done((f32[4,10,1,128]{3,2,0,1:T(1,128)S(1)}, f32[4,10,1,128]{3,2,0,1:T(1,128)S(1)}, u32[]{:S(2)}, u32[]{:S(2)}) %collective-permute-start.3) | collective-permute-done | bytes 20512 | tf_op jit(solution)/shard_map/ppermute | solution.py:429
  99.0 0.1 pad_maximum_fusion
  99.0 0.1 copy.23
  99.2 19.8 %density.1 = (f32[64,128]{1,0:T(8,128)}, bf16[64,128,32]{2,1,0:T(8,128)(2,1)S(1)}, bf16[64,16,256]{2,1,0:T(8,128)(2,1)S(1)}) custom-call(f32[4,104,128]{2,1,0:T(8,128)S(1)} %pad.4.ext_ref, f32[4,64,128]{2,1,0:T(8,128)S(1)} %pad_maximum_fusion.1.own_ref, f32[64,128]{1,0:T(8,128)S(1)} %bitcast.62, f32[3,64,128]{2,1,0:T(8,128)S(1)} %copy_bitcast_fusion.vel_ref), custom_call_target="tpu_custom_call" | custom-call | tf_op jit(solution)/shard_map/density/pallas_call | solution.py:234
  119.0 0.0 copy-done.3
  119.0 66.4 %fluid.3 = f32[128,128]{1,0:T(8,128)S(1)} custom-call(s32[128,128]{1,0:T(8,128)S(1)} %bitcast.55, f32[3072,128]{1,0:T(8,128)S(1)} %bitcast.53, bf16[64,128,32]{2,1,0:T(8,128)(2,1)S(1)} %get-tuple-element.13.table_ref, bf16[64,16,256]{2,1,0:T(8,128)(2,1)S(1)} %get-tuple-element.14.amp_ref), custom_call_target="tpu_custom_call" | custom-call | tf_op jit(solution)/shard_map/fluid/pallas_call | solution.py:365
  185.4 0.6 copy-done.7
  186.0 0.0 all-to-all-done.1
  186.0 8.3 %all-to-all-start.4 = ((f32[128,1,128]{2,1,0:T(1,128)}), f32[128,1,128]{2,1,0:T(1,128)}, u32[]{:S(2)}, u32[]{:S(2)}) async-start(f32[128,1,128]{2,1,0:T(1,128)} %bitcast.58), calls=%async_computation.4 | async-start | bytes 131072 | tf_op jit(solution)/shard_map/all_to_all | solution.py:437
  194.3 0.0 copy-start.5
  194.3 0.8 copy-done.5
  195.1 66.4 %fluid.2 = f32[128,128]{1,0:T(8,128)S(1)} custom-call(s32[128,128]{1,0:T(8,128)S(1)} %bitcast.56, f32[3072,128]{1,0:T(8,128)} %bitcast.19.y_ref, bf16[64,128,32]{2,1,0:T(8,128)(2,1)S(1)} %get-tuple-element.13.table_ref, bf16[64,16,256]{2,1,0:T(8,128)(2,1)S(1)} %get-tuple-element.14.amp_ref), custom_call_target="tpu_custom_call" | custom-call | tf_op jit(solution)/shard_map/fluid/pallas_call | solution.py:365
  261.5 0.6 copy-done.6
  262.1 0.0 all-to-all-done.4
  262.2 9.8 %all-to-all-start.2 = ((f32[128,1,128]{2,1,0:T(1,128)}), f32[128,1,128]{2,1,0:T(1,128)S(1)}, u32[]{:S(2)}, u32[]{:S(2)}) async-start(f32[128,1,128]{2,1,0:T(1,128)} %bitcast.57), calls=%async_computation.2 | async-start | bytes 131072 | tf_op jit(solution)/shard_map/all_to_all | solution.py:437
  271.9 0.0 collective-permute-done.4.next_ref
  271.9 0.0 copy-done.14
  272.0 40.0 %contact.1.contact_ref = f32[512,128]{1,0:T(8,128)S(1)} custom-call(s32[1,512]{1,0:T(1,128)S(1)} %bitcast.69, f32[3,512,128]{2,1,0:T(8,128)S(1)} %bitcast.52, f32[3,512,128]{2,1,0:T(8,128)} %broadcast_add_fusion.world_ref, f32[3,512,128]{2,1,0:T(8,128)} %collective-permute-done.4.next_ref), custom_call_target="tpu_custom_call" | custom-call | tf_op jit(solution)/shard_map/contact/pallas_call | solution.py:311
  312.0 0.0 all-to-all-done.2
  312.0 2.1 combine.1
  (26 shorter events, 0.1 us)
Async XLA Ops:
  0.6 76.3 %copy-start = (f32[8,8,3,128]{3,1,2,0:T(8,128)S(1)}, f32[8,8,3,128]{3,1,2,0:T(8,128)}, u32[]{:S(2)}) copy-start(f32[8,8,3,128]{3,1,2,0:T(8,128)} %param.12) | copy-start | bytes 294916
  2.1 62.4 %copy-start.9 = (s32[1,1,2,512]{3,1,2,0:T(1,128)}, s32[1,1,2,512]{3,1,2,0:T(1,128)S(1)}, u32[]{:S(2)}) copy-start(s32[1,1,2,512]{3,1,2,0:T(1,128)S(1)} %copy.30) | copy-start | bytes 12292
  2.8 1.1 copy-start.1
  14.0 50.5 %copy-start.12 = (s32[1,1024]{1,0:T(1,128)}, s32[1,1024]{1,0:T(1,128)S(1)}, u32[]{:S(2)}) copy-start(s32[1,1024]{1,0:T(1,128)S(1)} %get-tuple-element.10.rank_ref) | copy-start | bytes 12292
  64.5 5.9 %copy-start.8 = (f32[8,8,128]{2,1,0:T(8,128)S(1)}, f32[8,8,128]{2,1,0:T(8,128)}, u32[]{:S(2)}) copy-start(f32[8,8,128]{2,1,0:T(8,128)} %param.13) | copy-start | bytes 98308
  64.5 5.9 %copy-start.17 = (s32[8,8]{1,0:T(8,128)S(1)}, s32[8,8]{1,0:T(8,128)}, u32[]{:S(2)}) copy-start(s32[8,8]{1,0:T(8,128)} %param.14) | copy-start | bytes 772
  64.5 6.0 %copy-start.15 = (f32[8,8,3,128]{3,1,2,0:T(8,128)S(1)}, f32[8,8,3,128]{3,1,2,0:T(8,128)}, u32[]{:S(2)}) copy-start(f32[8,8,3,128]{3,1,2,0:T(8,128)} %param.11) | copy-start | bytes 294916
  64.5 10.6 %copy-start.2 = (f32[512,3,128]{2,0,1:T(8,128)S(1)}, f32[512,3,128]{2,0,1:T(8,128)}, u32[]{:S(2)}) copy-start(f32[512,3,128]{2,0,1:T(8,128)} %param.17) | copy-start | bytes 2359300
  64.5 10.6 %copy-start.16 = (f32[512,3]{0,1:T(4,128)S(1)}, f32[512,3]{0,1:T(4,128)}, u32[]{:S(2)}) copy-start(f32[512,3]{0,1:T(4,128)} %param.15) | copy-start | bytes 18436
  64.5 121.5 %all-to-all-start.1 = ((f32[128,24,128]{2,1,0:T(8,128)}), f32[128,24,128]{2,1,0:T(8,128)}, u32[]{:S(2)}, u32[]{:S(2)}) async-start(f32[128,24,128]{2,1,0:T(8,128)} %bitcast.18), calls=%async_computation.1 | async-start | bytes 3145728 | tf_op jit(solution)/shard_map/all_to_all | solution.py:437
  70.5 15.2 %collective-permute-start = (f32[4,1,8,128]{3,2,0,1:T(8,128)S(1)}, f32[4,1,8,128]{3,2,0,1:T(8,128)S(1)}, u32[]{:S(2)}, u32[]{:S(2)}) collective-permute-start(f32[4,1,8,128]{3,2,0,1:T(8,128)S(1)} %get-tuple-element.18), channel_id=1, source_target_pairs={{0,8},{8,16},{16,24},{24,32},{32,40},{40,48},{48,56},{56,64},{64,7... | collective-permute-start | bytes 49160 | tf_op jit(solution)/shard_map/ppermute | solution.py:427
  73.8 15.0 %collective-permute-start.1 = (f32[4,1,8,128]{3,2,0,1:T(8,128)S(1)}, f32[4,1,8,128]{3,2,0,1:T(8,128)S(1)}, u32[]{:S(2)}, u32[]{:S(2)}) collective-permute-start(f32[4,1,8,128]{3,2,0,1:T(8,128)S(1)} %get-tuple-element.19), channel_id=1, source_target_pairs={{8,0},{16,8},{24,16},{32,24},{40,32},{48,40},{56,48},{64,56},{72,6... | collective-permute-start | bytes 49160 | tf_op jit(solution)/shard_map/ppermute | solution.py:429
  76.3 195.6 %collective-permute-start.4 = (f32[3,512,128]{2,1,0:T(8,128)}, f32[3,512,128]{2,1,0:T(8,128)}, u32[]{:S(2)}, u32[]{:S(2)}) collective-permute-start(f32[3,512,128]{2,1,0:T(8,128)} %broadcast_add_fusion.world_ref), channel_id=1, source_target_pairs={{0,127},{1,0},{2,1},{3,2},{4,3},{5,4},{6,5},{7,6},{8,7},{9,8},{10,... | collective-permute-start | bytes 2359304 | tf_op jit(solution)/shard_map/ppermute | solution.py:468
  76.9 42.1 %copy-start.3 = (f32[128,24,128]{2,1,0:T(8,128)S(1)}, f32[128,24,128]{2,1,0:T(8,128)}, u32[]{:S(2)}) copy-start(f32[128,24,128]{2,1,0:T(8,128)} %all_to_all.44) | copy-start | bytes 4718596
  77.0 42.1 %copy-start.4 = (s32[128,1,128]{2,1,0:T(1,128)S(1)}, s32[128,1,128]{2,1,0:T(1,128)}, u32[]{:S(2)}) copy-start(s32[128,1,128]{2,1,0:T(1,128)} %all_to_all.43) | copy-start | bytes 196612
  88.8 6.0 %collective-permute-start.2 = (f32[4,10,1,128]{3,2,0,1:T(1,128)S(1)}, f32[4,10,1,128]{3,2,0,1:T(1,128)S(1)}, u32[]{:S(2)}, u32[]{:S(2)}) collective-permute-start(f32[4,10,1,128]{3,2,0,1:T(1,128)S(1)} %get-tuple-element.16), channel_id=1, source_target_pairs={{0,1},{1,2},{2,3},{3,4},{4,5},{5,6},{6,7},{8,9},{9,10},{10,11},{11... | collective-permute-start | bytes 61448 | tf_op jit(solution)/shard_map/ppermute | solution.py:427
  92.8 6.2 %collective-permute-start.3 = (f32[4,10,1,128]{3,2,0,1:T(1,128)S(1)}, f32[4,10,1,128]{3,2,0,1:T(1,128)S(1)}, u32[]{:S(2)}, u32[]{:S(2)}) collective-permute-start(f32[4,10,1,128]{3,2,0,1:T(1,128)S(1)} %get-tuple-element.17), channel_id=1, source_target_pairs={{1,0},{2,1},{3,2},{4,3},{5,4},{6,5},{7,6},{9,8},{10,9},{11,10},{12... | collective-permute-start | bytes 61448 | tf_op jit(solution)/shard_map/ppermute | solution.py:429
  185.4 0.6 copy-start.7
  186.0 76.1 %all-to-all-start.4 = ((f32[128,1,128]{2,1,0:T(1,128)}), f32[128,1,128]{2,1,0:T(1,128)}, u32[]{:S(2)}, u32[]{:S(2)}) async-start(f32[128,1,128]{2,1,0:T(1,128)} %bitcast.58), calls=%async_computation.4 | async-start | bytes 131072 | tf_op jit(solution)/shard_map/all_to_all | solution.py:437
  194.3 0.8 copy-start.5
  195.1 76.8 %copy-start.14 = (s32[512]{0:T(512)S(1)}, s32[512]{0:T(512)}, u32[]{:S(2)}) copy-start(s32[512]{0:T(512)} %param.21) | copy-start | bytes 6148
  261.5 0.6 copy-start.6
  262.1 49.9 %copy-start.10 = (s32[1,1,2,512]{3,1,2,0:T(1,128)S(1)}, s32[1,1,2,512]{3,1,2,0:T(1,128)}, u32[]{:S(2)}) copy-start(s32[1,1,2,512]{3,1,2,0:T(1,128)} %copy-done.9) | copy-start | bytes 12292
  262.1 49.9 %copy-start.11 = (f32[512,3]{0,1:T(4,128)S(1)}, f32[512,3]{0,1:T(4,128)}, u32[]{:S(2)}) copy-start(f32[512,3]{0,1:T(4,128)} %param.16) | copy-start | bytes 18436
  262.1 49.9 %copy-start.13 = (s32[1,1024]{1,0:T(1,128)S(1)}, s32[1,1024]{1,0:T(1,128)}, u32[]{:S(2)}) copy-start(s32[1,1024]{1,0:T(1,128)} %copy-done.12) | copy-start | bytes 12292
  262.2 49.9 %all-to-all-start.2 = ((f32[128,1,128]{2,1,0:T(1,128)}), f32[128,1,128]{2,1,0:T(1,128)S(1)}, u32[]{:S(2)}, u32[]{:S(2)}) async-start(f32[128,1,128]{2,1,0:T(1,128)} %bitcast.57), calls=%async_computation.2 | async-start | bytes 131072 | tf_op jit(solution)/shard_map/all_to_all | solution.py:437
where the time goes:
time: 315 us; the launch traced here: 314 us
  Pallas kernels  205 us (65%)
  blocking collectives  50.5 us (16%)
  starting transfers between devices  35 us (11%)
  waiting for transfers between devices  16 us (5%)
  local copies, waits for them, and re-layouts  5.52 us (2%)
    pallas_call x2, Pallas kernels, fluid(): pl.pallas_call(functools.partial(fluid_kernel, first), out_shape=jax.Shap...  133 us
    all_to_all x2, blocking collectives, swap_all(): return lax.all_to_all(array, AXES, split_axis=0, concat_axis=0, tiled=True)  50.5 us
    pallas_call x1, Pallas kernels, contact(): pl.pallas_call(contact_kernel, out_shape=jax.ShapeDtypeStruct((clumps, W)...  40 us
    all_to_all x3, starting transfers between devices, swap_all(): return lax.all_to_all(array, AXES, split_axis=0, concat_axis=0, tiled=True)  23.9 us
    pallas_call x1, Pallas kernels, density(): pl.pallas_call(density_kernel, out_shape=(jax.ShapeDtypeStruct((blocks, W...  19.8 us
    pallas_call x1, Pallas kernels, prep(): pl.pallas_call(prep_kernel, out_shape=(send, send, jax.ShapeDtypeStruct((...  10 us
    ppermute x2, waiting for transfers between devices, extended(): lax.ppermute(tail, axis, [(i, (i + 1) % count) for i in range(ends)])  8.72 us
    ppermute x2, starting transfers between devices, extended(): lax.ppermute(tail, axis, [(i, (i + 1) % count) for i in range(ends)])  7.31 us
  transfers between devices with their start and end apart: 8, of which 3 were waited for; matrix products, arithmetic and copies ran while one was open for 0% of the time, Pallas kernels for 61%

commit v1 on v0

--- a/solution.py
+++ b/solution.py
@@ -19,6 +19,8 @@
 AXES = ("stream", "span")
 W = 128
 FEATS = 32
+ROWS = 49
+UNROLL = 4
 DEAD = -30000.0
 BF = jnp.bfloat16
 F32 = jnp.float32
@@ -76,8 +78,7 @@
     return jnp.sum(v, axis=1, keepdims=True)
 
 
-def prep_kernel(dev_ref, blk_ref, dev_s, off_s, arm_ref, first_ref, second_ref, ids_ref, rank_ref,
-                buf, rank_s, sems):
+def prep_kernel(dev_ref, blk_ref, dev_s, off_s, arm_ref, send_ref, rank_ref, buf, rank_s, sems):
     entries = dev_ref.shape[1]
     parts = entries // W
     dev = dev_ref[...]
@@ -100,7 +101,8 @@
     move.start()
     named = jnp.where(row == rank, blk_ref[...] + 1, 0).astype(F32).astype(BF)
     ids = lax.dot_general(hot_b, named, (((1,), (1,)), ((), ())), preferred_element_type=F32)
-    ids_ref[...] = ids.astype(jnp.int32) - 1
+    for d in range(W):
+        buf[d * ROWS + 48 : d * ROWS + 49, :] = ids[d : d + 1, :]
     move.wait()
 
     clumps = entries // 2
@@ -110,23 +112,17 @@
             for j in range(8):
                 c = i * 8 + j
                 e = k * clumps + c
-                d = dev_s[0, e]
-                r = rank_s[0, e]
-                base = ((r >> 3) * W + d) * 24 + (r & 7)
+                base = dev_s[0, e] * ROWS + rank_s[0, e]
                 for q in range(3):
-                    buf[pl.ds(base + 8 * q, 1), :] = (
+                    buf[pl.ds(base + 16 * q, 1), :] = (
                         arm_ref[q, pl.ds(c, 1), :] + off_s[q, e]
                     )
         return carry
 
     lax.fori_loop(0, clumps // 8, step, 0)
-    half = W * 24
-    one = pltpu.make_async_copy(buf.at[pl.ds(0, half)], first_ref, sems.at[0])
-    two = pltpu.make_async_copy(buf.at[pl.ds(half, half)], second_ref, sems.at[1])
-    one.start()
-    two.start()
-    one.wait()
-    two.wait()
+    out = pltpu.make_async_copy(buf, send_ref, sems.at[0])
+    out.start()
+    out.wait()
 
 
 def prep(dev, blk, off, arms):
@@ -134,21 +130,18 @@
     vm = pl.BlockSpec(memory_space=pltpu.VMEM)
     sm = pl.BlockSpec(memory_space=pltpu.SMEM)
     hbm = pl.BlockSpec(memory_space=pl.ANY)
-    send = jax.ShapeDtypeStruct((W * 24, W), F32)
     return pl.pallas_call(
         prep_kernel,
         out_shape=(
-            send,
-            send,
-            jax.ShapeDtypeStruct((W, W), jnp.int32),
+            jax.ShapeDtypeStruct((W * ROWS, W), F32),
             jax.ShapeDtypeStruct((1, entries), jnp.int32),
         ),
         in_specs=[vm, vm, sm, sm, vm],
-        out_specs=(hbm, hbm, vm, vm),
+        out_specs=(hbm, vm),
         scratch_shapes=[
-            pltpu.VMEM((2 * W * 24, W), F32),
+            pltpu.VMEM((W * ROWS, W), F32),
             pltpu.SMEM((1, entries), jnp.int32),
-            pltpu.SemaphoreType.DMA((2,)),
+            pltpu.SemaphoreType.DMA((1,)),
         ],
         compiler_params=pltpu.CompilerParams(vmem_limit_bytes=24 << 20),
         name="prep",
@@ -203,7 +196,7 @@
             sums[pl.ds(b, 1), :] = jnp.sum(total, axis=0, keepdims=True)
             return inner
 
-        lax.fori_loop(0, rows_y, block, 0)
+        lax.fori_loop(0, rows_y, block, 0, unroll=4)
         density = DENS * (mass_ref[pl.ds(at, 8), :] + sums[...])
         dens_ref[pl.ds(at, 8), :] = density
         weight = own_ref[3, pl.ds(at, 8), :] / density
@@ -264,44 +257,57 @@
     clumps = arm_ref.shape[1]
     cand[:, 0:clumps, :] = world_ref[...]
     cand[:, clumps : 2 * clumps, :] = next_ref[...]
-    zero_tail(feat)
-    zero_tail(right)
     zero = jnp.zeros((8, W), F32)
-    for q in (4, 5, 6, 7, 12, 13, 14, 15):
-        lead[8 * q : 8 * q + 8, :] = zero
+    for t in range(UNROLL):
+        zero_tail(feat, t * FEATS * 8)
+        zero_tail(right, t * FEATS * 8)
+        for q in (4, 5, 6, 7, 12, 13, 14, 15):
+            lead[t * W + 8 * q : t * W + 8 * q + 8, :] = zero
     upper = lax.broadcasted_iota(jnp.int32, (16, W), 0) < 8
 
-    def group(g, carry):
-        at = pl.multiple_of(g * 8, 8)
-        for j in range(8):
-            p = partner_s[0, at + j]
-            for q in range(3):
-                gat[8 * q + j : 8 * q + j + 1, :] = cand[q, pl.ds(p, 1), :]
-        zb = [gat[8 * q : 8 * q + 8, :] - 0.5 for q in range(3)]
-        za = [world_ref[q, pl.ds(at, 8), :] - 0.5 for q in range(3)]
-        put_rows(feat, left_rows(*[split3(v) for v in zb], norm_of(*zb, C_CONTACT)))
-        scaled = [split3(v * (2.0 * C_CONTACT)) for v in za]
-        put_rows(right, right_rows(*scaled, norm_of(*za, C_CONTACT)))
-        for q, v in enumerate(zb + [jnp.ones((8, W), F32)]):
-            hi = v.astype(BF).astype(F32)
-            lead[8 * q : 8 * q + 8, :] = hi
-            lead[8 * (q + 8) : 8 * (q + 8) + 8, :] = v - hi
-        for j in range(8):
-            lhs = jnp.transpose(take_rows(feat, j)).astype(BF)
-            kernel = gauss(lhs, take_rows(right, j).astype(BF))
-            l16 = lead[pl.ds(j, 16, stride=8), :]
-            both = jnp.concatenate([l16, jnp.where(upper, l16, 0.0)], axis=1).astype(BF)
-            res = jnp.dot(both, two_halves(kernel), preferred_element_type=F32)
-            acc[8 * j : 8 * j + 8, :] = res[0:8] + res[8:16]
-        s = [acc[pl.ds(q, 8, stride=8), :] for q in range(4)]
-        f = [STIFF * (za[q] * s[3] - s[q]) for q in range(3)]
-        arm = [arm_ref[q, pl.ds(at, 8), :] for q in range(3)]
-        t = [arm[1] * f[2] - arm[2] * f[1], arm[2] * f[0] - arm[0] * f[2],
-             arm[0] * f[1] - arm[1] * f[0]]
-        out_ref[pl.ds(at, 8), :] = columns_to_lanes([lane_sum(v) for v in f + t])
+    def group(i, carry):
+        zas, ats = [], []
+        for t in range(UNROLL):
+            at = pl.multiple_of((i * UNROLL + t) * 8, 8)
+            ats.append(at)
+            for j in range(8):
+                p = partner_s[0, at + j]
+                for q in range(3):
+                    spot = 24 * t + 8 * q + j
+                    gat[spot : spot + 1, :] = cand[q, pl.ds(p, 1), :]
+            za = [world_ref[q, pl.ds(at, 8), :] - 0.5 for q in range(3)]
+            zas.append(za)
+            scaled = [split3(v * (2.0 * C_CONTACT)) for v in za]
+            put_rows(right, right_rows(*scaled, norm_of(*za, C_CONTACT)), t * FEATS * 8)
+        for t in range(UNROLL):
+            zb = [gat[24 * t + 8 * q : 24 * t + 8 * q + 8, :] - 0.5 for q in range(3)]
+            parts = [split3(v) for v in zb]
+            put_rows(feat, left_rows(*parts, norm_of(*zb, C_CONTACT)), t * FEATS * 8)
+            for q, v in enumerate(zb + [jnp.ones((8, W), F32)]):
+                hi = v.astype(BF).astype(F32)
+                spot = t * W + 8 * q
+                lead[spot : spot + 8, :] = hi
+                lead[spot + 64 : spot + 72, :] = v - hi
+        for t in range(UNROLL):
+            for j in range(8):
+                lhs = jnp.transpose(take_rows(feat, j, t * FEATS * 8)).astype(BF)
+                kernel = gauss(lhs, take_rows(right, j, t * FEATS * 8).astype(BF))
+                l16 = lead[pl.ds(t * W + j, 16, stride=8), :]
+                both = jnp.concatenate([l16, jnp.where(upper, l16, 0.0)], axis=1).astype(BF)
+                res = jnp.dot(both, two_halves(kernel), preferred_element_type=F32)
+                spot = 64 * t + 8 * j
+                acc[spot : spot + 8, :] = res[0:8] + res[8:16]
+        for t in range(UNROLL):
+            at, za = ats[t], zas[t]
+            s = [acc[pl.ds(64 * t + q, 8, stride=8), :] for q in range(4)]
+            f = [STIFF * (za[q] * s[3] - s[q]) for q in range(3)]
+            arm = [arm_ref[q, pl.ds(at, 8), :] for q in range(3)]
+            tq = [arm[1] * f[2] - arm[2] * f[1], arm[2] * f[0] - arm[0] * f[2],
+                  arm[0] * f[1] - arm[1] * f[0]]
+            out_ref[pl.ds(at, 8), :] = columns_to_lanes([lane_sum(v) for v in f + tq])
         return carry
 
-    lax.fori_loop(0, clumps // 8, group, 0)
+    lax.fori_loop(0, clumps // (8 * UNROLL), group, 0)
 
 
 def contact(partner, arms, world, following):
@@ -315,74 +321,102 @@
         out_specs=vm,
         scratch_shapes=[
             pltpu.VMEM((3, 2 * clumps, W), F32),
-            pltpu.VMEM((24, W), F32),
-            pltpu.VMEM((FEATS * 8, W), F32),
-            pltpu.VMEM((FEATS * 8, W), F32),
-            pltpu.VMEM((W, W), F32),
-            pltpu.VMEM((64, W), F32),
+            pltpu.VMEM((UNROLL * 24, W), F32),
+            pltpu.VMEM((UNROLL * FEATS * 8, W), F32),
+            pltpu.VMEM((UNROLL * FEATS * 8, W), F32),
+            pltpu.VMEM((UNROLL * W, W), F32),
+            pltpu.VMEM((UNROLL * 64, W), F32),
         ],
         compiler_params=pltpu.CompilerParams(vmem_limit_bytes=24 << 20),
         name="contact",
     )(partner, arms, world, following)
 
 
-def fluid_kernel(first, ids_s, y_ref, table_ref, amp_ref, out_ref, right, acc):
-    zero_tail(right)
+def fluid_kernel(y_ref, table_ref, amp_ref, out_ref, names, names_s, right, acc, sems):
+    for t in range(2 * UNROLL):
+        zero_tail(right, t * FEATS * 8)
     lane = lax.broadcasted_iota(jnp.int32, (8, W), 1)
     mine = (lane >> 4) == lax.broadcasted_iota(jnp.int32, (8, W), 0)
     place = lane & 15
-
-    def group(g, carry):
-        at = pl.multiple_of(g * 24, 8)
-        y = [y_ref[pl.ds(at + 8 * q, 8), :] for q in range(3)]
-        u = [v - 0.5 for v in y]
-        scaled = [split3(v * (2.0 * C_FLUID)) for v in u]
-        put_rows(right, right_rows(*scaled, norm_of(*u, C_FLUID)))
-        valid = jnp.zeros((1, W), jnp.int32)
-        for j in range(8):
-            name = ids_s[g, first + j]
-            valid = jnp.where((lane[0:1] >> 4) == j, name, valid)
-            b = jnp.maximum(name, 0)
-            kernel = gauss(table_ref[b], take_rows(right, j).astype(BF))
-            res = jnp.dot(amp_ref[b], two_halves(kernel), preferred_element_type=F32)
-            acc[8 * j : 8 * j + 8, :] = res[0:8] + res[8:16]
-        s = [acc[pl.ds(q, 8, stride=8), :] for q in range(4)]
-        cross = [y[1] * s[2] - y[2] * s[1], y[2] * s[0] - y[0] * s[2], y[0] * s[1] - y[1] * s[0]]
-        moment = [y[q] * s[3] for q in range(3)]
-        out = jnp.zeros((8, W), F32)
-        for q, v in enumerate(s + cross + moment):
-            out = jnp.where(place == q, lane_sum(v), out)
-        row = jnp.sum(jnp.where(mine, out, 0.0), axis=0, keepdims=True)
-        out_ref[pl.ds(g, 1), :] = jnp.where(valid >= 0, row, 0.0)
+    devices = out_ref.shape[0] // 2
+
+    def read(g, carry):
+        names[pl.ds(g, 1), :] = y_ref[pl.ds(g * ROWS + 48, 1), :].astype(jnp.int32) - 1
         return carry
 
-    lax.fori_loop(0, out_ref.shape[0], group, 0)
-
-
-def fluid(first, ids, spots, table, amp):
+    lax.fori_loop(0, devices, read, 0, unroll=8)
+    move = pltpu.make_async_copy(names, names_s, sems.at[0])
+    move.start()
+    move.wait()
+
+    def group(i, carry):
+        ys, valids = [], []
+        for t in range(2 * UNROLL):
+            g = i * UNROLL + t // 2
+            at = g * ROWS + (t % 2) * 8
+            y = [y_ref[pl.ds(at + 16 * q, 8), :] for q in range(3)]
+            ys.append(y)
+            u = [v - 0.5 for v in y]
+            scaled = [split3(v * (2.0 * C_FLUID)) for v in u]
+            put_rows(right, right_rows(*scaled, norm_of(*u, C_FLUID)), t * FEATS * 8)
+        for t in range(2 * UNROLL):
+            g = i * UNROLL + t // 2
+            valid = jnp.zeros((1, W), jnp.int32)
+            for j in range(8):
+                name = names_s[g, (t % 2) * 8 + j]
+                valid = jnp.where((lane[0:1] >> 4) == j, name, valid)
+                b = jnp.maximum(name, 0)
+                kernel = gauss(table_ref[b], take_rows(right, j, t * FEATS * 8).astype(BF))
+                res = jnp.dot(amp_ref[b], two_halves(kernel), preferred_element_type=F32)
+                spot = 64 * t + 8 * j
+                acc[spot : spot + 8, :] = res[0:8] + res[8:16]
+            valids.append(valid)
+        for t in range(2 * UNROLL):
+            g = i * UNROLL + t // 2
+            y = ys[t]
+            s = [acc[pl.ds(64 * t + q, 8, stride=8), :] for q in range(4)]
+            cross = [y[1] * s[2] - y[2] * s[1], y[2] * s[0] - y[0] * s[2],
+                     y[0] * s[1] - y[1] * s[0]]
+            moment = [y[q] * s[3] for q in range(3)]
+            out = jnp.zeros((8, W), F32)
+            for q, v in enumerate(s + cross + moment):
+                out = jnp.where(place == q, lane_sum(v), out)
+            row = jnp.sum(jnp.where(mine, out, 0.0), axis=0, keepdims=True)
+            out_ref[pl.ds(2 * g + t % 2, 1), :] = jnp.where(valids[t] >= 0, row, 0.0)
+        return carry
+
+    lax.fori_loop(0, devices // UNROLL, group, 0)
+
+
+def fluid(spots, table, amp):
     vm = pl.BlockSpec(memory_space=pltpu.VMEM)
-    sm = pl.BlockSpec(memory_space=pltpu.SMEM)
     return pl.pallas_call(
-        functools.partial(fluid_kernel, first),
-        out_shape=jax.ShapeDtypeStruct((W, W), F32),
-        in_specs=[sm, vm, vm, vm],
+        fluid_kernel,
+        out_shape=jax.ShapeDtypeStruct((2 * W, W), F32),
+        in_specs=[vm, vm, vm],
         out_specs=vm,
-        scratch_shapes=[pltpu.VMEM((FEATS * 8, W), F32), pltpu.VMEM((64, W), F32)],
+        scratch_shapes=[
+            pltpu.VMEM((W, W), jnp.int32),
+            pltpu.SMEM((W, W), jnp.int32),
+            pltpu.VMEM((2 * UNROLL * FEATS * 8, W), F32),
+            pltpu.VMEM((2 * UNROLL * 64, W), F32),
+            pltpu.SemaphoreType.DMA((1,)),
+        ],
         compiler_params=pltpu.CompilerParams(vmem_limit_bytes=24 << 20),
         name="fluid",
-    )(ids, spots, table, amp)
-
-
-def combine_kernel(dev_ref, rank_ref, off_ref, vel_ref, one_ref, two_ref, contact_ref, out_ref):
+    )(spots, table, amp)
+
+
+def combine_kernel(dev_ref, rank_ref, off_ref, vel_ref, got_ref, contact_ref, out_ref):
     entries = dev_ref.shape[1]
     clumps = entries // 2
     row = lax.broadcasted_iota(jnp.int32, (W, entries), 0)
     hot = (row == dev_ref[...]).astype(BF)
     rank = rank_ref[...]
     picked = jnp.zeros((16, entries), F32)
-    for chunk, ref in enumerate((one_ref, two_ref)):
+    for chunk in range(2):
         spread = jnp.zeros((W, entries), F32)
-        for part in split3(jnp.transpose(ref[...])):
+        for part in split3(jnp.transpose(got_ref[pl.ds(chunk, W, stride=2), :])):
             spread = spread + jnp.dot(part.astype(BF), hot, preferred_element_type=F32)
         spread = jnp.where((row >> 4) + 8 * chunk == rank, spread, 0.0)
         picked = picked + jnp.sum(spread.reshape(8, 16, entries), axis=0)
@@ -404,16 +438,16 @@
         out_ref[q : q + 1, :] = total[q]
 
 
-def combine(dev, rank, off, vel, one, two, touch):
+def combine(dev, rank, off, vel, got, touch):
     vm = pl.BlockSpec(memory_space=pltpu.VMEM)
     return pl.pallas_call(
         combine_kernel,
         out_shape=jax.ShapeDtypeStruct((6, vel.shape[1]), F32),
-        in_specs=[vm] * 7,
+        in_specs=[vm] * 6,
         out_specs=vm,
         compiler_params=pltpu.CompilerParams(vmem_limit_bytes=24 << 20),
         name="combine",
-    )(dev, rank, off, vel, one, two, touch)
+    )(dev, rank, off, vel, got, touch)
 
 
 def extended(cells, sides):
@@ -460,10 +494,8 @@
     blk = margin_block.T.reshape(1, entries)
     off = jnp.transpose(margin_offset, (2, 1, 0)).reshape(3, entries)
     vel = clump_vel.T
-    first, second, ids, rank = prep(dev, blk, off, arms)
-    names = swap_all(ids)
-    got_first = swap_all(first.reshape(devices, 24, width))
-    got_second = swap_all(second.reshape(devices, 24, width))
+    send, rank = prep(dev, blk, off, arms)
+    got = swap_all(send.reshape(devices, 1, ROWS * width))
     world = arms + clump_center.T[:, :, None]
     following = lax.ppermute(world, AXES, [(i, (i + devices - 1) % devices) for i in range(devices)])
     touch = contact(contact_partner.reshape(1, clumps), arms, world, following)
@@ -476,9 +508,10 @@
     own = planes.reshape(4, blocks, width)
     speed = jnp.moveaxis(fluid_vel, 2, 0).reshape(3, blocks, width)
     dens, table, amp = density(ext, own, fluid_mass.reshape(blocks, width), speed)
-    one = swap_all(fluid(0, names, got_first.reshape(devices * 24, width), table, amp))
-    two = swap_all(fluid(8, names, got_second.reshape(devices * 24, width), table, amp))
-    loads = combine(dev, rank, off, vel, one, two, touch)
+    got, touch = lax.optimization_barrier((got, touch))
+    sums = fluid(got.reshape(devices * ROWS, width), table, amp)
+    back = swap_all(sums.reshape(devices, 1, 2 * width)).reshape(2 * devices, width)
+    loads = combine(dev, rank, off, vel, back, touch)
     return (dens.reshape(rows_x, rows_y, width), loads)
 
 

time: 315 us -> 175 us (0.56)
  Pallas kernels: 205 us -> 87.8 us
  blocking collectives: 50.5 us -> 17.6 us
  waiting for transfers between devices: 16 us -> 31.5 us
  starting transfers between devices: 35 us -> 24.5 us
  local copies, waits for them, and re-layouts: 5.52 us -> 10.6 us
    pallas_call x3 -> x2, Pallas kernels: 143 us -> 57.5 us  [the longest x1 49.2 us: fluid(): pl.pallas_call(fluid_kernel, out_shape=jax.ShapeDtypeStruct((2 * W, W), F...]
    all_to_all x2 -> x1, blocking collectives: 50.5 us -> 17.6 us  [swap_all(): return lax.all_to_all(array, AXES, split_axis=0, concat_axis=0, tiled=True)]
    ppermute x2, waiting for transfers between devices: 7.26 us -> 31.4 us  [extended(): lax.ppermute(head, axis, [((i + 1) % count, i) for i in range(ends)])]
    pallas_call x1, Pallas kernels: 40 us -> 17.1 us  [contact(): pl.pallas_call(contact_kernel, out_shape=jax.ShapeDtypeStruct((clumps, W)...]
    all_to_all x3 -> x1, starting transfers between devices: 23.9 us -> 11.5 us  [swap_all(): return lax.all_to_all(array, AXES, split_axis=0, concat_axis=0, tiled=True)]
    ppermute x2, waiting for transfers between devices: 8.72 us -> 0.01 us  [extended(): lax.ppermute(tail, axis, [(i, (i + 1) % count) for i in range(ends)])]
    pallas_call x1, Pallas kernels: 19.8 us -> 11.9 us  [density(): pl.pallas_call(density_kernel, out_shape=(jax.ShapeDtypeStruct((blocks, W...]
    unnamed x39 -> x35, local copies, waits for them, and re-layouts: 5.39 us -> 10.5 us
  transfers between devices with their start and end apart: 8 -> 6, of which waited for: 3 -> 2; matrix products, arithmetic and copies ran while one was open for 0% -> 1% of each run, Pallas kernels for 61% -> 17%
where the time goes in v1:
time: 175 us; the launch traced here: 174 us
  Pallas kernels  87.8 us (50%)
  waiting for transfers between devices  31.5 us (18%)
  starting transfers between devices  24.5 us (14%)
  blocking collectives  17.6 us (10%)
  local copies, waits for them, and re-layouts  10.6 us (6%)
    pallas_call x1, Pallas kernels, fluid(): pl.pallas_call(fluid_kernel, out_shape=jax.ShapeDtypeStruct((2 * W, W), F...  49.2 us
    ppermute x2, waiting for transfers between devices, extended(): lax.ppermute(head, axis, [((i + 1) % count, i) for i in range(ends)])  31.4 us
    all_to_all x1, blocking collectives, swap_all(): return lax.all_to_all(array, AXES, split_axis=0, concat_axis=0, tiled=True)  17.6 us
    pallas_call x1, Pallas kernels, contact(): pl.pallas_call(contact_kernel, out_shape=jax.ShapeDtypeStruct((clumps, W)...  17.1 us
    pallas_call x1, Pallas kernels, density(): pl.pallas_call(density_kernel, out_shape=(jax.ShapeDtypeStruct((blocks, W...  11.9 us
    all_to_all x1, starting transfers between devices, swap_all(): return lax.all_to_all(array, AXES, split_axis=0, concat_axis=0, tiled=True)  11.5 us
    unnamed x35, local copies, waits for them, and re-layouts  10.5 us
    pallas_call x1, Pallas kernels, prep(): pl.pallas_call(prep_kernel, out_shape=(jax.ShapeDtypeStruct((W * ROWS, W)...  8.24 us
  transfers between devices with their start and end apart: 6, of which 2 were waited for; matrix products, arithmetic and copies ran while one was open for 1% of the time, Pallas kernels for 17%

profile of v1, /device:TPU:1, one launch (start us, length us, event | category | flops | bytes accessed | tf_op | source)
XLA Modules:
  0.0 174.4 jit_solution(3355268974021811576)
XLA Ops:
  0.6 0.0 copy-start
  0.6 0.7 copy.29
  1.4 0.7 copy.30
  2.1 0.7 copy.31
  2.8 0.0 copy-start.1
  2.8 1.1 copy-done.1
  3.9 8.2 %prep.1 = (f32[6272,128]{1,0:T(8,128)S(1)}, s32[1,1024]{1,0:T(1,128)S(1)}) custom-call(s32[1,1024]{1,0:T(1,128)S(1)} %bitcast.48, s32[1,1024]{1,0:T(1,128)S(1)} %bitcast.51, s32[1,1024]{1,0:T(1,128)S(1)} %bitcast.49, f32[3,1024]{1,0:T(4,128)S(1)} %bitcast.45, f32[3,512,128]{2,1,0:T(8,128)S(1)} %bitcast.40), custom_call_target="tpu_custom_call" | custom-call | tf_op jit(solution)/shard_map/prep/pallas_call | solution.py:133
  12.2 0.0 copy-start.3
  12.2 1.6 copy-done.3
  13.8 0.0 copy-start.10
  13.8 11.5 %all-to-all-start = ((f32[128,1,6272]{2,1,0:T(1,128)}), f32[128,1,6272]{2,1,0:T(1,128)S(1)}, u32[]{:S(2)}, u32[]{:S(2)}) async-start(f32[128,1,6272]{2,1,0:T(1,128)} %bitcast.42), calls=%async_computation | async-start | bytes 6422528 | tf_op jit(solution)/shard_map/all_to_all | solution.py:471
  25.3 0.0 copy-done.10
  25.4 0.0 copy-done.15
  25.4 0.0 copy-start.2
  25.4 0.0 copy-start.12
  25.4 0.1 fusion.1
  25.5 0.0 copy-done.13
  25.5 1.4 collective-permute-start.1
  26.9 4.0 %collective-permute-start = (f32[4,1,8,128]{3,2,0,1:T(8,128)S(1)}, f32[4,1,8,128]{3,2,0,1:T(8,128)S(1)}, u32[]{:S(2)}, u32[]{:S(2)}) collective-permute-start(f32[4,1,8,128]{3,2,0,1:T(8,128)S(1)} %get-tuple-element.18), channel_id=1, source_target_pairs={{0,8},{8,16},{16,24},{24,32},{32,40},{40,48},{48,56},{56,64},{64,7... | collective-permute-start | bytes 49160 | tf_op jit(solution)/shard_map/ppermute | solution.py:461
  30.9 0.0 copy-done.14
  30.9 1.4 broadcast_add_fusion.world_ref
  32.3 1.7 collective-permute-start.4
  34.0 0.0 copy-done
  34.0 27.5 %collective-permute-done.1 = f32[4,1,8,128]{3,2,0,1:T(8,128)S(1)} collective-permute-done((f32[4,1,8,128]{3,2,0,1:T(8,128)S(1)}, f32[4,1,8,128]{3,2,0,1:T(8,128)S(1)}, u32[]{:S(2)}, u32[]{:S(2)}) %collective-permute-start.1) | collective-permute-done | bytes 16416 | tf_op jit(solution)/shard_map/ppermute | solution.py:463
  61.6 0.0 collective-permute-done
  61.6 2.8 %collective-permute-start.3 = (f32[4,10,1,128]{3,2,0,1:T(1,128)S(1)}, f32[4,10,1,128]{3,2,0,1:T(1,128)S(1)}, u32[]{:S(2)}, u32[]{:S(2)}) collective-permute-start(f32[4,10,1,128]{3,2,0,1:T(1,128)S(1)} %get-tuple-element.17), channel_id=1, source_target_pairs={{1,0},{2,1},{3,2},{4,3},{5,4},{6,5},{7,6},{9,8},{10,9},{11,10},{12... | collective-permute-start | bytes 61448 | tf_op jit(solution)/shard_map/ppermute | solution.py:463
  64.4 3.1 %collective-permute-start.2 = (f32[4,10,1,128]{3,2,0,1:T(1,128)S(1)}, f32[4,10,1,128]{3,2,0,1:T(1,128)S(1)}, u32[]{:S(2)}, u32[]{:S(2)}) collective-permute-start(f32[4,10,1,128]{3,2,0,1:T(1,128)S(1)} %get-tuple-element.16), channel_id=1, source_target_pairs={{0,1},{1,2},{2,3},{3,4},{4,5},{5,6},{6,7},{8,9},{9,10},{10,11},{11... | collective-permute-start | bytes 61448 | tf_op jit(solution)/shard_map/ppermute | solution.py:461
  67.6 3.9 %collective-permute-done.3 = f32[4,10,1,128]{3,2,0,1:T(1,128)S(1)} collective-permute-done((f32[4,10,1,128]{3,2,0,1:T(1,128)S(1)}, f32[4,10,1,128]{3,2,0,1:T(1,128)S(1)}, u32[]{:S(2)}, u32[]{:S(2)}) %collective-permute-start.3) | collective-permute-done | bytes 20512 | tf_op jit(solution)/shard_map/ppermute | solution.py:463
  71.5 0.0 collective-permute-done.2
  71.5 0.1 pad_maximum_fusion
  71.6 0.1 copy.23
  71.7 11.9 %density.1 = (f32[64,128]{1,0:T(8,128)}, bf16[64,128,32]{2,1,0:T(8,128)(2,1)S(1)}, bf16[64,16,256]{2,1,0:T(8,128)(2,1)S(1)}) custom-call(f32[4,104,128]{2,1,0:T(8,128)S(1)} %pad.4.ext_ref, f32[4,64,128]{2,1,0:T(8,128)S(1)} %pad_maximum_fusion.1.own_ref, f32[64,128]{1,0:T(8,128)S(1)} %bitcast.47, f32[3,64,128]{2,1,0:T(8,128)S(1)} %copy_bitcast_fusion.vel_ref), custom_call_target="tpu_custom_call" | custom-call | tf_op jit(solution)/shard_map/density/pallas_call | solution.py:227
  83.6 1.3 copy-done.4
  84.9 0.8 copy-done.8
  85.8 0.0 collective-permute-done.4.next_ref
  85.8 0.0 copy-done.2
  85.8 0.0 copy-done.12
  85.8 0.0 copy-start.11
  85.8 17.1 %contact.1.contact_ref = f32[512,128]{1,0:T(8,128)S(1)} custom-call(s32[1,512]{1,0:T(1,128)S(1)} %bitcast.53, f32[3,512,128]{2,1,0:T(8,128)S(1)} %bitcast.41, f32[3,512,128]{2,1,0:T(8,128)S(1)} %broadcast_add_fusion.world_ref, f32[3,512,128]{2,1,0:T(8,128)S(1)} %collective-permute-done.4.next_ref), custom_call_target="tpu_custom_call" | custom-call | tf_op jit(solution)/shard_map/contact/pallas_call | solution.py:317
  102.9 0.7 copy-done.6
  103.6 0.0 all-to-all-done
  103.6 1.6 copy-done.5
  105.2 1.0 copy-done.9
  106.3 49.2 %fluid.1 = f32[256,128]{1,0:T(8,128)S(1)} custom-call(f32[6272,128]{1,0:T(8,128)S(1)} %bitcast.39, bf16[64,128,32]{2,1,0:T(8,128)(2,1)S(1)} %copy-done.5, bf16[64,16,256]{2,1,0:T(8,128)(2,1)S(1)} %copy-done.9), custom_call_target="tpu_custom_call" | custom-call | tf_op jit(solution)/shard_map/fluid/pallas_call | solution.py:393
  155.5 17.6 %all_to_all.10 = f32[128,1,256]{2,1,0:T(1,128)S(1)} all-to-all(f32[128,1,256]{2,1,0:T(1,128)S(1)} %bitcast.44), channel_id=1, replica_groups=mesh['stream'=16,'span'=8] {'stream','span'}, dimensions={0} | all-to-all | bytes 262144 | tf_op jit(solution)/shard_map/all_to_all | solution.py:471
  173.1 0.0 copy-done.11
  173.1 0.0 copy-done.7
  173.1 1.3 combine.1
  (16 shorter events, 0.1 us)
Async XLA Ops:
  0.6 33.4 %copy-start = (f32[8,8,3,128]{3,1,2,0:T(8,128)S(1)}, f32[8,8,3,128]{3,1,2,0:T(8,128)}, u32[]{:S(2)}) copy-start(f32[8,8,3,128]{3,1,2,0:T(8,128)} %param.12) | copy-start | bytes 294916
  2.8 1.1 copy-start.1
  12.2 1.7 copy-start.3
  13.8 11.5 %copy-start.10 = (f32[8,8,128]{2,1,0:T(8,128)S(1)}, f32[8,8,128]{2,1,0:T(8,128)}, u32[]{:S(2)}) copy-start(f32[8,8,128]{2,1,0:T(8,128)} %param.13) | copy-start | bytes 98308
  13.8 11.5 %copy-start.15 = (s32[8,8]{1,0:T(8,128)S(1)}, s32[8,8]{1,0:T(8,128)}, u32[]{:S(2)}) copy-start(s32[8,8]{1,0:T(8,128)} %param.14) | copy-start | bytes 772
  13.8 11.6 %copy-start.13 = (f32[8,8,3,128]{3,1,2,0:T(8,128)S(1)}, f32[8,8,3,128]{3,1,2,0:T(8,128)}, u32[]{:S(2)}) copy-start(f32[8,8,3,128]{3,1,2,0:T(8,128)} %param.11) | copy-start | bytes 294916
  13.8 17.1 %copy-start.14 = (f32[512,3]{0,1:T(4,128)S(1)}, f32[512,3]{0,1:T(4,128)}, u32[]{:S(2)}) copy-start(f32[512,3]{0,1:T(4,128)} %param.15) | copy-start | bytes 18436
  13.8 89.8 %all-to-all-start = ((f32[128,1,6272]{2,1,0:T(1,128)}), f32[128,1,6272]{2,1,0:T(1,128)S(1)}, u32[]{:S(2)}, u32[]{:S(2)}) async-start(f32[128,1,6272]{2,1,0:T(1,128)} %bitcast.42), calls=%async_computation | async-start | bytes 6422528 | tf_op jit(solution)/shard_map/all_to_all | solution.py:471
  25.4 60.4 %copy-start.2 = (f32[512,3,128]{2,0,1:T(8,128)S(1)}, f32[512,3,128]{2,0,1:T(8,128)}, u32[]{:S(2)}) copy-start(f32[512,3,128]{2,0,1:T(8,128)} %param.17) | copy-start | bytes 2359300
  25.4 60.4 %copy-start.12 = (s32[512]{0:T(512)S(1)}, s32[512]{0:T(512)}, u32[]{:S(2)}) copy-start(s32[512]{0:T(512)} %param.21) | copy-start | bytes 6148
  25.5 36.1 %collective-permute-start.1 = (f32[4,1,8,128]{3,2,0,1:T(8,128)S(1)}, f32[4,1,8,128]{3,2,0,1:T(8,128)S(1)}, u32[]{:S(2)}, u32[]{:S(2)}) collective-permute-start(f32[4,1,8,128]{3,2,0,1:T(8,128)S(1)} %get-tuple-element.19), channel_id=1, source_target_pairs={{8,0},{16,8},{24,16},{32,24},{40,32},{48,40},{56,48},{64,56},{72,6... | collective-permute-start | bytes 49160 | tf_op jit(solution)/shard_map/ppermute | solution.py:463
  26.9 34.7 %collective-permute-start = (f32[4,1,8,128]{3,2,0,1:T(8,128)S(1)}, f32[4,1,8,128]{3,2,0,1:T(8,128)S(1)}, u32[]{:S(2)}, u32[]{:S(2)}) collective-permute-start(f32[4,1,8,128]{3,2,0,1:T(8,128)S(1)} %get-tuple-element.18), channel_id=1, source_target_pairs={{0,8},{8,16},{16,24},{24,32},{32,40},{40,48},{48,56},{56,64},{64,7... | collective-permute-start | bytes 49160 | tf_op jit(solution)/shard_map/ppermute | solution.py:461
  32.3 53.4 %collective-permute-start.4 = (f32[3,512,128]{2,1,0:T(8,128)S(1)}, f32[3,512,128]{2,1,0:T(8,128)S(1)}, u32[]{:S(2)}, u32[]{:S(2)}) collective-permute-start(f32[3,512,128]{2,1,0:T(8,128)S(1)} %broadcast_add_fusion.world_ref), channel_id=1, source_target_pairs={{0,127},{1,0},{2,1},{3,2},{4,3},{5,4},{6,5},{7,6},{8,7},{9,8},{10,... | collective-permute-start | bytes 2359304 | tf_op jit(solution)/shard_map/ppermute | solution.py:500
  61.6 9.9 %collective-permute-start.3 = (f32[4,10,1,128]{3,2,0,1:T(1,128)S(1)}, f32[4,10,1,128]{3,2,0,1:T(1,128)S(1)}, u32[]{:S(2)}, u32[]{:S(2)}) collective-permute-start(f32[4,10,1,128]{3,2,0,1:T(1,128)S(1)} %get-tuple-element.17), channel_id=1, source_target_pairs={{1,0},{2,1},{3,2},{4,3},{5,4},{6,5},{7,6},{9,8},{10,9},{11,10},{12... | collective-permute-start | bytes 61448 | tf_op jit(solution)/shard_map/ppermute | solution.py:463
  64.4 7.1 %collective-permute-start.2 = (f32[4,10,1,128]{3,2,0,1:T(1,128)S(1)}, f32[4,10,1,128]{3,2,0,1:T(1,128)S(1)}, u32[]{:S(2)}, u32[]{:S(2)}) collective-permute-start(f32[4,10,1,128]{3,2,0,1:T(1,128)S(1)} %get-tuple-element.16), channel_id=1, source_target_pairs={{0,1},{1,2},{2,3},{3,4},{4,5},{5,6},{6,7},{8,9},{9,10},{10,11},{11... | collective-permute-start | bytes 61448 | tf_op jit(solution)/shard_map/ppermute | solution.py:461
  83.6 1.3 copy-start.4
  84.9 0.8 copy-start.8
  85.8 87.3 %copy-start.11 = (f32[512,3]{0,1:T(4,128)S(1)}, f32[512,3]{0,1:T(4,128)}, u32[]{:S(2)}) copy-start(f32[512,3]{0,1:T(4,128)} %param.16) | copy-start | bytes 18436
  102.9 0.7 copy-start.6
  103.6 1.6 copy-start.5
  105.2 1.0 copy-start.9
  106.3 66.8 %copy-start.7 = (f32[512,128]{1,0:T(8,128)S(1)}, f32[512,128]{1,0:T(8,128)}, u32[]{:S(2)}) copy-start(f32[512,128]{1,0:T(8,128)} %copy-done.6) | copy-start | bytes 786436

commit v2 on v1

--- a/solution.py
+++ b/solution.py
@@ -19,8 +19,9 @@
 AXES = ("stream", "span")
 W = 128
 FEATS = 32
-ROWS = 49
+ROWS = 25
 UNROLL = 4
+GROUPS = 8
 DEAD = -30000.0
 BF = jnp.bfloat16
 F32 = jnp.float32
@@ -78,7 +79,7 @@
     return jnp.sum(v, axis=1, keepdims=True)
 
 
-def prep_kernel(dev_ref, blk_ref, dev_s, off_s, arm_ref, send_ref, rank_ref, buf, rank_s, sems):
+def prep_kernel(dev_ref, blk_ref, dev_s, off_s, arm_ref, first_ref, second_ref, rank_ref, buf, rank_s, sems):
     entries = dev_ref.shape[1]
     parts = entries // W
     dev = dev_ref[...]
@@ -101,8 +102,11 @@
     move.start()
     named = jnp.where(row == rank, blk_ref[...] + 1, 0).astype(F32).astype(BF)
     ids = lax.dot_general(hot_b, named, (((1,), (1,)), ((), ())), preferred_element_type=F32)
+    late = pltpu.roll(ids, W - 8, 1)
     for d in range(W):
-        buf[d * ROWS + 48 : d * ROWS + 49, :] = ids[d : d + 1, :]
+        for part, rows in enumerate((ids, late)):
+            spot = (part * W + d) * ROWS + 24
+            buf[spot : spot + 1, :] = rows[d : d + 1, :]
     move.wait()
 
     clumps = entries // 2
@@ -112,38 +116,41 @@
             for j in range(8):
                 c = i * 8 + j
                 e = k * clumps + c
-                base = dev_s[0, e] * ROWS + rank_s[0, e]
+                r = rank_s[0, e]
+                base = ((r >> 3) * W + dev_s[0, e]) * ROWS + (r & 7)
                 for q in range(3):
-                    buf[pl.ds(base + 16 * q, 1), :] = (
+                    buf[pl.ds(base + 8 * q, 1), :] = (
                         arm_ref[q, pl.ds(c, 1), :] + off_s[q, e]
                     )
         return carry
 
     lax.fori_loop(0, clumps // 8, step, 0)
-    out = pltpu.make_async_copy(buf, send_ref, sems.at[0])
-    out.start()
-    out.wait()
+    half = W * ROWS
+    one = pltpu.make_async_copy(buf.at[pl.ds(0, half)], first_ref, sems.at[0])
+    two = pltpu.make_async_copy(buf.at[pl.ds(half, half)], second_ref, sems.at[1])
+    one.start()
+    two.start()
+    one.wait()
+    two.wait()
 
 
 def prep(dev, blk, off, arms):
     entries = dev.shape[1]
     vm = pl.BlockSpec(memory_space=pltpu.VMEM)
     sm = pl.BlockSpec(memory_space=pltpu.SMEM)
-    hbm = pl.BlockSpec(memory_space=pl.ANY)
+    hbm = pl.BlockSpec(memory_space=pltpu.HBM)
+    send = jax.ShapeDtypeStruct((W * ROWS, W), F32)
     return pl.pallas_call(
         prep_kernel,
-        out_shape=(
-            jax.ShapeDtypeStruct((W * ROWS, W), F32),
-            jax.ShapeDtypeStruct((1, entries), jnp.int32),
-        ),
+        out_shape=(send, send, jax.ShapeDtypeStruct((1, entries), jnp.int32)),
         in_specs=[vm, vm, sm, sm, vm],
-        out_specs=(hbm, vm),
+        out_specs=(hbm, hbm, vm),
         scratch_shapes=[
-            pltpu.VMEM((W * ROWS, W), F32),
+            pltpu.VMEM((2 * W * ROWS, W), F32),
             pltpu.SMEM((1, entries), jnp.int32),
-            pltpu.SemaphoreType.DMA((1,)),
+            pltpu.SemaphoreType.DMA((2,)),
         ],
-        compiler_params=pltpu.CompilerParams(vmem_limit_bytes=24 << 20),
+        compiler_params=pltpu.CompilerParams(vmem_limit_bytes=16 << 20),
         name="prep",
     )(dev, blk, dev, off, arms)
 
@@ -240,7 +247,7 @@
             pltpu.VMEM((ext.shape[1], W, FEATS), BF),
             pltpu.VMEM((W, W), F32),
         ],
-        compiler_params=pltpu.CompilerParams(vmem_limit_bytes=24 << 20),
+        compiler_params=pltpu.CompilerParams(vmem_limit_bytes=14 << 20),
         name="density",
     )(ext, own, mass, vel)
 
@@ -253,8 +260,9 @@
     return out
 
 
-def contact_kernel(partner_s, arm_ref, world_ref, next_ref, out_ref, cand, gat, feat, right, lead, acc):
+def contact_kernel(partner_s, arm_ref, world_ref, next_ref, after_ref, out_ref, done_ref, cand, gat, feat, right, lead, acc):
     clumps = arm_ref.shape[1]
+    done_ref[...] = jnp.zeros_like(done_ref)
     cand[:, 0:clumps, :] = world_ref[...]
     cand[:, clumps : 2 * clumps, :] = next_ref[...]
     zero = jnp.zeros((8, W), F32)
@@ -310,15 +318,15 @@
     lax.fori_loop(0, clumps // (8 * UNROLL), group, 0)
 
 
-def contact(partner, arms, world, following):
+def contact(partner, arms, world, following, after):
     clumps = arms.shape[1]
     vm = pl.BlockSpec(memory_space=pltpu.VMEM)
     sm = pl.BlockSpec(memory_space=pltpu.SMEM)
     return pl.pallas_call(
         contact_kernel,
-        out_shape=jax.ShapeDtypeStruct((clumps, W), F32),
-        in_specs=[sm, vm, vm, vm],
-        out_specs=vm,
+        out_shape=(jax.ShapeDtypeStruct((clumps, W), F32), jax.ShapeDtypeStruct((8, W), F32)),
+        in_specs=[sm, vm, vm, vm, pl.BlockSpec(memory_space=pl.ANY)],
+        out_specs=(vm, vm),
         scratch_shapes=[
             pltpu.VMEM((3, 2 * clumps, W), F32),
             pltpu.VMEM((UNROLL * 24, W), F32),
@@ -327,21 +335,25 @@
             pltpu.VMEM((UNROLL * W, W), F32),
             pltpu.VMEM((UNROLL * 64, W), F32),
         ],
-        compiler_params=pltpu.CompilerParams(vmem_limit_bytes=24 << 20),
+        compiler_params=pltpu.CompilerParams(vmem_limit_bytes=10 << 20),
         name="contact",
-    )(partner, arms, world, following)
-
-
-def fluid_kernel(y_ref, table_ref, amp_ref, out_ref, names, names_s, right, acc, sems):
-    for t in range(2 * UNROLL):
+    )(partner, arms, world, following, after)
+
+
+def fluid_kernel(y_ref, table_ref, amp_ref, *rest):
+    *prior, out_ref, names, names_s, right, acc, sems = rest
+    for t in range(GROUPS):
         zero_tail(right, t * FEATS * 8)
     lane = lax.broadcasted_iota(jnp.int32, (8, W), 1)
     mine = (lane >> 4) == lax.broadcasted_iota(jnp.int32, (8, W), 0)
     place = lane & 15
-    devices = out_ref.shape[0] // 2
+    devices = W
+    step, first = len(prior) + 1, len(prior)
+    if prior:
+        out_ref[pl.ds(0, W, stride=2), :] = prior[0][...]
 
     def read(g, carry):
-        names[pl.ds(g, 1), :] = y_ref[pl.ds(g * ROWS + 48, 1), :].astype(jnp.int32) - 1
+        names[pl.ds(g, 1), :] = y_ref[pl.ds(g * ROWS + 24, 1), :].astype(jnp.int32) - 1
         return carry
 
     lax.fori_loop(0, devices, read, 0, unroll=8)
@@ -351,19 +363,19 @@
 
     def group(i, carry):
         ys, valids = [], []
-        for t in range(2 * UNROLL):
-            g = i * UNROLL + t // 2
-            at = g * ROWS + (t % 2) * 8
-            y = [y_ref[pl.ds(at + 16 * q, 8), :] for q in range(3)]
+        for t in range(GROUPS):
+            g = i * GROUPS + t
+            at = g * ROWS
+            y = [y_ref[pl.ds(at + 8 * q, 8), :] for q in range(3)]
             ys.append(y)
             u = [v - 0.5 for v in y]
             scaled = [split3(v * (2.0 * C_FLUID)) for v in u]
             put_rows(right, right_rows(*scaled, norm_of(*u, C_FLUID)), t * FEATS * 8)
-        for t in range(2 * UNROLL):
-            g = i * UNROLL + t // 2
+        for t in range(GROUPS):
+            g = i * GROUPS + t
             valid = jnp.zeros((1, W), jnp.int32)
             for j in range(8):
-                name = names_s[g, (t % 2) * 8 + j]
+                name = names_s[g, j]
                 valid = jnp.where((lane[0:1] >> 4) == j, name, valid)
                 b = jnp.maximum(name, 0)
                 kernel = gauss(table_ref[b], take_rows(right, j, t * FEATS * 8).astype(BF))
@@ -371,8 +383,8 @@
                 spot = 64 * t + 8 * j
                 acc[spot : spot + 8, :] = res[0:8] + res[8:16]
             valids.append(valid)
-        for t in range(2 * UNROLL):
-            g = i * UNROLL + t // 2
+        for t in range(GROUPS):
+            g = i * GROUPS + t
             y = ys[t]
             s = [acc[pl.ds(64 * t + q, 8, stride=8), :] for q in range(4)]
             cross = [y[1] * s[2] - y[2] * s[1], y[2] * s[0] - y[0] * s[2],
@@ -382,29 +394,29 @@
             for q, v in enumerate(s + cross + moment):
                 out = jnp.where(place == q, lane_sum(v), out)
             row = jnp.sum(jnp.where(mine, out, 0.0), axis=0, keepdims=True)
-            out_ref[pl.ds(2 * g + t % 2, 1), :] = jnp.where(valids[t] >= 0, row, 0.0)
+            out_ref[pl.ds(step * g + first, 1), :] = jnp.where(valids[t] >= 0, row, 0.0)
         return carry
 
-    lax.fori_loop(0, devices // UNROLL, group, 0)
-
-
-def fluid(spots, table, amp):
+    lax.fori_loop(0, devices // GROUPS, group, 0)
+
+
+def fluid(spots, table, amp, *prior):
     vm = pl.BlockSpec(memory_space=pltpu.VMEM)
     return pl.pallas_call(
         fluid_kernel,
-        out_shape=jax.ShapeDtypeStruct((2 * W, W), F32),
-        in_specs=[vm, vm, vm],
+        out_shape=jax.ShapeDtypeStruct(((len(prior) + 1) * W, W), F32),
+        in_specs=[vm] * (3 + len(prior)),
         out_specs=vm,
         scratch_shapes=[
             pltpu.VMEM((W, W), jnp.int32),
             pltpu.SMEM((W, W), jnp.int32),
-            pltpu.VMEM((2 * UNROLL * FEATS * 8, W), F32),
-            pltpu.VMEM((2 * UNROLL * 64, W), F32),
+            pltpu.VMEM((GROUPS * FEATS * 8, W), F32),
+            pltpu.VMEM((GROUPS * 64, W), F32),
             pltpu.SemaphoreType.DMA((1,)),
         ],
-        compiler_params=pltpu.CompilerParams(vmem_limit_bytes=24 << 20),
+        compiler_params=pltpu.CompilerParams(vmem_limit_bytes=12 << 20),
         name="fluid",
-    )(spots, table, amp)
+    )(spots, table, amp, *prior)
 
 
 def combine_kernel(dev_ref, rank_ref, off_ref, vel_ref, got_ref, contact_ref, out_ref):
@@ -445,7 +457,7 @@
         out_shape=jax.ShapeDtypeStruct((6, vel.shape[1]), F32),
         in_specs=[vm] * 6,
         out_specs=vm,
-        compiler_params=pltpu.CompilerParams(vmem_limit_bytes=24 << 20),
+        compiler_params=pltpu.CompilerParams(vmem_limit_bytes=14 << 20),
         name="combine",
     )(dev, rank, off, vel, got, touch)
 
@@ -465,6 +477,22 @@
             axis=dim,
         )
     return cells
+
+
+def gate_kernel(array_ref, after_ref, out_ref):
+    del array_ref, after_ref, out_ref
+
+
+def gated(array, after):
+    hbm = pl.BlockSpec(memory_space=pltpu.HBM)
+    return pl.pallas_call(
+        gate_kernel,
+        out_shape=jax.ShapeDtypeStruct(array.shape, array.dtype),
+        in_specs=[hbm, pl.BlockSpec(memory_space=pl.ANY)],
+        out_specs=hbm,
+        input_output_aliases={0: 0},
+        name="gate",
+    )(array, after)
 
 
 def swap_all(array):
@@ -490,27 +518,32 @@
     entries = 2 * clumps
     devices = lax.axis_size(AXES)
     arms = jnp.transpose(clump_arm, (1, 0, 2))
+    world = arms + clump_center.T[:, :, None]
+    following = lax.ppermute(world, AXES, [(i, (i + devices - 1) % devices) for i in range(devices)])
+    lanes = jnp.arange(width, dtype=jnp.int32)
+    live = jnp.where(lanes[None, None, :] < fluid_count[..., None], fluid_mass, 0.0)
+    planes = jnp.concatenate([jnp.moveaxis(fluid_pos, 2, 0), live[None]], axis=0)
+    tall = extended(planes, (("stream", 1),))
     dev = margin_device.T.reshape(1, entries)
     blk = margin_block.T.reshape(1, entries)
     off = jnp.transpose(margin_offset, (2, 1, 0)).reshape(3, entries)
     vel = clump_vel.T
-    send, rank = prep(dev, blk, off, arms)
-    got = swap_all(send.reshape(devices, 1, ROWS * width))
-    world = arms + clump_center.T[:, :, None]
-    following = lax.ppermute(world, AXES, [(i, (i + devices - 1) % devices) for i in range(devices)])
-    touch = contact(contact_partner.reshape(1, clumps), arms, world, following)
-    lanes = jnp.arange(width, dtype=jnp.int32)
-    live = jnp.where(lanes[None, None, :] < fluid_count[..., None], fluid_mass, 0.0)
-    planes = jnp.concatenate([jnp.moveaxis(fluid_pos, 2, 0), live[None]], axis=0)
-    ext = extended(planes, (("stream", 1), ("span", 2)))
+    dev, tall = lax.optimization_barrier((dev, tall))
+    ext = extended(tall, (("span", 2),))
+    first, second, rank = prep(dev, blk, off, arms)
+    first, second, ext, following = lax.optimization_barrier((first, second, ext, following))
+    got_first = swap_all(first.reshape(devices, 1, ROWS * width))
     ext = ext.reshape(4, (rows_x + 2) * (rows_y + 2), width)
     ext = jnp.pad(ext, ((0, 0), (0, 4), (0, 0)))
     own = planes.reshape(4, blocks, width)
     speed = jnp.moveaxis(fluid_vel, 2, 0).reshape(3, blocks, width)
     dens, table, amp = density(ext, own, fluid_mass.reshape(blocks, width), speed)
-    got, touch = lax.optimization_barrier((got, touch))
-    sums = fluid(got.reshape(devices * ROWS, width), table, amp)
-    back = swap_all(sums.reshape(devices, 1, 2 * width)).reshape(2 * devices, width)
+    touch, done = contact(contact_partner.reshape(1, clumps), arms, world, following, dens)
+    second = gated(second, done)
+    got_second = swap_all(second.reshape(devices, 1, ROWS * width))
+    one = fluid(got_first.reshape(devices * ROWS, width), table, amp)
+    both = fluid(got_second.reshape(devices * ROWS, width), table, amp, one)
+    back = swap_all(both.reshape(devices, 1, 2 * width)).reshape(2 * devices, width)
     loads = combine(dev, rank, off, vel, back, touch)
     return (dens.reshape(rows_x, rows_y, width), loads)
 

time: 175 us -> 161 us (0.920)
  waiting for transfers between devices: 31.5 us -> 3.4 us
  starting transfers between devices: 24.5 us -> 35 us
  Pallas kernels: 87.8 us -> 94.3 us
  local copies, waits for them, and re-layouts: 10.6 us -> 4.87 us
  blocking collectives: 17.6 us -> 19.5 us
    ppermute x2, waiting for transfers between devices: 31.4 us -> 3.39 us  [extended(): lax.ppermute(head, axis, [((i + 1) % count, i) for i in range(ends)])]
    all_to_all x1 -> x2, starting transfers between devices: 11.5 us -> 18.6 us  [swap_all(): return lax.all_to_all(array, AXES, split_axis=0, concat_axis=0, tiled=True)]
    pallas_call x3 -> x5, Pallas kernels: 74.6 us -> 81.1 us  [the longest x2 53.8 us: fluid(): pl.pallas_call(fluid_kernel, out_shape=jax.ShapeDtypeStruct(((len(prior)...]
    unnamed x35 -> x39, local copies, waits for them, and re-layouts: 10.5 us -> 4.71 us
    ppermute x2, starting transfers between devices: 4.2 us -> 7.02 us  [extended(): lax.ppermute(head, axis, [((i + 1) % count, i) for i in range(ends)])]
    all_to_all x1, blocking collectives: 17.6 us -> 19.5 us  [swap_all(): return lax.all_to_all(array, AXES, split_axis=0, concat_axis=0, tiled=True)]
  transfers between devices with their start and end apart: 6 -> 7, of which waited for: 2 -> 1; matrix products, arithmetic and copies ran while one was open for 1% -> 1% of each run, Pallas kernels for 17% -> 41%
where the time goes in v2:
time: 161 us; the launch traced here: 160 us
  Pallas kernels  94.3 us (59%)
  starting transfers between devices  35 us (22%)
  blocking collectives  19.5 us (12%)
  local copies, waits for them, and re-layouts  4.87 us (3%)
  waiting for transfers between devices  3.4 us (2%)
  other arithmetic  2.42 us (2%)
    pallas_call x2, Pallas kernels, fluid(): pl.pallas_call(fluid_kernel, out_shape=jax.ShapeDtypeStruct(((len(prior)...  53.8 us
    all_to_all x1, blocking collectives, swap_all(): return lax.all_to_all(array, AXES, split_axis=0, concat_axis=0, tiled=True)  19.5 us
    all_to_all x2, starting transfers between devices, swap_all(): return lax.all_to_all(array, AXES, split_axis=0, concat_axis=0, tiled=True)  18.6 us
    pallas_call x1, Pallas kernels, contact(): pl.pallas_call(contact_kernel, out_shape=(jax.ShapeDtypeStruct((clumps, W...  17.1 us
    pallas_call x1, Pallas kernels, density(): pl.pallas_call(density_kernel, out_shape=(jax.ShapeDtypeStruct((blocks, W...  11.9 us
    pallas_call x1, Pallas kernels, prep(): pl.pallas_call(prep_kernel, out_shape=(send, send, jax.ShapeDtypeStruct((...  10.1 us
    ppermute x2, starting transfers between devices, extended(): lax.ppermute(tail, axis, [(i, (i + 1) % count) for i in range(ends)])  7.88 us
    ppermute x2, starting transfers between devices, extended(): lax.ppermute(head, axis, [((i + 1) % count, i) for i in range(ends)])  7.02 us
  transfers between devices with their start and end apart: 7, of which 1 were waited for; matrix products, arithmetic and copies ran while one was open for 1% of the time, Pallas kernels for 41%

profile of v2, /device:TPU:1, one launch (start us, length us, event | category | flops | bytes accessed | tf_op | source)
XLA Modules:
  0.0 160.5 jit_solution(15694507322351957319)
XLA Ops:
  0.6 0.0 copy-start
  0.6 0.0 copy-start.1
  0.7 0.0 copy-start.14
  0.7 0.0 copy-start.16
  0.7 0.0 copy-start.17
  0.7 0.0 copy-start.15
  0.7 1.5 broadcast_add_fusion.world_ref
  2.2 0.0 copy-start.3
  2.2 1.5 collective-permute-start.4
  3.7 0.8 fusion.1
  4.5 0.0 copy-done.14
  4.6 3.2 %collective-permute-start = (f32[4,1,8,128]{3,2,0,1:T(8,128)S(1)}, f32[4,1,8,128]{3,2,0,1:T(8,128)S(1)}, u32[]{:S(2)}, u32[]{:S(2)}) collective-permute-start(f32[4,1,8,128]{3,2,0,1:T(8,128)S(1)} %get-tuple-element.32), channel_id=1, source_target_pairs={{0,8},{8,16},{16,24},{24,32},{32,40},{40,48},{48,56},{56,64},{64,7... | collective-permute-start | bytes 49160 | tf_op jit(solution)/shard_map/ppermute | solution.py:473
  7.8 1.3 collective-permute-start.1
  9.1 0.0 copy-done.16
  9.1 0.0 collective-permute-done
  9.1 3.4 %collective-permute-done.1 = f32[4,1,8,128]{3,2,0,1:T(8,128)S(1)} collective-permute-done((f32[4,1,8,128]{3,2,0,1:T(8,128)S(1)}, f32[4,1,8,128]{3,2,0,1:T(8,128)S(1)}, u32[]{:S(2)}, u32[]{:S(2)}) %collective-permute-start.1) | collective-permute-done | bytes 16416 | tf_op jit(solution)/shard_map/ppermute | solution.py:475
  12.5 4.7 %collective-permute-start.2 = (f32[4,10,1,128]{3,2,0,1:T(1,128)S(1)}, f32[4,10,1,128]{3,2,0,1:T(1,128)S(1)}, u32[]{:S(2)}, u32[]{:S(2)}) collective-permute-start(f32[4,10,1,128]{3,2,0,1:T(1,128)S(1)} %get-tuple-element.30), channel_id=1, source_target_pairs={{0,1},{1,2},{2,3},{3,4},{4,5},{5,6},{6,7},{8,9},{9,10},{10,11},{11... | collective-permute-start | bytes 61448 | tf_op jit(solution)/shard_map/ppermute | solution.py:473
  17.2 5.7 %collective-permute-start.3 = (f32[4,10,1,128]{3,2,0,1:T(1,128)S(1)}, f32[4,10,1,128]{3,2,0,1:T(1,128)S(1)}, u32[]{:S(2)}, u32[]{:S(2)}) collective-permute-start(f32[4,10,1,128]{3,2,0,1:T(1,128)S(1)} %get-tuple-element.31), channel_id=1, source_target_pairs={{1,0},{2,1},{3,2},{4,3},{5,4},{6,5},{7,6},{9,8},{10,9},{11,10},{12... | collective-permute-start | bytes 61448 | tf_op jit(solution)/shard_map/ppermute | solution.py:475
  23.0 0.0 copy-done.17
  23.0 0.0 copy-done.15
  23.0 0.0 copy-done.1
  23.0 10.1 %prep.1 = (f32[3200,128]{1,0:T(8,128)}, f32[3200,128]{1,0:T(8,128)S(1)}, s32[1,1024]{1,0:T(1,128)S(1)}) custom-call(s32[1,1024]{1,0:T(1,128)S(1)} %bitcast.49, s32[1,1024]{1,0:T(1,128)S(1)} %bitcast.53, s32[1,1024]{1,0:T(1,128)S(1)} %bitcast.50, f32[3,1024]{1,0:T(4,128)S(1)} %bitcast.46, f32[3,512,128]{2,1,0:T(8,128)S(1)} %bitcast.41), custom_call_target="tpu_custom_call" | custom-call | tf_op jit(solution)/shard_map/prep/pallas_call | solution.py:143
  33.2 0.0 copy-done.3
  33.2 1.2 copy-done.2
  34.4 0.0 collective-permute-done.2
  34.4 0.0 collective-permute-done.3
  34.4 0.1 pad_maximum_fusion
  34.4 0.0 collective-permute-done.4.next_ref
  34.4 0.9 copy-done.5
  35.3 8.4 %all-to-all-start.1 = ((f32[128,1,3200]{2,1,0:T(1,128)}), f32[128,1,3200]{2,1,0:T(1,128)}, u32[]{:S(2)}, u32[]{:S(2)}) async-start(f32[128,1,3200]{2,1,0:T(1,128)} %bitcast.19), calls=%async_computation.1 | async-start | bytes 3276800 | tf_op jit(solution)/shard_map/all_to_all | solution.py:499
  43.8 0.0 copy-start.9
  43.8 0.0 copy-start.13
  43.9 0.1 copy.24
  44.0 0.5 copy-done.9
  44.5 11.9 %density.1 = (f32[64,128]{1,0:T(8,128)}, bf16[64,128,32]{2,1,0:T(8,128)(2,1)S(1)}, bf16[64,16,256]{2,1,0:T(8,128)(2,1)S(1)}) custom-call(f32[4,104,128]{2,1,0:T(8,128)S(1)} %pad.4.ext_ref, f32[4,64,128]{2,1,0:T(8,128)S(1)} %pad_maximum_fusion.2.own_ref, f32[64,128]{1,0:T(8,128)S(1)} %bitcast.48, f32[3,64,128]{2,1,0:T(8,128)S(1)} %copy_bitcast_fusion.vel_ref), custom_call_target="tpu_custom_call" | custom-call | tf_op jit(solution)/shard_map/density/pallas_call | solution.py:234
  56.4 0.0 copy-done.6
  56.4 0.8 copy-done.10
  57.2 17.1 %contact.1 = (f32[512,128]{1,0:T(8,128)S(1)}, f32[8,128]{1,0:T(8,128)S(1)}) custom-call(s32[1,512]{1,0:T(1,128)S(1)} %bitcast.55, f32[3,512,128]{2,1,0:T(8,128)S(1)} %bitcast.42, f32[3,512,128]{2,1,0:T(8,128)S(1)} %copy-done.4, f32[3,512,128]{2,1,0:T(8,128)S(1)} %copy-done.6, f32[64,128]{1,0:T(8,128)S(1)} %copy-done.10), custom_call_target="tpu_custom_call" | custom-call | tf_op jit(solution)/shard_map/contact/pallas_call | solution.py:325
  74.3 0.7 copy-done.7
  75.0 0.6 copy-done.12
  75.6 0.0 all-to-all-done.1
  75.6 10.2 %all-to-all-start = ((f32[128,1,3200]{2,1,0:T(1,128)}), f32[128,1,3200]{2,1,0:T(1,128)}, u32[]{:S(2)}, u32[]{:S(2)}) async-start(f32[128,1,3200]{2,1,0:T(1,128)} %bitcast.43), calls=%async_computation | async-start | bytes 3276800 | tf_op jit(solution)/shard_map/all_to_all | solution.py:499
  85.8 26.9 %fluid.2.rest_0_ = f32[128,128]{1,0:T(8,128)S(1)} custom-call(f32[3200,128]{1,0:T(8,128)} %bitcast.20.y_ref, bf16[64,128,32]{2,1,0:T(8,128)(2,1)S(1)} %get-tuple-element.26.table_ref, bf16[64,16,256]{2,1,0:T(8,128)(2,1)S(1)} %get-tuple-element.27.amp_ref), custom_call_target="tpu_custom_call" | custom-call | tf_op jit(solution)/shard_map/fluid/pallas_call | solution.py:405
  112.7 0.0 all-to-all-done
  112.7 0.0 copy-start.11
  112.7 26.9 %fluid.3 = f32[256,128]{1,0:T(8,128)S(1)} custom-call(f32[3200,128]{1,0:T(8,128)} %bitcast.18.y_ref, bf16[64,128,32]{2,1,0:T(8,128)(2,1)S(1)} %get-tuple-element.26.table_ref, bf16[64,16,256]{2,1,0:T(8,128)(2,1)S(1)} %get-tuple-element.27.amp_ref, f32[128,128]{1,0:T(8,128)S(1)} %fluid.2.rest_0_), custom_call_target="tpu_custom_call" | custom-call | tf_op jit(solution)/shard_map/fluid/pallas_call | solution.py:405
  139.7 19.5 %all_to_all.15 = f32[128,1,256]{2,1,0:T(1,128)S(1)} all-to-all(f32[128,1,256]{2,1,0:T(1,128)S(1)} %bitcast.45), channel_id=1, replica_groups=mesh['stream'=16,'span'=8] {'stream','span'}, dimensions={0} | all-to-all | bytes 262144 | tf_op jit(solution)/shard_map/all_to_all | solution.py:499
  159.2 1.3 combine.1
  (25 shorter events, 0.1 us)
Async XLA Ops:
  0.6 43.2 %copy-start = (f32[8,8,3,128]{3,1,2,0:T(8,128)S(1)}, f32[8,8,3,128]{3,1,2,0:T(8,128)}, u32[]{:S(2)}) copy-start(f32[8,8,3,128]{3,1,2,0:T(8,128)} %param.12) | copy-start | bytes 294916
  0.6 22.4 %copy-start.1 = (f32[512,3,128]{2,0,1:T(8,128)S(1)}, f32[512,3,128]{2,0,1:T(8,128)}, u32[]{:S(2)}) copy-start(f32[512,3,128]{2,0,1:T(8,128)} %param.17) | copy-start | bytes 2359300
  0.7 3.9 %copy-start.14 = (f32[8,8,3,128]{3,1,2,0:T(8,128)S(1)}, f32[8,8,3,128]{3,1,2,0:T(8,128)}, u32[]{:S(2)}) copy-start(f32[8,8,3,128]{3,1,2,0:T(8,128)} %param.11) | copy-start | bytes 294916
  0.7 8.4 %copy-start.16 = (s32[512,2]{0,1:T(2,128)S(1)}, s32[512,2]{0,1:T(2,128)}, u32[]{:S(2)}) copy-start(s32[512,2]{0,1:T(2,128)} %param.18) | copy-start | bytes 12292
  0.7 22.3 %copy-start.17 = (s32[512,2]{0,1:T(2,128)S(1)}, s32[512,2]{0,1:T(2,128)}, u32[]{:S(2)}) copy-start(s32[512,2]{0,1:T(2,128)} %param.19) | copy-start | bytes 12292
  0.7 22.3 %copy-start.15 = (f32[512,2,3]{0,1,2:T(2,128)S(1)}, f32[512,2,3]{0,1,2:T(2,128)}, u32[]{:S(2)}) copy-start(f32[512,2,3]{0,1,2:T(2,128)} %param.20) | copy-start | bytes 36868
  2.2 31.0 %copy-start.3 = (f32[3,512,128]{2,1,0:T(8,128)}, f32[3,512,128]{2,1,0:T(8,128)S(1)}, u32[]{:S(2)}) copy-start(f32[3,512,128]{2,1,0:T(8,128)S(1)} %broadcast_add_fusion.world_ref) | copy-start | bytes 2359300
  2.2 32.2 %collective-permute-start.4 = (f32[3,512,128]{2,1,0:T(8,128)S(1)}, f32[3,512,128]{2,1,0:T(8,128)S(1)}, u32[]{:S(2)}, u32[]{:S(2)}) collective-permute-start(f32[3,512,128]{2,1,0:T(8,128)S(1)} %broadcast_add_fusion.world_ref), channel_id=1, source_target_pairs={{0,127},{1,0},{2,1},{3,2},{4,3},{5,4},{6,5},{7,6},{8,7},{9,8},{10,... | collective-permute-start | bytes 2359304 | tf_op jit(solution)/shard_map/ppermute | solution.py:522
  4.6 4.5 %collective-permute-start = (f32[4,1,8,128]{3,2,0,1:T(8,128)S(1)}, f32[4,1,8,128]{3,2,0,1:T(8,128)S(1)}, u32[]{:S(2)}, u32[]{:S(2)}) collective-permute-start(f32[4,1,8,128]{3,2,0,1:T(8,128)S(1)} %get-tuple-element.32), channel_id=1, source_target_pairs={{0,8},{8,16},{16,24},{24,32},{32,40},{40,48},{48,56},{56,64},{64,7... | collective-permute-start | bytes 49160 | tf_op jit(solution)/shard_map/ppermute | solution.py:473
  7.8 4.7 %collective-permute-start.1 = (f32[4,1,8,128]{3,2,0,1:T(8,128)S(1)}, f32[4,1,8,128]{3,2,0,1:T(8,128)S(1)}, u32[]{:S(2)}, u32[]{:S(2)}) collective-permute-start(f32[4,1,8,128]{3,2,0,1:T(8,128)S(1)} %get-tuple-element.33), channel_id=1, source_target_pairs={{8,0},{16,8},{24,16},{32,24},{40,32},{48,40},{56,48},{64,56},{72,6... | collective-permute-start | bytes 49160 | tf_op jit(solution)/shard_map/ppermute | solution.py:475
  12.5 21.8 %collective-permute-start.2 = (f32[4,10,1,128]{3,2,0,1:T(1,128)S(1)}, f32[4,10,1,128]{3,2,0,1:T(1,128)S(1)}, u32[]{:S(2)}, u32[]{:S(2)}) collective-permute-start(f32[4,10,1,128]{3,2,0,1:T(1,128)S(1)} %get-tuple-element.30), channel_id=1, source_target_pairs={{0,1},{1,2},{2,3},{3,4},{4,5},{5,6},{6,7},{8,9},{9,10},{10,11},{11... | collective-permute-start | bytes 61448 | tf_op jit(solution)/shard_map/ppermute | solution.py:473
  17.2 17.1 %collective-permute-start.3 = (f32[4,10,1,128]{3,2,0,1:T(1,128)S(1)}, f32[4,10,1,128]{3,2,0,1:T(1,128)S(1)}, u32[]{:S(2)}, u32[]{:S(2)}) collective-permute-start(f32[4,10,1,128]{3,2,0,1:T(1,128)S(1)} %get-tuple-element.31), channel_id=1, source_target_pairs={{1,0},{2,1},{3,2},{4,3},{5,4},{6,5},{7,6},{9,8},{10,9},{11,10},{12... | collective-permute-start | bytes 61448 | tf_op jit(solution)/shard_map/ppermute | solution.py:475
  33.2 1.2 copy-start.2
  34.4 0.9 copy-start.5
  35.3 40.3 %all-to-all-start.1 = ((f32[128,1,3200]{2,1,0:T(1,128)}), f32[128,1,3200]{2,1,0:T(1,128)}, u32[]{:S(2)}, u32[]{:S(2)}) async-start(f32[128,1,3200]{2,1,0:T(1,128)} %bitcast.19), calls=%async_computation.1 | async-start | bytes 3276800 | tf_op jit(solution)/shard_map/all_to_all | solution.py:499
  43.8 0.8 copy-start.9
  43.8 12.7 %copy-start.4 = (f32[3,512,128]{2,1,0:T(8,128)S(1)}, f32[3,512,128]{2,1,0:T(8,128)}, u32[]{:S(2)}) copy-start(f32[3,512,128]{2,1,0:T(8,128)} %copy-done.3) | copy-start | bytes 2359300
  43.8 12.7 %copy-start.6 = (f32[3,512,128]{2,1,0:T(8,128)S(1)}, f32[3,512,128]{2,1,0:T(8,128)}, u32[]{:S(2)}) copy-start(f32[3,512,128]{2,1,0:T(8,128)} %copy-done.5) | copy-start | bytes 2359300
  43.8 12.6 %copy-start.13 = (s32[512]{0:T(512)S(1)}, s32[512]{0:T(512)}, u32[]{:S(2)}) copy-start(s32[512]{0:T(512)} %param.21) | copy-start | bytes 6148
  56.4 0.8 copy-start.10
  74.3 0.7 copy-start.7
  75.0 0.6 copy-start.12
  75.6 37.1 %all-to-all-start = ((f32[128,1,3200]{2,1,0:T(1,128)}), f32[128,1,3200]{2,1,0:T(1,128)}, u32[]{:S(2)}, u32[]{:S(2)}) async-start(f32[128,1,3200]{2,1,0:T(1,128)} %bitcast.43), calls=%async_computation | async-start | bytes 3276800 | tf_op jit(solution)/shard_map/all_to_all | solution.py:499
  112.7 46.5 %copy-start.8 = (f32[512,128]{1,0:T(8,128)S(1)}, f32[512,128]{1,0:T(8,128)}, u32[]{:S(2)}) copy-start(f32[512,128]{1,0:T(8,128)} %copy-done.7) | copy-start | bytes 786436
  112.7 46.5 %copy-start.11 = (f32[512,3]{0,1:T(4,128)S(1)}, f32[512,3]{0,1:T(4,128)}, u32[]{:S(2)}) copy-start(f32[512,3]{0,1:T(4,128)} %param.16) | copy-start | bytes 18436

commit v3 on v1

--- a/solution.py
+++ b/solution.py
@@ -21,6 +21,7 @@
 FEATS = 32
 ROWS = 49
 UNROLL = 4
+GROUPS = 16
 DEAD = -30000.0
 BF = jnp.bfloat16
 F32 = jnp.float32
@@ -129,7 +130,7 @@
     entries = dev.shape[1]
     vm = pl.BlockSpec(memory_space=pltpu.VMEM)
     sm = pl.BlockSpec(memory_space=pltpu.SMEM)
-    hbm = pl.BlockSpec(memory_space=pl.ANY)
+    hbm = pl.BlockSpec(memory_space=pltpu.HBM)
     return pl.pallas_call(
         prep_kernel,
         out_shape=(
@@ -143,7 +144,7 @@
             pltpu.SMEM((1, entries), jnp.int32),
             pltpu.SemaphoreType.DMA((1,)),
         ],
-        compiler_params=pltpu.CompilerParams(vmem_limit_bytes=24 << 20),
+        compiler_params=pltpu.CompilerParams(vmem_limit_bytes=40 << 20),
         name="prep",
     )(dev, blk, dev, off, arms)
 
@@ -240,7 +241,7 @@
             pltpu.VMEM((ext.shape[1], W, FEATS), BF),
             pltpu.VMEM((W, W), F32),
         ],
-        compiler_params=pltpu.CompilerParams(vmem_limit_bytes=24 << 20),
+        compiler_params=pltpu.CompilerParams(vmem_limit_bytes=14 << 20),
         name="density",
     )(ext, own, mass, vel)
 
@@ -253,8 +254,9 @@
     return out
 
 
-def contact_kernel(partner_s, arm_ref, world_ref, next_ref, out_ref, cand, gat, feat, right, lead, acc):
+def contact_kernel(partner_s, arm_ref, world_ref, next_ref, after_ref, out_ref, done_ref, cand, gat, feat, right, lead, acc):
     clumps = arm_ref.shape[1]
+    done_ref[...] = jnp.zeros_like(done_ref)
     cand[:, 0:clumps, :] = world_ref[...]
     cand[:, clumps : 2 * clumps, :] = next_ref[...]
     zero = jnp.zeros((8, W), F32)
@@ -310,15 +312,15 @@
     lax.fori_loop(0, clumps // (8 * UNROLL), group, 0)
 
 
-def contact(partner, arms, world, following):
+def contact(partner, arms, world, following, after):
     clumps = arms.shape[1]
     vm = pl.BlockSpec(memory_space=pltpu.VMEM)
     sm = pl.BlockSpec(memory_space=pltpu.SMEM)
     return pl.pallas_call(
         contact_kernel,
-        out_shape=jax.ShapeDtypeStruct((clumps, W), F32),
-        in_specs=[sm, vm, vm, vm],
-        out_specs=vm,
+        out_shape=(jax.ShapeDtypeStruct((clumps, W), F32), jax.ShapeDtypeStruct((8, W), F32)),
+        in_specs=[sm, vm, vm, vm, pl.BlockSpec(memory_space=pl.ANY)],
+        out_specs=(vm, vm),
         scratch_shapes=[
             pltpu.VMEM((3, 2 * clumps, W), F32),
             pltpu.VMEM((UNROLL * 24, W), F32),
@@ -327,13 +329,20 @@
             pltpu.VMEM((UNROLL * W, W), F32),
             pltpu.VMEM((UNROLL * 64, W), F32),
         ],
-        compiler_params=pltpu.CompilerParams(vmem_limit_bytes=24 << 20),
+        compiler_params=pltpu.CompilerParams(vmem_limit_bytes=10 << 20),
         name="contact",
-    )(partner, arms, world, following)
-
-
-def fluid_kernel(y_ref, table_ref, amp_ref, out_ref, names, names_s, right, acc, sems):
-    for t in range(2 * UNROLL):
+    )(partner, arms, world, following, after)
+
+
+def fluid_kernel(y_ref, table_hbm, amp_hbm, after_ref, out_ref, names, names_s, right, acc,
+                 table_ref, amp_ref, sems):
+    load = [
+        pltpu.make_async_copy(table_hbm, table_ref, sems.at[1]),
+        pltpu.make_async_copy(amp_hbm, amp_ref, sems.at[2]),
+    ]
+    for copy in load:
+        copy.start()
+    for t in range(GROUPS):
         zero_tail(right, t * FEATS * 8)
     lane = lax.broadcasted_iota(jnp.int32, (8, W), 1)
     mine = (lane >> 4) == lax.broadcasted_iota(jnp.int32, (8, W), 0)
@@ -348,19 +357,21 @@
     move = pltpu.make_async_copy(names, names_s, sems.at[0])
     move.start()
     move.wait()
+    for copy in load:
+        copy.wait()
 
     def group(i, carry):
         ys, valids = [], []
-        for t in range(2 * UNROLL):
-            g = i * UNROLL + t // 2
+        for t in range(GROUPS):
+            g = i * (GROUPS // 2) + t // 2
             at = g * ROWS + (t % 2) * 8
             y = [y_ref[pl.ds(at + 16 * q, 8), :] for q in range(3)]
             ys.append(y)
             u = [v - 0.5 for v in y]
             scaled = [split3(v * (2.0 * C_FLUID)) for v in u]
             put_rows(right, right_rows(*scaled, norm_of(*u, C_FLUID)), t * FEATS * 8)
-        for t in range(2 * UNROLL):
-            g = i * UNROLL + t // 2
+        for t in range(GROUPS):
+            g = i * (GROUPS // 2) + t // 2
             valid = jnp.zeros((1, W), jnp.int32)
             for j in range(8):
                 name = names_s[g, (t % 2) * 8 + j]
@@ -371,8 +382,8 @@
                 spot = 64 * t + 8 * j
                 acc[spot : spot + 8, :] = res[0:8] + res[8:16]
             valids.append(valid)
-        for t in range(2 * UNROLL):
-            g = i * UNROLL + t // 2
+        for t in range(GROUPS):
+            g = i * (GROUPS // 2) + t // 2
             y = ys[t]
             s = [acc[pl.ds(64 * t + q, 8, stride=8), :] for q in range(4)]
             cross = [y[1] * s[2] - y[2] * s[1], y[2] * s[0] - y[0] * s[2],
@@ -385,26 +396,29 @@
             out_ref[pl.ds(2 * g + t % 2, 1), :] = jnp.where(valids[t] >= 0, row, 0.0)
         return carry
 
-    lax.fori_loop(0, devices // UNROLL, group, 0)
-
-
-def fluid(spots, table, amp):
+    lax.fori_loop(0, devices // (GROUPS // 2), group, 0)
+
+
+def fluid(spots, table, amp, after):
     vm = pl.BlockSpec(memory_space=pltpu.VMEM)
+    hbm = pl.BlockSpec(memory_space=pltpu.HBM)
     return pl.pallas_call(
         fluid_kernel,
         out_shape=jax.ShapeDtypeStruct((2 * W, W), F32),
-        in_specs=[vm, vm, vm],
+        in_specs=[vm, hbm, hbm, hbm],
         out_specs=vm,
         scratch_shapes=[
             pltpu.VMEM((W, W), jnp.int32),
             pltpu.SMEM((W, W), jnp.int32),
-            pltpu.VMEM((2 * UNROLL * FEATS * 8, W), F32),
-            pltpu.VMEM((2 * UNROLL * 64, W), F32),
-            pltpu.SemaphoreType.DMA((1,)),
+            pltpu.VMEM((GROUPS * FEATS * 8, W), F32),
+            pltpu.VMEM((GROUPS * 64, W), F32),
+            pltpu.VMEM(table.shape, BF),
+            pltpu.VMEM(amp.shape, BF),
+            pltpu.SemaphoreType.DMA((3,)),
         ],
-        compiler_params=pltpu.CompilerParams(vmem_limit_bytes=24 << 20),
+        compiler_params=pltpu.CompilerParams(vmem_limit_bytes=18 << 20),
         name="fluid",
-    )(spots, table, amp)
+    )(spots, table, amp, after)
 
 
 def combine_kernel(dev_ref, rank_ref, off_ref, vel_ref, got_ref, contact_ref, out_ref):
@@ -445,7 +459,7 @@
         out_shape=jax.ShapeDtypeStruct((6, vel.shape[1]), F32),
         in_specs=[vm] * 6,
         out_specs=vm,
-        compiler_params=pltpu.CompilerParams(vmem_limit_bytes=24 << 20),
+        compiler_params=pltpu.CompilerParams(vmem_limit_bytes=14 << 20),
         name="combine",
     )(dev, rank, off, vel, got, touch)
 
@@ -490,26 +504,28 @@
     entries = 2 * clumps
     devices = lax.axis_size(AXES)
     arms = jnp.transpose(clump_arm, (1, 0, 2))
+    world = arms + clump_center.T[:, :, None]
+    following = lax.ppermute(world, AXES, [(i, (i + devices - 1) % devices) for i in range(devices)])
+    lanes = jnp.arange(width, dtype=jnp.int32)
+    live = jnp.where(lanes[None, None, :] < fluid_count[..., None], fluid_mass, 0.0)
+    planes = jnp.concatenate([jnp.moveaxis(fluid_pos, 2, 0), live[None]], axis=0)
+    tall = extended(planes, (("stream", 1),))
     dev = margin_device.T.reshape(1, entries)
     blk = margin_block.T.reshape(1, entries)
     off = jnp.transpose(margin_offset, (2, 1, 0)).reshape(3, entries)
     vel = clump_vel.T
+    dev, tall = lax.optimization_barrier((dev, tall))
+    ext = extended(tall, (("span", 2),))
     send, rank = prep(dev, blk, off, arms)
+    send, ext, following = lax.optimization_barrier((send, ext, following))
     got = swap_all(send.reshape(devices, 1, ROWS * width))
-    world = arms + clump_center.T[:, :, None]
-    following = lax.ppermute(world, AXES, [(i, (i + devices - 1) % devices) for i in range(devices)])
-    touch = contact(contact_partner.reshape(1, clumps), arms, world, following)
-    lanes = jnp.arange(width, dtype=jnp.int32)
-    live = jnp.where(lanes[None, None, :] < fluid_count[..., None], fluid_mass, 0.0)
-    planes = jnp.concatenate([jnp.moveaxis(fluid_pos, 2, 0), live[None]], axis=0)
-    ext = extended(planes, (("stream", 1), ("span", 2)))
     ext = ext.reshape(4, (rows_x + 2) * (rows_y + 2), width)
     ext = jnp.pad(ext, ((0, 0), (0, 4), (0, 0)))
     own = planes.reshape(4, blocks, width)
     speed = jnp.moveaxis(fluid_vel, 2, 0).reshape(3, blocks, width)
     dens, table, amp = density(ext, own, fluid_mass.reshape(blocks, width), speed)
-    got, touch = lax.optimization_barrier((got, touch))
-    sums = fluid(got.reshape(devices * ROWS, width), table, amp)
+    touch, done = contact(contact_partner.reshape(1, clumps), arms, world, following, dens)
+    sums = fluid(got.reshape(devices * ROWS, width), table, amp, done)
     back = swap_all(sums.reshape(devices, 1, 2 * width)).reshape(2 * devices, width)
     loads = combine(dev, rank, off, vel, back, touch)
     return (dens.reshape(rows_x, rows_y, width), loads)

time: 175 us -> 152 us (0.87)
  waiting for transfers between devices: 31.5 us -> 7.62 us
  local copies, waits for them, and re-layouts: 10.6 us -> 16.6 us
  Pallas kernels: 87.8 us -> 82 us
  other arithmetic: 1.59 us -> 4.71 us
  blocking collectives: 17.6 us -> 14.7 us
    ppermute x2, waiting for transfers between devices: 31.4 us -> 2.72 us  [extended(): lax.ppermute(head, axis, [((i + 1) % count, i) for i in range(ends)])]
    pallas_call x1, Pallas kernels: 49.2 us -> 43.4 us  [fluid(): pl.pallas_call(fluid_kernel, out_shape=jax.ShapeDtypeStruct((2 * W, W), F...]
    unnamed x35 -> x41, local copies, waits for them, and re-layouts: 10.5 us -> 15.5 us
    all_to_all x1, waiting for transfers between devices: 0.01 us -> 4.89 us  [swap_all(): return lax.all_to_all(array, AXES, split_axis=0, concat_axis=0, tiled=True)]
    all_to_all x1, starting transfers between devices: 11.5 us -> 8.02 us  [swap_all(): return lax.all_to_all(array, AXES, split_axis=0, concat_axis=0, tiled=True)]
    all_to_all x1, blocking collectives: 17.6 us -> 14.7 us  [swap_all(): return lax.all_to_all(array, AXES, split_axis=0, concat_axis=0, tiled=True)]
    ppermute x2, starting transfers between devices: 4.2 us -> 7.02 us  [extended(): lax.ppermute(head, axis, [((i + 1) % count, i) for i in range(ends)])]
  transfers between devices with their start and end apart: 6 -> 6, of which waited for: 2 -> 2; matrix products, arithmetic and copies ran while one was open for 1% -> 4% of each run, Pallas kernels for 17% -> 25%
where the time goes in v3:
time: 152 us; the launch traced here: 151 us
  Pallas kernels  82 us (54%)
  starting transfers between devices  24.4 us (16%)
  local copies, waits for them, and re-layouts  16.6 us (11%)
  blocking collectives  14.7 us (10%)
  waiting for transfers between devices  7.62 us (5%)
  other arithmetic  4.71 us (3%)
    pallas_call x1, Pallas kernels, fluid(): pl.pallas_call(fluid_kernel, out_shape=jax.ShapeDtypeStruct((2 * W, W), F...  43.4 us
    pallas_call x1, Pallas kernels, contact(): pl.pallas_call(contact_kernel, out_shape=(jax.ShapeDtypeStruct((clumps, W...  17.1 us
    unnamed x41, local copies, waits for them, and re-layouts  15.5 us
    all_to_all x1, blocking collectives, swap_all(): return lax.all_to_all(array, AXES, split_axis=0, concat_axis=0, tiled=True)  14.7 us
    pallas_call x1, Pallas kernels, density(): pl.pallas_call(density_kernel, out_shape=(jax.ShapeDtypeStruct((blocks, W...  11.9 us
    pallas_call x1, Pallas kernels, prep(): pl.pallas_call(prep_kernel, out_shape=(jax.ShapeDtypeStruct((W * ROWS, W)...  8.24 us
    all_to_all x1, starting transfers between devices, swap_all(): return lax.all_to_all(array, AXES, split_axis=0, concat_axis=0, tiled=True)  8.02 us
    ppermute x2, starting transfers between devices, extended(): lax.ppermute(tail, axis, [(i, (i + 1) % count) for i in range(ends)])  7.86 us
  transfers between devices with their start and end apart: 6, of which 2 were waited for; matrix products, arithmetic and copies ran while one was open for 4% of the time, Pallas kernels for 25%

profile of v3, /device:TPU:1, one launch (start us, length us, event | category | flops | bytes accessed | tf_op | source)
XLA Modules:
  0.0 150.9 jit_solution(14810315655069759954)
XLA Ops:
  0.6 0.0 copy-start
  0.6 1.4 broadcast_add_fusion.world_ref
  2.1 0.0 copy-start.4
  2.1 1.5 collective-permute-start.4
  3.6 0.8 fusion.1
  4.4 0.7 pad_maximum_fusion.4
  5.2 3.2 %collective-permute-start = (f32[4,1,8,128]{3,2,0,1:T(8,128)S(1)}, f32[4,1,8,128]{3,2,0,1:T(8,128)S(1)}, u32[]{:S(2)}, u32[]{:S(2)}) collective-permute-start(f32[4,1,8,128]{3,2,0,1:T(8,128)S(1)} %get-tuple-element.28), channel_id=1, source_target_pairs={{0,8},{8,16},{16,24},{24,32},{32,40},{40,48},{48,56},{56,64},{64,7... | collective-permute-start | bytes 49160 | tf_op jit(solution)/shard_map/ppermute | solution.py:475
  8.4 1.3 collective-permute-start.1
  9.7 0.7 copy.29
  10.4 0.0 collective-permute-done
  10.4 2.7 %collective-permute-done.1 = f32[4,1,8,128]{3,2,0,1:T(8,128)S(1)} collective-permute-done((f32[4,1,8,128]{3,2,0,1:T(8,128)S(1)}, f32[4,1,8,128]{3,2,0,1:T(8,128)S(1)}, u32[]{:S(2)}, u32[]{:S(2)}) %collective-permute-start.1) | collective-permute-done | bytes 16416 | tf_op jit(solution)/shard_map/ppermute | solution.py:477
  13.1 0.9 pad_maximum_fusion.1
  14.0 4.7 %collective-permute-start.2 = (f32[4,10,1,128]{3,2,0,1:T(1,128)S(1)}, f32[4,10,1,128]{3,2,0,1:T(1,128)S(1)}, u32[]{:S(2)}, u32[]{:S(2)}) collective-permute-start(f32[4,10,1,128]{3,2,0,1:T(1,128)S(1)} %get-tuple-element.26), channel_id=1, source_target_pairs={{0,1},{1,2},{2,3},{3,4},{4,5},{5,6},{6,7},{8,9},{9,10},{10,11},{11... | collective-permute-start | bytes 61448 | tf_op jit(solution)/shard_map/ppermute | solution.py:475
  18.7 5.7 %collective-permute-start.3 = (f32[4,10,1,128]{3,2,0,1:T(1,128)S(1)}, f32[4,10,1,128]{3,2,0,1:T(1,128)S(1)}, u32[]{:S(2)}, u32[]{:S(2)}) collective-permute-start(f32[4,10,1,128]{3,2,0,1:T(1,128)S(1)} %get-tuple-element.27), channel_id=1, source_target_pairs={{1,0},{2,1},{3,2},{4,3},{5,4},{6,5},{7,6},{9,8},{10,9},{11,10},{12... | collective-permute-start | bytes 61448 | tf_op jit(solution)/shard_map/ppermute | solution.py:477
  24.5 0.7 copy.30
  25.1 0.7 copy.31
  25.9 1.1 copy-done.1
  27.0 8.2 %prep.1 = (f32[6272,128]{1,0:T(8,128)S(1)}, s32[1,1024]{1,0:T(1,128)S(1)}) custom-call(s32[1,1024]{1,0:T(1,128)S(1)} %bitcast.48, s32[1,1024]{1,0:T(1,128)S(1)} %bitcast.52, s32[1,1024]{1,0:T(1,128)S(1)} %bitcast.49, f32[3,1024]{1,0:T(4,128)S(1)} %bitcast.45, f32[3,512,128]{2,1,0:T(8,128)S(1)} %bitcast.40), custom_call_target="tpu_custom_call" | custom-call | tf_op jit(solution)/shard_map/prep/pallas_call | solution.py:134
  35.2 0.0 copy-done.4
  35.3 0.0 copy-start.3
  35.3 1.6 %copy-done.3 = f32[6272,128]{1,0:T(8,128)} copy-done((f32[6272,128]{1,0:T(8,128)}, f32[6272,128]{1,0:T(8,128)S(1)}, u32[]{:S(2)}) %copy-start.3) | copy-done | bytes 3211288
  36.9 0.0 collective-permute-done.2
  36.9 0.0 collective-permute-done.3
  36.9 0.8 pad_maximum_fusion
  37.7 0.0 collective-permute-done.4.next_ref
  37.7 0.9 copy-done.8
  38.6 8.0 %all-to-all-start = ((f32[128,1,6272]{2,1,0:T(1,128)}), f32[128,1,6272]{2,1,0:T(1,128)S(1)}, u32[]{:S(2)}, u32[]{:S(2)}) async-start(f32[128,1,6272]{2,1,0:T(1,128)} %bitcast.42), calls=%async_computation | async-start | bytes 6422528 | tf_op jit(solution)/shard_map/all_to_all | solution.py:485
  46.7 0.0 copy-done.18
  46.7 0.0 copy-done
  46.7 1.1 copy.23
  47.8 0.0 copy-done.14
  47.8 11.9 %density.1 = (f32[64,128]{1,0:T(8,128)}, bf16[64,128,32]{2,1,0:T(8,128)(2,1)S(1)}, bf16[64,16,256]{2,1,0:T(8,128)(2,1)S(1)}) custom-call(f32[4,104,128]{2,1,0:T(8,128)S(1)} %pad.4.ext_ref, f32[4,64,128]{2,1,0:T(8,128)S(1)} %pad_maximum_fusion.2.own_ref, f32[64,128]{1,0:T(8,128)S(1)} %bitcast.47, f32[3,64,128]{2,1,0:T(8,128)S(1)} %copy_bitcast_fusion.vel_ref), custom_call_target="tpu_custom_call" | custom-call | tf_op jit(solution)/shard_map/density/pallas_call | solution.py:228
  59.8 1.3 copy-done.6
  61.1 0.8 copy-done.10
  61.9 0.0 copy-done.17
  61.9 1.1 copy-done.2
  63.0 1.1 copy-done.5
  64.2 1.1 copy-done.9
  65.3 0.8 copy-done.15
  66.0 17.1 %contact.1 = (f32[512,128]{1,0:T(8,128)S(1)}, f32[8,128]{1,0:T(8,128)S(1)}) custom-call(s32[1,512]{1,0:T(1,128)S(1)} %bitcast.54, f32[3,512,128]{2,1,0:T(8,128)S(1)} %bitcast.41, f32[3,512,128]{2,1,0:T(8,128)S(1)} %copy-done.5, f32[3,512,128]{2,1,0:T(8,128)S(1)} %copy-done.9, f32[64,128]{1,0:T(8,128)S(1)} %copy-done.15), custom_call_target="tpu_custom_call" | custom-call | tf_op jit(solution)/shard_map/contact/pallas_call | solution.py:319
  83.2 0.7 copy-done.12
  83.9 4.9 %all-to-all-done = f32[128,1,6272]{2,1,0:T(1,128)S(1)} async-done(((f32[128,1,6272]{2,1,0:T(1,128)}), f32[128,1,6272]{2,1,0:T(1,128)S(1)}, u32[]{:S(2)}, u32[]{:S(2)}) %all-to-all-start) | async-done | bytes 3211296 | tf_op jit(solution)/shard_map/all_to_all | solution.py:485
  88.8 1.6 %copy-done.7 = bf16[64,128,32]{2,1,0:T(8,128)(2,1)S(1)} copy-done((bf16[64,128,32]{2,1,0:T(8,128)(2,1)S(1)}, bf16[64,128,32]{2,1,0:T(8,128)(2,1)}, u32[]{:S(2)}) %copy-start.7) | copy-done | bytes 524312
  90.4 1.0 copy-done.11
  91.4 43.4 %fluid.1 = f32[256,128]{1,0:T(8,128)S(1)} custom-call(f32[6272,128]{1,0:T(8,128)S(1)} %bitcast.39, bf16[64,128,32]{2,1,0:T(8,128)(2,1)S(1)} %copy-done.7, bf16[64,16,256]{2,1,0:T(8,128)(2,1)S(1)} %copy-done.11, f32[8,128]{1,0:T(8,128)S(1)} %get-tuple-element.24.after_ref), custom_call_target="tpu_custom_call" | custom-call | tf_op jit(solution)/shard_map/fluid/pallas_call | solution.py:405
  134.9 14.7 %all_to_all.10 = f32[128,1,256]{2,1,0:T(1,128)S(1)} all-to-all(f32[128,1,256]{2,1,0:T(1,128)S(1)} %bitcast.44), channel_id=1, replica_groups=mesh['stream'=16,'span'=8] {'stream','span'}, dimensions={0} | all-to-all | bytes 262144 | tf_op jit(solution)/shard_map/all_to_all | solution.py:485
  149.6 0.0 copy-done.16
  149.6 1.3 combine.1
  (23 shorter events, 0.1 us)
Async XLA Ops:
  0.6 46.1 %copy-start = (f32[8,8,3,128]{3,1,2,0:T(8,128)S(1)}, f32[8,8,3,128]{3,1,2,0:T(8,128)}, u32[]{:S(2)}) copy-start(f32[8,8,3,128]{3,1,2,0:T(8,128)} %param.12) | copy-start | bytes 294916
  2.1 33.1 %copy-start.4 = (f32[3,512,128]{2,1,0:T(8,128)}, f32[3,512,128]{2,1,0:T(8,128)S(1)}, u32[]{:S(2)}) copy-start(f32[3,512,128]{2,1,0:T(8,128)S(1)} %broadcast_add_fusion.world_ref) | copy-start | bytes 2359300
  2.1 35.6 %collective-permute-start.4 = (f32[3,512,128]{2,1,0:T(8,128)S(1)}, f32[3,512,128]{2,1,0:T(8,128)S(1)}, u32[]{:S(2)}, u32[]{:S(2)}) collective-permute-start(f32[3,512,128]{2,1,0:T(8,128)S(1)} %broadcast_add_fusion.world_ref), channel_id=1, source_target_pairs={{0,127},{1,0},{2,1},{3,2},{4,3},{5,4},{6,5},{7,6},{8,7},{9,8},{10,... | collective-permute-start | bytes 2359304 | tf_op jit(solution)/shard_map/ppermute | solution.py:508
  5.2 5.2 %collective-permute-start = (f32[4,1,8,128]{3,2,0,1:T(8,128)S(1)}, f32[4,1,8,128]{3,2,0,1:T(8,128)S(1)}, u32[]{:S(2)}, u32[]{:S(2)}) collective-permute-start(f32[4,1,8,128]{3,2,0,1:T(8,128)S(1)} %get-tuple-element.28), channel_id=1, source_target_pairs={{0,8},{8,16},{16,24},{24,32},{32,40},{40,48},{48,56},{56,64},{64,7... | collective-permute-start | bytes 49160 | tf_op jit(solution)/shard_map/ppermute | solution.py:475
  8.4 4.7 %collective-permute-start.1 = (f32[4,1,8,128]{3,2,0,1:T(8,128)S(1)}, f32[4,1,8,128]{3,2,0,1:T(8,128)S(1)}, u32[]{:S(2)}, u32[]{:S(2)}) collective-permute-start(f32[4,1,8,128]{3,2,0,1:T(8,128)S(1)} %get-tuple-element.29), channel_id=1, source_target_pairs={{8,0},{16,8},{24,16},{32,24},{40,32},{48,40},{56,48},{64,56},{72,6... | collective-permute-start | bytes 49160 | tf_op jit(solution)/shard_map/ppermute | solution.py:477
  14.0 22.9 %collective-permute-start.2 = (f32[4,10,1,128]{3,2,0,1:T(1,128)S(1)}, f32[4,10,1,128]{3,2,0,1:T(1,128)S(1)}, u32[]{:S(2)}, u32[]{:S(2)}) collective-permute-start(f32[4,10,1,128]{3,2,0,1:T(1,128)S(1)} %get-tuple-element.26), channel_id=1, source_target_pairs={{0,1},{1,2},{2,3},{3,4},{4,5},{5,6},{6,7},{8,9},{9,10},{10,11},{11... | collective-permute-start | bytes 61448 | tf_op jit(solution)/shard_map/ppermute | solution.py:475
  18.7 18.2 %collective-permute-start.3 = (f32[4,10,1,128]{3,2,0,1:T(1,128)S(1)}, f32[4,10,1,128]{3,2,0,1:T(1,128)S(1)}, u32[]{:S(2)}, u32[]{:S(2)}) collective-permute-start(f32[4,10,1,128]{3,2,0,1:T(1,128)S(1)} %get-tuple-element.27), channel_id=1, source_target_pairs={{1,0},{2,1},{3,2},{4,3},{5,4},{6,5},{7,6},{9,8},{10,9},{11,10},{12... | collective-permute-start | bytes 61448 | tf_op jit(solution)/shard_map/ppermute | solution.py:477
  25.9 1.1 copy-start.1
  35.3 1.6 %copy-start.3 = (f32[6272,128]{1,0:T(8,128)}, f32[6272,128]{1,0:T(8,128)S(1)}, u32[]{:S(2)}) copy-start(f32[6272,128]{1,0:T(8,128)S(1)} %get-tuple-element.20) | copy-start | bytes 9633796
  37.7 0.9 copy-start.8
  38.6 8.0 %copy-start.18 = (f32[8,8,3,128]{3,1,2,0:T(8,128)S(1)}, f32[8,8,3,128]{3,1,2,0:T(8,128)}, u32[]{:S(2)}) copy-start(f32[8,8,3,128]{3,1,2,0:T(8,128)} %param.11) | copy-start | bytes 294916
  38.6 9.2 %copy-start.14 = (f32[8,8,128]{2,1,0:T(8,128)S(1)}, f32[8,8,128]{2,1,0:T(8,128)}, u32[]{:S(2)}) copy-start(f32[8,8,128]{2,1,0:T(8,128)} %param.13) | copy-start | bytes 98308
  38.6 23.3 %copy-start.17 = (s32[512]{0:T(512)S(1)}, s32[512]{0:T(512)}, u32[]{:S(2)}) copy-start(s32[512]{0:T(512)} %param.21) | copy-start | bytes 6148
  38.6 50.2 %all-to-all-start = ((f32[128,1,6272]{2,1,0:T(1,128)}), f32[128,1,6272]{2,1,0:T(1,128)S(1)}, u32[]{:S(2)}, u32[]{:S(2)}) async-start(f32[128,1,6272]{2,1,0:T(1,128)} %bitcast.42), calls=%async_computation | async-start | bytes 6422528 | tf_op jit(solution)/shard_map/all_to_all | solution.py:485
  59.8 1.4 copy-start.6
  61.1 0.8 copy-start.10
  61.9 1.1 copy-start.2
  63.0 1.1 copy-start.5
  64.2 1.1 copy-start.9
  65.3 0.8 copy-start.15
  66.0 83.5 %copy-start.16 = (f32[512,3]{0,1:T(4,128)S(1)}, f32[512,3]{0,1:T(4,128)}, u32[]{:S(2)}) copy-start(f32[512,3]{0,1:T(4,128)} %param.16) | copy-start | bytes 18436
  83.2 0.7 copy-start.12
  88.8 1.6 %copy-start.7 = (bf16[64,128,32]{2,1,0:T(8,128)(2,1)S(1)}, bf16[64,128,32]{2,1,0:T(8,128)(2,1)}, u32[]{:S(2)}) copy-start(bf16[64,128,32]{2,1,0:T(8,128)(2,1)} %copy-done.6) | copy-start | bytes 1572868
  90.4 1.0 copy-start.11
  91.4 58.1 %copy-start.13 = (f32[512,128]{1,0:T(8,128)S(1)}, f32[512,128]{1,0:T(8,128)}, u32[]{:S(2)}) copy-start(f32[512,128]{1,0:T(8,128)} %copy-done.12) | copy-start | bytes 786436

commit v4 on v1

--- a/solution.py
+++ b/solution.py
@@ -21,6 +21,7 @@
 FEATS = 32
 ROWS = 49
 UNROLL = 4
+GROUPS = 16
 DEAD = -30000.0
 BF = jnp.bfloat16
 F32 = jnp.float32
@@ -129,7 +130,7 @@
     entries = dev.shape[1]
     vm = pl.BlockSpec(memory_space=pltpu.VMEM)
     sm = pl.BlockSpec(memory_space=pltpu.SMEM)
-    hbm = pl.BlockSpec(memory_space=pl.ANY)
+    hbm = pl.BlockSpec(memory_space=pltpu.HBM)
     return pl.pallas_call(
         prep_kernel,
         out_shape=(
@@ -143,12 +144,12 @@
             pltpu.SMEM((1, entries), jnp.int32),
             pltpu.SemaphoreType.DMA((1,)),
         ],
-        compiler_params=pltpu.CompilerParams(vmem_limit_bytes=24 << 20),
+        compiler_params=pltpu.CompilerParams(vmem_limit_bytes=40 << 20),
         name="prep",
     )(dev, blk, dev, off, arms)
 
 
-def density_kernel(ext_ref, own_ref, mass_ref, vel_ref, dens_ref, table_ref, amp_ref,
+def density_kernel(ext_ref, own_ref, mass_ref, vel_ref, after_ref, dens_ref, table_ref, amp_ref,
                    feat, right, sums, left, wide):
     rows_y = 8
     zero_tail(feat)
@@ -221,7 +222,7 @@
     lax.fori_loop(0, 8, own_row, 0)
 
 
-def density(ext, own, mass, vel):
+def density(ext, own, mass, vel, after):
     blocks = mass.shape[0]
     vm = pl.BlockSpec(memory_space=pltpu.VMEM)
     return pl.pallas_call(
@@ -231,7 +232,7 @@
             jax.ShapeDtypeStruct((blocks, W, FEATS), BF),
             jax.ShapeDtypeStruct((blocks, 16, 2 * W), BF),
         ),
-        in_specs=[vm] * 4,
+        in_specs=[vm] * 5,
         out_specs=(vm, vm, vm),
         scratch_shapes=[
             pltpu.VMEM((FEATS * 8, W), F32),
@@ -240,9 +241,9 @@
             pltpu.VMEM((ext.shape[1], W, FEATS), BF),
             pltpu.VMEM((W, W), F32),
         ],
-        compiler_params=pltpu.CompilerParams(vmem_limit_bytes=24 << 20),
+        compiler_params=pltpu.CompilerParams(vmem_limit_bytes=14 << 20),
         name="density",
-    )(ext, own, mass, vel)
+    )(ext, own, mass, vel, after)
 
 
 def columns_to_lanes(cols):
@@ -253,8 +254,9 @@
     return out
 
 
-def contact_kernel(partner_s, arm_ref, world_ref, next_ref, out_ref, cand, gat, feat, right, lead, acc):
+def contact_kernel(partner_s, arm_ref, world_ref, next_ref, out_ref, done_ref, cand, gat, feat, right, lead, acc):
     clumps = arm_ref.shape[1]
+    done_ref[...] = jnp.zeros_like(done_ref)
     cand[:, 0:clumps, :] = world_ref[...]
     cand[:, clumps : 2 * clumps, :] = next_ref[...]
     zero = jnp.zeros((8, W), F32)
@@ -316,9 +318,9 @@
     sm = pl.BlockSpec(memory_space=pltpu.SMEM)
     return pl.pallas_call(
         contact_kernel,
-        out_shape=jax.ShapeDtypeStruct((clumps, W), F32),
+        out_shape=(jax.ShapeDtypeStruct((clumps, W), F32), jax.ShapeDtypeStruct((8, W), F32)),
         in_specs=[sm, vm, vm, vm],
-        out_specs=vm,
+        out_specs=(vm, vm),
         scratch_shapes=[
             pltpu.VMEM((3, 2 * clumps, W), F32),
             pltpu.VMEM((UNROLL * 24, W), F32),
@@ -327,13 +329,13 @@
             pltpu.VMEM((UNROLL * W, W), F32),
             pltpu.VMEM((UNROLL * 64, W), F32),
         ],
-        compiler_params=pltpu.CompilerParams(vmem_limit_bytes=24 << 20),
+        compiler_params=pltpu.CompilerParams(vmem_limit_bytes=10 << 20),
         name="contact",
     )(partner, arms, world, following)
 
 
 def fluid_kernel(y_ref, table_ref, amp_ref, out_ref, names, names_s, right, acc, sems):
-    for t in range(2 * UNROLL):
+    for t in range(GROUPS):
         zero_tail(right, t * FEATS * 8)
     lane = lax.broadcasted_iota(jnp.int32, (8, W), 1)
     mine = (lane >> 4) == lax.broadcasted_iota(jnp.int32, (8, W), 0)
@@ -351,16 +353,16 @@
 
     def group(i, carry):
         ys, valids = [], []
-        for t in range(2 * UNROLL):
-            g = i * UNROLL + t // 2
+        for t in range(GROUPS):
+            g = i * (GROUPS // 2) + t // 2
             at = g * ROWS + (t % 2) * 8
             y = [y_ref[pl.ds(at + 16 * q, 8), :] for q in range(3)]
             ys.append(y)
             u = [v - 0.5 for v in y]
             scaled = [split3(v * (2.0 * C_FLUID)) for v in u]
             put_rows(right, right_rows(*scaled, norm_of(*u, C_FLUID)), t * FEATS * 8)
-        for t in range(2 * UNROLL):
-            g = i * UNROLL + t // 2
+        for t in range(GROUPS):
+            g = i * (GROUPS // 2) + t // 2
             valid = jnp.zeros((1, W), jnp.int32)
             for j in range(8):
                 name = names_s[g, (t % 2) * 8 + j]
@@ -371,8 +373,8 @@
                 spot = 64 * t + 8 * j
                 acc[spot : spot + 8, :] = res[0:8] + res[8:16]
             valids.append(valid)
-        for t in range(2 * UNROLL):
-            g = i * UNROLL + t // 2
+        for t in range(GROUPS):
+            g = i * (GROUPS // 2) + t // 2
             y = ys[t]
             s = [acc[pl.ds(64 * t + q, 8, stride=8), :] for q in range(4)]
             cross = [y[1] * s[2] - y[2] * s[1], y[2] * s[0] - y[0] * s[2],
@@ -385,7 +387,7 @@
             out_ref[pl.ds(2 * g + t % 2, 1), :] = jnp.where(valids[t] >= 0, row, 0.0)
         return carry
 
-    lax.fori_loop(0, devices // UNROLL, group, 0)
+    lax.fori_loop(0, devices // (GROUPS // 2), group, 0)
 
 
 def fluid(spots, table, amp):
@@ -393,16 +395,16 @@
     return pl.pallas_call(
         fluid_kernel,
         out_shape=jax.ShapeDtypeStruct((2 * W, W), F32),
-        in_specs=[vm, vm, vm],
+        in_specs=[vm] * 3,
         out_specs=vm,
         scratch_shapes=[
             pltpu.VMEM((W, W), jnp.int32),
             pltpu.SMEM((W, W), jnp.int32),
-            pltpu.VMEM((2 * UNROLL * FEATS * 8, W), F32),
-            pltpu.VMEM((2 * UNROLL * 64, W), F32),
+            pltpu.VMEM((GROUPS * FEATS * 8, W), F32),
+            pltpu.VMEM((GROUPS * 64, W), F32),
             pltpu.SemaphoreType.DMA((1,)),
         ],
-        compiler_params=pltpu.CompilerParams(vmem_limit_bytes=24 << 20),
+        compiler_params=pltpu.CompilerParams(vmem_limit_bytes=14 << 20),
         name="fluid",
     )(spots, table, amp)
 
@@ -445,7 +447,7 @@
         out_shape=jax.ShapeDtypeStruct((6, vel.shape[1]), F32),
         in_specs=[vm] * 6,
         out_specs=vm,
-        compiler_params=pltpu.CompilerParams(vmem_limit_bytes=24 << 20),
+        compiler_params=pltpu.CompilerParams(vmem_limit_bytes=14 << 20),
         name="combine",
     )(dev, rank, off, vel, got, touch)
 
@@ -465,6 +467,22 @@
             axis=dim,
         )
     return cells
+
+
+def gate_kernel(array_ref, after_ref, out_ref):
+    del array_ref, after_ref, out_ref
+
+
+def gated(array, after):
+    hbm = pl.BlockSpec(memory_space=pltpu.HBM)
+    return pl.pallas_call(
+        gate_kernel,
+        out_shape=jax.ShapeDtypeStruct(array.shape, array.dtype),
+        in_specs=[hbm, pl.BlockSpec(memory_space=pl.ANY)],
+        out_specs=hbm,
+        input_output_aliases={0: 0},
+        name="gate",
+    )(array, after)
 
 
 def swap_all(array):
@@ -495,20 +513,22 @@
     off = jnp.transpose(margin_offset, (2, 1, 0)).reshape(3, entries)
     vel = clump_vel.T
     send, rank = prep(dev, blk, off, arms)
-    got = swap_all(send.reshape(devices, 1, ROWS * width))
-    world = arms + clump_center.T[:, :, None]
+    ready = rank[0, 0] >= 0
+    world = jnp.where(ready, arms + clump_center.T[:, :, None], 0.0)
     following = lax.ppermute(world, AXES, [(i, (i + devices - 1) % devices) for i in range(devices)])
-    touch = contact(contact_partner.reshape(1, clumps), arms, world, following)
     lanes = jnp.arange(width, dtype=jnp.int32)
     live = jnp.where(lanes[None, None, :] < fluid_count[..., None], fluid_mass, 0.0)
     planes = jnp.concatenate([jnp.moveaxis(fluid_pos, 2, 0), live[None]], axis=0)
+    planes = jnp.where(ready, planes, 0.0)
     ext = extended(planes, (("stream", 1), ("span", 2)))
     ext = ext.reshape(4, (rows_x + 2) * (rows_y + 2), width)
+    send = gated(send, ext[0, 0:8] + following[0, 0:8])
+    got = swap_all(send.reshape(devices, 1, ROWS * width))
+    touch, done = contact(contact_partner.reshape(1, clumps), arms, world, following)
     ext = jnp.pad(ext, ((0, 0), (0, 4), (0, 0)))
     own = planes.reshape(4, blocks, width)
     speed = jnp.moveaxis(fluid_vel, 2, 0).reshape(3, blocks, width)
-    dens, table, amp = density(ext, own, fluid_mass.reshape(blocks, width), speed)
-    got, touch = lax.optimization_barrier((got, touch))
+    dens, table, amp = density(ext, own, fluid_mass.reshape(blocks, width), speed, done)
     sums = fluid(got.reshape(devices * ROWS, width), table, amp)
     back = swap_all(sums.reshape(devices, 1, 2 * width)).reshape(2 * devices, width)
     loads = combine(dev, rank, off, vel, back, touch)

time: 175 us -> 156 us (0.89)
  waiting for transfers between devices: 31.5 us -> 9.29 us
  local copies, waits for them, and re-layouts: 10.6 us -> 17.1 us
  Pallas kernels: 87.8 us -> 81.9 us
  other arithmetic: 1.59 us -> 4.77 us
  blocking collectives: 17.6 us -> 14.5 us
    ppermute x2, waiting for transfers between devices: 31.4 us -> 4.22 us  [extended(): lax.ppermute(head, axis, [((i + 1) % count, i) for i in range(ends)])]
    pallas_call x1, Pallas kernels: 49.2 us -> 43.3 us  [fluid(): pl.pallas_call(fluid_kernel, out_shape=jax.ShapeDtypeStruct((2 * W, W), F...]
    unnamed x35 -> x37, local copies, waits for them, and re-layouts: 10.5 us -> 15.6 us
    all_to_all x1, waiting for transfers between devices: 0.01 us -> 5.06 us  [swap_all(): return lax.all_to_all(array, AXES, split_axis=0, concat_axis=0, tiled=True)]
    all_to_all x1, blocking collectives: 17.6 us -> 14.5 us  [swap_all(): return lax.all_to_all(array, AXES, split_axis=0, concat_axis=0, tiled=True)]
    ppermute x2, starting transfers between devices: 4.2 us -> 7.06 us  [extended(): lax.ppermute(head, axis, [((i + 1) % count, i) for i in range(ends)])]
    select_n x0 -> x3, other arithmetic: none -> 2.64 us  [the longest x2 1.67 us: body(): planes = jnp.where(ready, planes, 0.0)]
    all_to_all x1, starting transfers between devices: 11.5 us -> 9.71 us  [swap_all(): return lax.all_to_all(array, AXES, split_axis=0, concat_axis=0, tiled=True)]
  transfers between devices with their start and end apart: 6 -> 6, of which waited for: 2 -> 3; matrix products, arithmetic and copies ran while one was open for 1% -> 3% of each run, Pallas kernels for 17% -> 19%
where the time goes in v4:
time: 156 us; the launch traced here: 155 us
  Pallas kernels  81.9 us (53%)
  starting transfers between devices  26.1 us (17%)
  local copies, waits for them, and re-layouts  17.1 us (11%)
  blocking collectives  14.5 us (9%)
  waiting for transfers between devices  9.29 us (6%)
  other arithmetic  4.77 us (3%)
    pallas_call x1, Pallas kernels, fluid(): pl.pallas_call(fluid_kernel, out_shape=jax.ShapeDtypeStruct((2 * W, W), F...  43.3 us
    pallas_call x1, Pallas kernels, contact(): pl.pallas_call(contact_kernel, out_shape=(jax.ShapeDtypeStruct((clumps, W...  17.1 us
    unnamed x37, local copies, waits for them, and re-layouts  15.6 us
    all_to_all x1, blocking collectives, swap_all(): return lax.all_to_all(array, AXES, split_axis=0, concat_axis=0, tiled=True)  14.5 us
    pallas_call x1, Pallas kernels, density(): pl.pallas_call(density_kernel, out_shape=(jax.ShapeDtypeStruct((blocks, W...  11.9 us
    all_to_all x1, starting transfers between devices, swap_all(): return lax.all_to_all(array, AXES, split_axis=0, concat_axis=0, tiled=True)  9.71 us
    pallas_call x1, Pallas kernels, prep(): pl.pallas_call(prep_kernel, out_shape=(jax.ShapeDtypeStruct((W * ROWS, W)...  8.24 us
    ppermute x2, starting transfers between devices, extended(): lax.ppermute(tail, axis, [(i, (i + 1) % count) for i in range(ends)])  7.83 us
  transfers between devices with their start and end apart: 6, of which 3 were waited for; matrix products, arithmetic and copies ran while one was open for 3% of the time, Pallas kernels for 19%

profile of v4, /device:TPU:1, one launch (start us, length us, event | category | flops | bytes accessed | tf_op | source)
XLA Modules:
  0.0 155.1 jit_solution(1448364397829055252)
XLA Ops:
  0.6 0.0 copy-start
  0.6 0.7 copy.32
  1.4 0.7 copy.33
  2.1 0.7 copy.34
  2.8 1.1 copy-done.2
  3.9 8.2 %prep.1 = (f32[6272,128]{1,0:T(8,128)S(1)}, s32[1,1024]{1,0:T(1,128)S(1)}) custom-call(s32[1,1024]{1,0:T(1,128)S(1)} %bitcast.51, s32[1,1024]{1,0:T(1,128)S(1)} %bitcast.54, s32[1,1024]{1,0:T(1,128)S(1)} %bitcast.52, f32[3,1024]{1,0:T(4,128)S(1)} %bitcast.48, f32[3,512,128]{2,1,0:T(8,128)S(1)} %bitcast.44), custom_call_target="tpu_custom_call" | custom-call | tf_op jit(solution)/shard_map/prep/pallas_call | solution.py:134
  12.2 0.0 copy-start.1
  12.2 1.6 %copy-done.1 = f32[6272,128]{1,0:T(8,128)} copy-done((f32[6272,128]{1,0:T(8,128)}, f32[6272,128]{1,0:T(8,128)S(1)}, u32[]{:S(2)}) %copy-start.1) | copy-done | bytes 3211288
  13.8 0.5 slice.21
  15.0 1.0 add_select_fusion.world_ref
  15.9 1.5 collective-permute-start.4
  17.4 0.9 copy-done.4
  18.3 1.4 fusion.1
  19.8 0.9 maximum_select_fusion
  20.7 3.2 %collective-permute-start = (f32[4,1,8,128]{3,2,0,1:T(8,128)S(1)}, f32[4,1,8,128]{3,2,0,1:T(8,128)S(1)}, u32[]{:S(2)}, u32[]{:S(2)}) collective-permute-start(f32[4,1,8,128]{3,2,0,1:T(8,128)S(1)} %get-tuple-element.18), channel_id=1, source_target_pairs={{0,8},{8,16},{16,24},{24,32},{32,40},{40,48},{48,56},{56,64},{64,7... | collective-permute-start | bytes 49160 | tf_op jit(solution)/shard_map/ppermute | solution.py:463
  23.9 1.3 collective-permute-start.1
  25.2 0.0 collective-permute-done
  25.2 3.4 %collective-permute-done.1 = f32[4,1,8,128]{3,2,0,1:T(8,128)S(1)} collective-permute-done((f32[4,1,8,128]{3,2,0,1:T(8,128)S(1)}, f32[4,1,8,128]{3,2,0,1:T(8,128)S(1)}, u32[]{:S(2)}, u32[]{:S(2)}) %collective-permute-start.1) | collective-permute-done | bytes 16416 | tf_op jit(solution)/shard_map/ppermute | solution.py:465
  28.7 4.6 %collective-permute-start.2 = (f32[4,10,1,128]{3,2,0,1:T(1,128)S(1)}, f32[4,10,1,128]{3,2,0,1:T(1,128)S(1)}, u32[]{:S(2)}, u32[]{:S(2)}) collective-permute-start(f32[4,10,1,128]{3,2,0,1:T(1,128)S(1)} %get-tuple-element.16), channel_id=1, source_target_pairs={{0,1},{1,2},{2,3},{3,4},{4,5},{5,6},{6,7},{8,9},{9,10},{10,11},{11... | collective-permute-start | bytes 61448 | tf_op jit(solution)/shard_map/ppermute | solution.py:463
  33.3 5.8 %collective-permute-start.3 = (f32[4,10,1,128]{3,2,0,1:T(1,128)S(1)}, f32[4,10,1,128]{3,2,0,1:T(1,128)S(1)}, u32[]{:S(2)}, u32[]{:S(2)}) collective-permute-start(f32[4,10,1,128]{3,2,0,1:T(1,128)S(1)} %get-tuple-element.17), channel_id=1, source_target_pairs={{1,0},{2,1},{3,2},{4,3},{5,4},{6,5},{7,6},{9,8},{10,9},{11,10},{12... | collective-permute-start | bytes 61448 | tf_op jit(solution)/shard_map/ppermute | solution.py:465
  39.1 0.0 collective-permute-done.2
  39.1 0.8 collective-permute-done.3
  39.9 0.1 pad_maximum_fusion
  40.0 0.1 copy.25
  40.1 0.0 collective-permute-done.4.next_ref
  40.1 0.6 fusion.3.after_ref
  40.7 0.9 copy-done.8
  41.6 9.7 %all-to-all-start = ((f32[128,1,6272]{2,1,0:T(1,128)}), f32[128,1,6272]{2,1,0:T(1,128)S(1)}, u32[]{:S(2)}, u32[]{:S(2)}) async-start(f32[128,1,6272]{2,1,0:T(1,128)} %bitcast.42), calls=%async_computation | async-start | bytes 6422528 | tf_op jit(solution)/shard_map/all_to_all | solution.py:489
  51.3 0.0 copy-start.14
  51.3 0.9 copy_bitcast_fusion.1
  52.2 0.8 maximum_select_fusion.1.own_ref
  53.0 0.0 copy-done.16
  53.0 0.0 copy-start.3
  53.0 1.1 copy-done.3
  54.2 1.1 copy-done.5
  55.3 1.1 copy-done.9
  56.4 17.1 %contact.1 = (f32[512,128]{1,0:T(8,128)S(1)}, f32[8,128]{1,0:T(8,128)S(1)}) custom-call(s32[1,512]{1,0:T(1,128)S(1)} %bitcast.56, f32[3,512,128]{2,1,0:T(8,128)S(1)} %bitcast.45, f32[3,512,128]{2,1,0:T(8,128)S(1)} %copy-done.5, f32[3,512,128]{2,1,0:T(8,128)S(1)} %copy-done.9), custom_call_target="tpu_custom_call" | custom-call | tf_op jit(solution)/shard_map/contact/pallas_call | solution.py:319
  73.6 0.7 copy-done.12
  74.3 0.0 copy-done.14
  74.3 11.9 %density.1 = (f32[64,128]{1,0:T(8,128)}, bf16[64,128,32]{2,1,0:T(8,128)(2,1)S(1)}, bf16[64,16,256]{2,1,0:T(8,128)(2,1)S(1)}) custom-call(f32[4,104,128]{2,1,0:T(8,128)S(1)} %pad.4.ext_ref, f32[4,64,128]{2,1,0:T(8,128)S(1)} %maximum_select_fusion.1.own_ref, f32[64,128]{1,0:T(8,128)S(1)} %bitcast.50, f32[3,64,128]{2,1,0:T(8,128)S(1)} %copy_bitcast_fusion.vel_ref, ...), custom_call_target="tpu_custom_call" | custom-call | tf_op jit(solution)/shard_map/density/pallas_call | solution.py:228
  86.2 1.3 copy-done.6
  87.6 0.8 copy-done.10
  88.4 5.1 %all-to-all-done = f32[128,1,6272]{2,1,0:T(1,128)S(1)} async-done(((f32[128,1,6272]{2,1,0:T(1,128)}), f32[128,1,6272]{2,1,0:T(1,128)S(1)}, u32[]{:S(2)}, u32[]{:S(2)}) %all-to-all-start) | async-done | bytes 3211296 | tf_op jit(solution)/shard_map/all_to_all | solution.py:489
  93.4 1.6 %copy-done.7 = bf16[64,128,32]{2,1,0:T(8,128)(2,1)S(1)} copy-done((bf16[64,128,32]{2,1,0:T(8,128)(2,1)S(1)}, bf16[64,128,32]{2,1,0:T(8,128)(2,1)}, u32[]{:S(2)}) %copy-start.7) | copy-done | bytes 524312
  95.0 1.0 copy-done.11
  96.1 43.3 %fluid.1 = f32[256,128]{1,0:T(8,128)S(1)} custom-call(f32[6272,128]{1,0:T(8,128)S(1)} %bitcast.43, bf16[64,128,32]{2,1,0:T(8,128)(2,1)S(1)} %copy-done.7, bf16[64,16,256]{2,1,0:T(8,128)(2,1)S(1)} %copy-done.11), custom_call_target="tpu_custom_call" | custom-call | tf_op jit(solution)/shard_map/fluid/pallas_call | solution.py:395
  139.4 14.5 %all_to_all.10 = f32[128,1,256]{2,1,0:T(1,128)S(1)} all-to-all(f32[128,1,256]{2,1,0:T(1,128)S(1)} %bitcast.47), channel_id=1, replica_groups=mesh['stream'=16,'span'=8] {'stream','span'}, dimensions={0} | all-to-all | bytes 262144 | tf_op jit(solution)/shard_map/all_to_all | solution.py:489
  153.8 1.3 combine.1
  (22 shorter events, 0.1 us)
Async XLA Ops:
  0.6 52.3 %copy-start = (f32[8,8,3,128]{3,1,2,0:T(8,128)S(1)}, f32[8,8,3,128]{3,1,2,0:T(8,128)}, u32[]{:S(2)}) copy-start(f32[8,8,3,128]{3,1,2,0:T(8,128)} %param.12) | copy-start | bytes 294916
  2.8 1.1 copy-start.2
  12.2 1.6 %copy-start.1 = (f32[6272,128]{1,0:T(8,128)}, f32[6272,128]{1,0:T(8,128)S(1)}, u32[]{:S(2)}) copy-start(f32[6272,128]{1,0:T(8,128)S(1)} %get-tuple-element.12.array_ref) | copy-start | bytes 9633796
  15.9 24.1 %collective-permute-start.4 = (f32[3,512,128]{2,1,0:T(8,128)S(1)}, f32[3,512,128]{2,1,0:T(8,128)S(1)}, u32[]{:S(2)}, u32[]{:S(2)}) collective-permute-start(f32[3,512,128]{2,1,0:T(8,128)S(1)} %add_select_fusion.world_ref), channel_id=1, source_target_pairs={{0,127},{1,0},{2,1},{3,2},{4,3},{5,4},{6,5},{7,6},{8,7},{9,8},{10,... | collective-permute-start | bytes 2359304 | tf_op jit(solution)/shard_map/ppermute | solution.py:518
  17.4 0.9 copy-start.4
  20.7 4.5 %collective-permute-start = (f32[4,1,8,128]{3,2,0,1:T(8,128)S(1)}, f32[4,1,8,128]{3,2,0,1:T(8,128)S(1)}, u32[]{:S(2)}, u32[]{:S(2)}) collective-permute-start(f32[4,1,8,128]{3,2,0,1:T(8,128)S(1)} %get-tuple-element.18), channel_id=1, source_target_pairs={{0,8},{8,16},{16,24},{24,32},{32,40},{40,48},{48,56},{56,64},{64,7... | collective-permute-start | bytes 49160 | tf_op jit(solution)/shard_map/ppermute | solution.py:463
  23.9 4.7 %collective-permute-start.1 = (f32[4,1,8,128]{3,2,0,1:T(8,128)S(1)}, f32[4,1,8,128]{3,2,0,1:T(8,128)S(1)}, u32[]{:S(2)}, u32[]{:S(2)}) collective-permute-start(f32[4,1,8,128]{3,2,0,1:T(8,128)S(1)} %get-tuple-element.19), channel_id=1, source_target_pairs={{8,0},{16,8},{24,16},{32,24},{40,32},{48,40},{56,48},{64,56},{72,6... | collective-permute-start | bytes 49160 | tf_op jit(solution)/shard_map/ppermute | solution.py:465
  28.7 10.4 %collective-permute-start.2 = (f32[4,10,1,128]{3,2,0,1:T(1,128)S(1)}, f32[4,10,1,128]{3,2,0,1:T(1,128)S(1)}, u32[]{:S(2)}, u32[]{:S(2)}) collective-permute-start(f32[4,10,1,128]{3,2,0,1:T(1,128)S(1)} %get-tuple-element.16), channel_id=1, source_target_pairs={{0,1},{1,2},{2,3},{3,4},{4,5},{5,6},{6,7},{8,9},{9,10},{10,11},{11... | collective-permute-start | bytes 61448 | tf_op jit(solution)/shard_map/ppermute | solution.py:463
  33.3 6.6 %collective-permute-start.3 = (f32[4,10,1,128]{3,2,0,1:T(1,128)S(1)}, f32[4,10,1,128]{3,2,0,1:T(1,128)S(1)}, u32[]{:S(2)}, u32[]{:S(2)}) collective-permute-start(f32[4,10,1,128]{3,2,0,1:T(1,128)S(1)} %get-tuple-element.17), channel_id=1, source_target_pairs={{1,0},{2,1},{3,2},{4,3},{5,4},{6,5},{7,6},{9,8},{10,9},{11,10},{12... | collective-permute-start | bytes 61448 | tf_op jit(solution)/shard_map/ppermute | solution.py:465
  40.7 0.9 copy-start.8
  41.6 11.5 %copy-start.16 = (s32[512]{0:T(512)S(1)}, s32[512]{0:T(512)}, u32[]{:S(2)}) copy-start(s32[512]{0:T(512)} %param.21) | copy-start | bytes 6148
  41.6 51.8 %all-to-all-start = ((f32[128,1,6272]{2,1,0:T(1,128)}), f32[128,1,6272]{2,1,0:T(1,128)S(1)}, u32[]{:S(2)}, u32[]{:S(2)}) async-start(f32[128,1,6272]{2,1,0:T(1,128)} %bitcast.42), calls=%async_computation | async-start | bytes 6422528 | tf_op jit(solution)/shard_map/all_to_all | solution.py:489
  51.3 23.0 %copy-start.14 = (f32[8,8,128]{2,1,0:T(8,128)S(1)}, f32[8,8,128]{2,1,0:T(8,128)}, u32[]{:S(2)}) copy-start(f32[8,8,128]{2,1,0:T(8,128)} %param.13) | copy-start | bytes 98308
  53.0 1.1 copy-start.3
  54.2 1.1 copy-start.5
  55.3 1.1 copy-start.9
  73.6 0.7 copy-start.12
  74.3 79.5 %copy-start.15 = (f32[512,3]{0,1:T(4,128)S(1)}, f32[512,3]{0,1:T(4,128)}, u32[]{:S(2)}) copy-start(f32[512,3]{0,1:T(4,128)} %param.16) | copy-start | bytes 18436
  86.2 1.3 copy-start.6
  87.6 0.8 copy-start.10
  93.4 1.6 %copy-start.7 = (bf16[64,128,32]{2,1,0:T(8,128)(2,1)S(1)}, bf16[64,128,32]{2,1,0:T(8,128)(2,1)}, u32[]{:S(2)}) copy-start(bf16[64,128,32]{2,1,0:T(8,128)(2,1)} %copy-done.6) | copy-start | bytes 1572868
  95.0 1.0 copy-start.11
  96.1 57.8 %copy-start.13 = (f32[512,128]{1,0:T(8,128)S(1)}, f32[512,128]{1,0:T(8,128)}, u32[]{:S(2)}) copy-start(f32[512,128]{1,0:T(8,128)} %copy-done.12) | copy-start | bytes 786436

commit v5 on v4

--- a/solution.py
+++ b/solution.py
@@ -21,7 +21,7 @@
 FEATS = 32
 ROWS = 49
 UNROLL = 4
-GROUPS = 16
+GROUPS = 32
 DEAD = -30000.0
 BF = jnp.bfloat16
 F32 = jnp.float32
@@ -149,7 +149,7 @@
     )(dev, blk, dev, off, arms)
 
 
-def density_kernel(ext_ref, own_ref, mass_ref, vel_ref, after_ref, dens_ref, table_ref, amp_ref,
+def density_kernel(ext_ref, own_ref, mass_ref, vel_ref, dens_ref, table_ref, amp_ref,
                    feat, right, sums, left, wide):
     rows_y = 8
     zero_tail(feat)
@@ -222,7 +222,7 @@
     lax.fori_loop(0, 8, own_row, 0)
 
 
-def density(ext, own, mass, vel, after):
+def density(ext, own, mass, vel):
     blocks = mass.shape[0]
     vm = pl.BlockSpec(memory_space=pltpu.VMEM)
     return pl.pallas_call(
@@ -232,7 +232,7 @@
             jax.ShapeDtypeStruct((blocks, W, FEATS), BF),
             jax.ShapeDtypeStruct((blocks, 16, 2 * W), BF),
         ),
-        in_specs=[vm] * 5,
+        in_specs=[vm] * 4,
         out_specs=(vm, vm, vm),
         scratch_shapes=[
             pltpu.VMEM((FEATS * 8, W), F32),
@@ -243,7 +243,7 @@
         ],
         compiler_params=pltpu.CompilerParams(vmem_limit_bytes=14 << 20),
         name="density",
-    )(ext, own, mass, vel, after)
+    )(ext, own, mass, vel)
 
 
 def columns_to_lanes(cols):
@@ -334,7 +334,7 @@
     )(partner, arms, world, following)
 
 
-def fluid_kernel(y_ref, table_ref, amp_ref, out_ref, names, names_s, right, acc, sems):
+def fluid_kernel(y_ref, table_ref, amp_ref, after_ref, out_ref, names, names_s, right, acc, sems):
     for t in range(GROUPS):
         zero_tail(right, t * FEATS * 8)
     lane = lax.broadcasted_iota(jnp.int32, (8, W), 1)
@@ -390,12 +390,12 @@
     lax.fori_loop(0, devices // (GROUPS // 2), group, 0)
 
 
-def fluid(spots, table, amp):
+def fluid(spots, table, amp, after):
     vm = pl.BlockSpec(memory_space=pltpu.VMEM)
     return pl.pallas_call(
         fluid_kernel,
         out_shape=jax.ShapeDtypeStruct((2 * W, W), F32),
-        in_specs=[vm] * 3,
+        in_specs=[vm] * 4,
         out_specs=vm,
         scratch_shapes=[
             pltpu.VMEM((W, W), jnp.int32),
@@ -406,7 +406,7 @@
         ],
         compiler_params=pltpu.CompilerParams(vmem_limit_bytes=14 << 20),
         name="fluid",
-    )(spots, table, amp)
+    )(spots, table, amp, after)
 
 
 def combine_kernel(dev_ref, rank_ref, off_ref, vel_ref, got_ref, contact_ref, out_ref):
@@ -519,17 +519,16 @@
     lanes = jnp.arange(width, dtype=jnp.int32)
     live = jnp.where(lanes[None, None, :] < fluid_count[..., None], fluid_mass, 0.0)
     planes = jnp.concatenate([jnp.moveaxis(fluid_pos, 2, 0), live[None]], axis=0)
-    planes = jnp.where(ready, planes, 0.0)
     ext = extended(planes, (("stream", 1), ("span", 2)))
     ext = ext.reshape(4, (rows_x + 2) * (rows_y + 2), width)
-    send = gated(send, ext[0, 0:8] + following[0, 0:8])
+    send = gated(send, ext[0, 0:8])
     got = swap_all(send.reshape(devices, 1, ROWS * width))
-    touch, done = contact(contact_partner.reshape(1, clumps), arms, world, following)
     ext = jnp.pad(ext, ((0, 0), (0, 4), (0, 0)))
     own = planes.reshape(4, blocks, width)
     speed = jnp.moveaxis(fluid_vel, 2, 0).reshape(3, blocks, width)
-    dens, table, amp = density(ext, own, fluid_mass.reshape(blocks, width), speed, done)
-    sums = fluid(got.reshape(devices * ROWS, width), table, amp)
+    dens, table, amp = density(ext, own, fluid_mass.reshape(blocks, width), speed)
+    touch, done = contact(contact_partner.reshape(1, clumps), arms, world, following)
+    sums = fluid(got.reshape(devices * ROWS, width), table, amp, done)
     back = swap_all(sums.reshape(devices, 1, 2 * width)).reshape(2 * devices, width)
     loads = combine(dev, rank, off, vel, back, touch)
     return (dens.reshape(rows_x, rows_y, width), loads)

time: 156 us -> 173 us (1.11)
  waiting for transfers between devices: 9.29 us -> 29.4 us
  blocking collectives: 14.5 us -> 18.5 us
  local copies, waits for them, and re-layouts: 17.1 us -> 13.3 us
  Pallas kernels: 81.9 us -> 78.9 us
    ppermute x1, waiting for transfers between devices: 0.01 us -> 26.2 us  [body(): lax.ppermute(world, AXES, [(i, (i + devices - 1) % devices) for i in rang...]
    all_to_all x1, waiting for transfers between devices: 5.06 us -> 0.01 us  [swap_all(): return lax.all_to_all(array, AXES, split_axis=0, concat_axis=0, tiled=True)]
    unnamed x37 -> x35, local copies, waits for them, and re-layouts: 15.6 us -> 11.1 us
    all_to_all x1, blocking collectives: 14.5 us -> 18.5 us  [swap_all(): return lax.all_to_all(array, AXES, split_axis=0, concat_axis=0, tiled=True)]
    ppermute x2, starting transfers between devices: 7.06 us -> 3.21 us  [extended(): lax.ppermute(head, axis, [((i + 1) % count, i) for i in range(ends)])]
    pallas_call x1, Pallas kernels: 43.3 us -> 40.4 us  [fluid(): pl.pallas_call(fluid_kernel, out_shape=jax.ShapeDtypeStruct((2 * W, W), F...]
    all_to_all x1, starting transfers between devices: 9.71 us -> 11.8 us  [swap_all(): return lax.all_to_all(array, AXES, split_axis=0, concat_axis=0, tiled=True)]
  transfers between devices with their start and end apart: 6 -> 6, of which waited for: 3 -> 2; matrix products, arithmetic and copies ran while one was open for 3% -> 3% of each run, Pallas kernels for 19% -> 22%
where the time goes in v5:
time: 173 us; the launch traced here: 172 us
  Pallas kernels  78.9 us (46%)
  waiting for transfers between devices  29.4 us (17%)
  starting transfers between devices  25.6 us (15%)
  blocking collectives  18.5 us (11%)
  local copies, waits for them, and re-layouts  13.3 us (8%)
  other arithmetic  4.97 us (3%)
    pallas_call x1, Pallas kernels, fluid(): pl.pallas_call(fluid_kernel, out_shape=jax.ShapeDtypeStruct((2 * W, W), F...  40.4 us
    ppermute x1, waiting for transfers between devices, body(): lax.ppermute(world, AXES, [(i, (i + devices - 1) % devices) for i in rang...  26.2 us
    all_to_all x1, blocking collectives, swap_all(): return lax.all_to_all(array, AXES, split_axis=0, concat_axis=0, tiled=True)  18.5 us
    pallas_call x1, Pallas kernels, contact(): pl.pallas_call(contact_kernel, out_shape=(jax.ShapeDtypeStruct((clumps, W...  17.1 us
    pallas_call x1, Pallas kernels, density(): pl.pallas_call(density_kernel, out_shape=(jax.ShapeDtypeStruct((blocks, W...  11.9 us
    all_to_all x1, starting transfers between devices, swap_all(): return lax.all_to_all(array, AXES, split_axis=0, concat_axis=0, tiled=True)  11.8 us
    unnamed x35, local copies, waits for them, and re-layouts  11.1 us
    ppermute x2, starting transfers between devices, extended(): lax.ppermute(tail, axis, [(i, (i + 1) % count) for i in range(ends)])  9.47 us
  transfers between devices with their start and end apart: 6, of which 2 were waited for; matrix products, arithmetic and copies ran while one was open for 3% of the time, Pallas kernels for 22%

profile of v5, /device:TPU:1, one launch (start us, length us, event | category | flops | bytes accessed | tf_op | source)
XLA Modules:
  0.0 172.2 jit_solution(16697236650627639563)
XLA Ops:
  0.6 0.0 copy-start
  0.6 0.9 fusion.1
  1.5 0.7 pad_maximum_fusion.7
  2.3 3.9 %collective-permute-start = (f32[4,1,8,128]{3,2,0,1:T(8,128)S(1)}, f32[4,1,8,128]{3,2,0,1:T(8,128)S(1)}, u32[]{:S(2)}, u32[]{:S(2)}) collective-permute-start(f32[4,1,8,128]{3,2,0,1:T(8,128)S(1)} %get-tuple-element.18), channel_id=1, source_target_pairs={{0,8},{8,16},{16,24},{24,32},{32,40},{40,48},{48,56},{56,64},{64,7... | collective-permute-start | bytes 49160 | tf_op jit(solution)/shard_map/ppermute | solution.py:463
  6.2 1.3 collective-permute-start.1
  7.5 0.0 collective-permute-done
  7.5 3.2 %collective-permute-done.1 = f32[4,1,8,128]{3,2,0,1:T(8,128)S(1)} collective-permute-done((f32[4,1,8,128]{3,2,0,1:T(8,128)S(1)}, f32[4,1,8,128]{3,2,0,1:T(8,128)S(1)}, u32[]{:S(2)}, u32[]{:S(2)}) %collective-permute-start.1) | collective-permute-done | bytes 16416 | tf_op jit(solution)/shard_map/ppermute | solution.py:465
  10.7 1.0 pad_maximum_fusion.5
  11.7 5.5 %collective-permute-start.2 = (f32[4,10,1,128]{3,2,0,1:T(1,128)S(1)}, f32[4,10,1,128]{3,2,0,1:T(1,128)S(1)}, u32[]{:S(2)}, u32[]{:S(2)}) collective-permute-start(f32[4,10,1,128]{3,2,0,1:T(1,128)S(1)} %get-tuple-element.16), channel_id=1, source_target_pairs={{0,1},{1,2},{2,3},{3,4},{4,5},{5,6},{6,7},{8,9},{9,10},{10,11},{11... | collective-permute-start | bytes 61448 | tf_op jit(solution)/shard_map/ppermute | solution.py:463
  17.2 1.9 %collective-permute-start.3 = (f32[4,10,1,128]{3,2,0,1:T(1,128)S(1)}, f32[4,10,1,128]{3,2,0,1:T(1,128)S(1)}, u32[]{:S(2)}, u32[]{:S(2)}) collective-permute-start(f32[4,10,1,128]{3,2,0,1:T(1,128)S(1)} %get-tuple-element.17), channel_id=1, source_target_pairs={{1,0},{2,1},{3,2},{4,3},{5,4},{6,5},{7,6},{9,8},{10,9},{11,10},{12... | collective-permute-start | bytes 61448 | tf_op jit(solution)/shard_map/ppermute | solution.py:465
  19.1 0.7 copy.34
  19.9 0.7 copy.32
  20.6 0.7 copy.33
  21.2 1.1 copy-done.2
  22.4 8.2 %prep.1 = (f32[6272,128]{1,0:T(8,128)S(1)}, s32[1,1024]{1,0:T(1,128)S(1)}) custom-call(s32[1,1024]{1,0:T(1,128)S(1)} %bitcast.51, s32[1,1024]{1,0:T(1,128)S(1)} %bitcast.54, s32[1,1024]{1,0:T(1,128)S(1)} %bitcast.52, f32[3,1024]{1,0:T(4,128)S(1)} %bitcast.48, f32[3,512,128]{2,1,0:T(8,128)S(1)} %bitcast.44), custom_call_target="tpu_custom_call" | custom-call | tf_op jit(solution)/shard_map/prep/pallas_call | solution.py:134
  30.6 0.0 copy-start.1
  30.6 1.6 copy-done.1
  32.3 0.0 collective-permute-done.2
  32.3 0.0 collective-permute-done.3
  32.3 1.0 pad_maximum_fusion
  33.3 0.1 copy.25
  33.4 0.0 copy-start.14
  33.4 0.7 copy-done.14
  34.1 0.6 slice_bitcast_fusion.after_ref
  34.7 11.8 %all-to-all-start = ((f32[128,1,6272]{2,1,0:T(1,128)}), f32[128,1,6272]{2,1,0:T(1,128)S(1)}, u32[]{:S(2)}, u32[]{:S(2)}) async-start(f32[128,1,6272]{2,1,0:T(1,128)} %bitcast.43), calls=%async_computation | async-start | bytes 6422528 | tf_op jit(solution)/shard_map/all_to_all | solution.py:489
  46.4 0.0 copy-start.3
  46.4 0.5 slice.23
  47.6 0.0 copy-done.15
  47.6 1.4 add_select_fusion.world_ref
  49.0 1.1 collective-permute-start.4
  50.2 0.0 copy-done.13
  50.2 0.0 copy-done
  50.2 1.0 pad.4.ext_ref
  51.2 0.0 copy-done.10
  51.2 11.9 %density.1 = (f32[64,128]{1,0:T(8,128)}, bf16[64,128,32]{2,1,0:T(8,128)(2,1)S(1)}, bf16[64,16,256]{2,1,0:T(8,128)(2,1)S(1)}) custom-call(f32[4,104,128]{2,1,0:T(8,128)S(1)} %pad.4.ext_ref, f32[4,64,128]{2,1,0:T(8,128)S(1)} %pad_maximum_fusion.1.own_ref, f32[64,128]{1,0:T(8,128)S(1)} %bitcast.50, f32[3,64,128]{2,1,0:T(8,128)S(1)} %copy_bitcast_fusion.vel_ref), custom_call_target="tpu_custom_call" | custom-call | tf_op jit(solution)/shard_map/density/pallas_call | solution.py:228
  63.1 1.3 copy-done.4
  64.4 0.8 copy-done.6
  65.2 26.2 %collective-permute-done.4.next_ref = f32[3,512,128]{2,1,0:T(8,128)S(1)} collective-permute-done((f32[3,512,128]{2,1,0:T(8,128)S(1)}, f32[3,512,128]{2,1,0:T(8,128)S(1)}, u32[]{:S(2)}, u32[]{:S(2)}) %collective-permute-start.4) | collective-permute-done | bytes 786464 | tf_op jit(solution)/shard_map/ppermute | solution.py:518
  91.5 0.0 copy-done.3
  91.5 17.1 %contact.1 = (f32[512,128]{1,0:T(8,128)S(1)}, f32[8,128]{1,0:T(8,128)S(1)}) custom-call(s32[1,512]{1,0:T(1,128)S(1)} %bitcast.56, f32[3,512,128]{2,1,0:T(8,128)S(1)} %bitcast.45, f32[3,512,128]{2,1,0:T(8,128)S(1)} %add_select_fusion.world_ref, f32[3,512,128]{2,1,0:T(8,128)S(1)} %collective-permute-done.4.next_ref), custom_call_target="tpu_custom_call" | custom-call | tf_op jit(solution)/shard_map/contact/pallas_call | solution.py:319
  108.6 0.7 copy-done.8
  109.3 0.0 all-to-all-done
  109.3 1.6 copy-done.5
  110.9 1.0 copy-done.7
  112.0 40.4 %fluid.1 = f32[256,128]{1,0:T(8,128)S(1)} custom-call(f32[6272,128]{1,0:T(8,128)S(1)} %bitcast.42, bf16[64,128,32]{2,1,0:T(8,128)(2,1)S(1)} %copy-done.5, bf16[64,16,256]{2,1,0:T(8,128)(2,1)S(1)} %copy-done.7, f32[8,128]{1,0:T(8,128)S(1)} %get-tuple-element.14.after_ref), custom_call_target="tpu_custom_call" | custom-call | tf_op jit(solution)/shard_map/fluid/pallas_call | solution.py:395
  152.4 18.5 %all_to_all.10 = f32[128,1,256]{2,1,0:T(1,128)S(1)} all-to-all(f32[128,1,256]{2,1,0:T(1,128)S(1)} %bitcast.47), channel_id=1, replica_groups=mesh['stream'=16,'span'=8] {'stream','span'}, dimensions={0} | all-to-all | bytes 262144 | tf_op jit(solution)/shard_map/all_to_all | solution.py:489
  170.9 0.0 copy-done.11
  170.9 1.3 combine.1
  (19 shorter events, 0.1 us)
Async XLA Ops:
  0.6 49.6 %copy-start = (f32[8,8,3,128]{3,1,2,0:T(8,128)S(1)}, f32[8,8,3,128]{3,1,2,0:T(8,128)}, u32[]{:S(2)}) copy-start(f32[8,8,3,128]{3,1,2,0:T(8,128)} %param.12) | copy-start | bytes 294916
  2.3 5.2 %collective-permute-start = (f32[4,1,8,128]{3,2,0,1:T(8,128)S(1)}, f32[4,1,8,128]{3,2,0,1:T(8,128)S(1)}, u32[]{:S(2)}, u32[]{:S(2)}) collective-permute-start(f32[4,1,8,128]{3,2,0,1:T(8,128)S(1)} %get-tuple-element.18), channel_id=1, source_target_pairs={{0,8},{8,16},{16,24},{24,32},{32,40},{40,48},{48,56},{56,64},{64,7... | collective-permute-start | bytes 49160 | tf_op jit(solution)/shard_map/ppermute | solution.py:463
  6.2 4.5 %collective-permute-start.1 = (f32[4,1,8,128]{3,2,0,1:T(8,128)S(1)}, f32[4,1,8,128]{3,2,0,1:T(8,128)S(1)}, u32[]{:S(2)}, u32[]{:S(2)}) collective-permute-start(f32[4,1,8,128]{3,2,0,1:T(8,128)S(1)} %get-tuple-element.19), channel_id=1, source_target_pairs={{8,0},{16,8},{24,16},{32,24},{40,32},{48,40},{56,48},{64,56},{72,6... | collective-permute-start | bytes 49160 | tf_op jit(solution)/shard_map/ppermute | solution.py:465
  11.7 20.6 %collective-permute-start.2 = (f32[4,10,1,128]{3,2,0,1:T(1,128)S(1)}, f32[4,10,1,128]{3,2,0,1:T(1,128)S(1)}, u32[]{:S(2)}, u32[]{:S(2)}) collective-permute-start(f32[4,10,1,128]{3,2,0,1:T(1,128)S(1)} %get-tuple-element.16), channel_id=1, source_target_pairs={{0,1},{1,2},{2,3},{3,4},{4,5},{5,6},{6,7},{8,9},{9,10},{10,11},{11... | collective-permute-start | bytes 61448 | tf_op jit(solution)/shard_map/ppermute | solution.py:463
  17.2 15.1 %collective-permute-start.3 = (f32[4,10,1,128]{3,2,0,1:T(1,128)S(1)}, f32[4,10,1,128]{3,2,0,1:T(1,128)S(1)}, u32[]{:S(2)}, u32[]{:S(2)}) collective-permute-start(f32[4,10,1,128]{3,2,0,1:T(1,128)S(1)} %get-tuple-element.17), channel_id=1, source_target_pairs={{1,0},{2,1},{3,2},{4,3},{5,4},{6,5},{7,6},{9,8},{10,9},{11,10},{12... | collective-permute-start | bytes 61448 | tf_op jit(solution)/shard_map/ppermute | solution.py:465
  21.2 1.1 copy-start.2
  30.6 1.7 copy-start.1
  33.4 0.7 copy-start.14
  34.6 13.0 %copy-start.15 = (f32[512,3]{0,1:T(4,128)S(1)}, f32[512,3]{0,1:T(4,128)}, u32[]{:S(2)}) copy-start(f32[512,3]{0,1:T(4,128)} %param.15) | copy-start | bytes 18436
  34.6 15.5 %copy-start.13 = (f32[8,8,3,128]{3,1,2,0:T(8,128)S(1)}, f32[8,8,3,128]{3,1,2,0:T(8,128)}, u32[]{:S(2)}) copy-start(f32[8,8,3,128]{3,1,2,0:T(8,128)} %param.11) | copy-start | bytes 294916
  34.7 16.5 %copy-start.10 = (f32[8,8,128]{2,1,0:T(8,128)S(1)}, f32[8,8,128]{2,1,0:T(8,128)}, u32[]{:S(2)}) copy-start(f32[8,8,128]{2,1,0:T(8,128)} %param.13) | copy-start | bytes 98308
  34.7 56.8 %copy-start.12 = (s32[512]{0:T(512)S(1)}, s32[512]{0:T(512)}, u32[]{:S(2)}) copy-start(s32[512]{0:T(512)} %param.21) | copy-start | bytes 6148
  34.7 74.7 %all-to-all-start = ((f32[128,1,6272]{2,1,0:T(1,128)}), f32[128,1,6272]{2,1,0:T(1,128)S(1)}, u32[]{:S(2)}, u32[]{:S(2)}) async-start(f32[128,1,6272]{2,1,0:T(1,128)} %bitcast.43), calls=%async_computation | async-start | bytes 6422528 | tf_op jit(solution)/shard_map/all_to_all | solution.py:489
  46.4 45.0 %copy-start.3 = (f32[512,3,128]{2,0,1:T(8,128)S(1)}, f32[512,3,128]{2,0,1:T(8,128)}, u32[]{:S(2)}) copy-start(f32[512,3,128]{2,0,1:T(8,128)} %param.17) | copy-start | bytes 2359300
  49.0 42.4 %collective-permute-start.4 = (f32[3,512,128]{2,1,0:T(8,128)S(1)}, f32[3,512,128]{2,1,0:T(8,128)S(1)}, u32[]{:S(2)}, u32[]{:S(2)}) collective-permute-start(f32[3,512,128]{2,1,0:T(8,128)S(1)} %add_select_fusion.world_ref), channel_id=1, source_target_pairs={{0,127},{1,0},{2,1},{3,2},{4,3},{5,4},{6,5},{7,6},{8,7},{9,8},{10,... | collective-permute-start | bytes 2359304 | tf_op jit(solution)/shard_map/ppermute | solution.py:518
  63.1 1.3 copy-start.4
  64.4 0.8 copy-start.6
  91.5 79.4 %copy-start.11 = (f32[512,3]{0,1:T(4,128)S(1)}, f32[512,3]{0,1:T(4,128)}, u32[]{:S(2)}) copy-start(f32[512,3]{0,1:T(4,128)} %param.16) | copy-start | bytes 18436
  108.6 0.7 copy-start.8
  109.3 1.6 copy-start.5
  110.9 1.0 copy-start.7
  112.0 58.9 %copy-start.9 = (f32[512,128]{1,0:T(8,128)S(1)}, f32[512,128]{1,0:T(8,128)}, u32[]{:S(2)}) copy-start(f32[512,128]{1,0:T(8,128)} %copy-done.8) | copy-start | bytes 786436

commit v6 on v3

--- a/solution.py
+++ b/solution.py
@@ -21,7 +21,7 @@
 FEATS = 32
 ROWS = 49
 UNROLL = 4
-GROUPS = 16
+GROUPS = 32
 DEAD = -30000.0
 BF = jnp.bfloat16
 F32 = jnp.float32

time: 152 us -> 149 us (0.980)
  Pallas kernels: 82 us -> 79.1 us
    pallas_call x1, Pallas kernels: 43.4 us -> 40.6 us  [fluid(): pl.pallas_call(fluid_kernel, out_shape=jax.ShapeDtypeStruct((2 * W, W), F...]
where the time goes in v6:
time: 149 us; the launch traced here: 148 us
  Pallas kernels  79.1 us (53%)
  starting transfers between devices  24.4 us (16%)
  local copies, waits for them, and re-layouts  16.6 us (11%)
  blocking collectives  14.7 us (10%)
  waiting for transfers between devices  7.62 us (5%)
  other arithmetic  4.71 us (3%)
    pallas_call x1, Pallas kernels, fluid(): pl.pallas_call(fluid_kernel, out_shape=jax.ShapeDtypeStruct((2 * W, W), F...  40.6 us
    pallas_call x1, Pallas kernels, contact(): pl.pallas_call(contact_kernel, out_shape=(jax.ShapeDtypeStruct((clumps, W...  17.1 us
    unnamed x41, local copies, waits for them, and re-layouts  15.5 us
    all_to_all x1, blocking collectives, swap_all(): return lax.all_to_all(array, AXES, split_axis=0, concat_axis=0, tiled=True)  14.7 us
    pallas_call x1, Pallas kernels, density(): pl.pallas_call(density_kernel, out_shape=(jax.ShapeDtypeStruct((blocks, W...  11.9 us
    pallas_call x1, Pallas kernels, prep(): pl.pallas_call(prep_kernel, out_shape=(jax.ShapeDtypeStruct((W * ROWS, W)...  8.24 us
    all_to_all x1, starting transfers between devices, swap_all(): return lax.all_to_all(array, AXES, split_axis=0, concat_axis=0, tiled=True)  8.02 us
    ppermute x2, starting transfers between devices, extended(): lax.ppermute(tail, axis, [(i, (i + 1) % count) for i in range(ends)])  7.86 us
  transfers between devices with their start and end apart: 6, of which 2 were waited for; matrix products, arithmetic and copies ran while one was open for 4% of the time, Pallas kernels for 25%

profile of v6, /device:TPU:1, one launch (start us, length us, event | category | flops | bytes accessed | tf_op | source)
XLA Modules:
  0.0 148.0 jit_solution(18183398614961214746)
XLA Ops:
  0.6 0.0 copy-start
  0.6 1.4 broadcast_add_fusion.world_ref
  2.1 0.0 copy-start.4
  2.1 1.5 %collective-permute-start.4 = (f32[3,512,128]{2,1,0:T(8,128)S(1)}, f32[3,512,128]{2,1,0:T(8,128)S(1)}, u32[]{:S(2)}, u32[]{:S(2)}) collective-permute-start(f32[3,512,128]{2,1,0:T(8,128)S(1)} %broadcast_add_fusion.world_ref), channel_id=1, source_target_pairs={{0,127},{1,0},{2,1},{3,2},{4,3},{5,4},{6,5},{7,6},{8,7},{9,8},{10,... | collective-permute-start | bytes 2359304 | tf_op jit(solution)/shard_map/ppermute | solution.py:508
  3.6 0.8 fusion.1
  4.4 0.7 pad_maximum_fusion.4
  5.2 3.2 %collective-permute-start = (f32[4,1,8,128]{3,2,0,1:T(8,128)S(1)}, f32[4,1,8,128]{3,2,0,1:T(8,128)S(1)}, u32[]{:S(2)}, u32[]{:S(2)}) collective-permute-start(f32[4,1,8,128]{3,2,0,1:T(8,128)S(1)} %get-tuple-element.28), channel_id=1, source_target_pairs={{0,8},{8,16},{16,24},{24,32},{32,40},{40,48},{48,56},{56,64},{64,7... | collective-permute-start | bytes 49160 | tf_op jit(solution)/shard_map/ppermute | solution.py:475
  8.4 1.3 collective-permute-start.1
  9.7 0.7 copy.29
  10.4 0.0 collective-permute-done
  10.4 2.7 %collective-permute-done.1 = f32[4,1,8,128]{3,2,0,1:T(8,128)S(1)} collective-permute-done((f32[4,1,8,128]{3,2,0,1:T(8,128)S(1)}, f32[4,1,8,128]{3,2,0,1:T(8,128)S(1)}, u32[]{:S(2)}, u32[]{:S(2)}) %collective-permute-start.1) | collective-permute-done | bytes 16416 | tf_op jit(solution)/shard_map/ppermute | solution.py:477
  13.1 0.9 pad_maximum_fusion.1
  14.0 4.7 %collective-permute-start.2 = (f32[4,10,1,128]{3,2,0,1:T(1,128)S(1)}, f32[4,10,1,128]{3,2,0,1:T(1,128)S(1)}, u32[]{:S(2)}, u32[]{:S(2)}) collective-permute-start(f32[4,10,1,128]{3,2,0,1:T(1,128)S(1)} %get-tuple-element.26), channel_id=1, source_target_pairs={{0,1},{1,2},{2,3},{3,4},{4,5},{5,6},{6,7},{8,9},{9,10},{10,11},{11... | collective-permute-start | bytes 61448 | tf_op jit(solution)/shard_map/ppermute | solution.py:475
  18.7 5.7 %collective-permute-start.3 = (f32[4,10,1,128]{3,2,0,1:T(1,128)S(1)}, f32[4,10,1,128]{3,2,0,1:T(1,128)S(1)}, u32[]{:S(2)}, u32[]{:S(2)}) collective-permute-start(f32[4,10,1,128]{3,2,0,1:T(1,128)S(1)} %get-tuple-element.27), channel_id=1, source_target_pairs={{1,0},{2,1},{3,2},{4,3},{5,4},{6,5},{7,6},{9,8},{10,9},{11,10},{12... | collective-permute-start | bytes 61448 | tf_op jit(solution)/shard_map/ppermute | solution.py:477
  24.5 0.7 copy.30
  25.1 0.7 copy.31
  25.9 1.1 copy-done.1
  27.0 8.2 %prep.1 = (f32[6272,128]{1,0:T(8,128)S(1)}, s32[1,1024]{1,0:T(1,128)S(1)}) custom-call(s32[1,1024]{1,0:T(1,128)S(1)} %bitcast.48, s32[1,1024]{1,0:T(1,128)S(1)} %bitcast.52, s32[1,1024]{1,0:T(1,128)S(1)} %bitcast.49, f32[3,1024]{1,0:T(4,128)S(1)} %bitcast.45, f32[3,512,128]{2,1,0:T(8,128)S(1)} %bitcast.40), custom_call_target="tpu_custom_call" | custom-call | tf_op jit(solution)/shard_map/prep/pallas_call | solution.py:134
  35.2 0.0 copy-done.4
  35.3 0.0 copy-start.3
  35.3 1.6 %copy-done.3 = f32[6272,128]{1,0:T(8,128)} copy-done((f32[6272,128]{1,0:T(8,128)}, f32[6272,128]{1,0:T(8,128)S(1)}, u32[]{:S(2)}) %copy-start.3) | copy-done | bytes 3211288
  36.9 0.0 collective-permute-done.2
  36.9 0.0 collective-permute-done.3
  36.9 0.8 pad_maximum_fusion
  37.7 0.0 collective-permute-done.4.next_ref
  37.7 0.9 copy-done.8
  38.6 8.0 %all-to-all-start = ((f32[128,1,6272]{2,1,0:T(1,128)}), f32[128,1,6272]{2,1,0:T(1,128)S(1)}, u32[]{:S(2)}, u32[]{:S(2)}) async-start(f32[128,1,6272]{2,1,0:T(1,128)} %bitcast.42), calls=%async_computation | async-start | bytes 6422528 | tf_op jit(solution)/shard_map/all_to_all | solution.py:485
  46.7 0.0 copy-done.18
  46.7 0.0 copy-done
  46.7 1.1 copy.23
  47.8 0.0 copy-done.14
  47.8 11.9 %density.1 = (f32[64,128]{1,0:T(8,128)}, bf16[64,128,32]{2,1,0:T(8,128)(2,1)S(1)}, bf16[64,16,256]{2,1,0:T(8,128)(2,1)S(1)}) custom-call(f32[4,104,128]{2,1,0:T(8,128)S(1)} %pad.4.ext_ref, f32[4,64,128]{2,1,0:T(8,128)S(1)} %pad_maximum_fusion.2.own_ref, f32[64,128]{1,0:T(8,128)S(1)} %bitcast.47, f32[3,64,128]{2,1,0:T(8,128)S(1)} %copy_bitcast_fusion.vel_ref), custom_call_target="tpu_custom_call" | custom-call | tf_op jit(solution)/shard_map/density/pallas_call | solution.py:228
  59.8 1.3 copy-done.6
  61.1 0.8 copy-done.10
  61.9 0.0 copy-done.17
  61.9 1.1 copy-done.2
  63.0 1.1 copy-done.5
  64.2 1.1 copy-done.9
  65.3 0.8 copy-done.15
  66.0 17.1 %contact.1 = (f32[512,128]{1,0:T(8,128)S(1)}, f32[8,128]{1,0:T(8,128)S(1)}) custom-call(s32[1,512]{1,0:T(1,128)S(1)} %bitcast.54, f32[3,512,128]{2,1,0:T(8,128)S(1)} %bitcast.41, f32[3,512,128]{2,1,0:T(8,128)S(1)} %copy-done.5, f32[3,512,128]{2,1,0:T(8,128)S(1)} %copy-done.9, f32[64,128]{1,0:T(8,128)S(1)} %copy-done.15), custom_call_target="tpu_custom_call" | custom-call | tf_op jit(solution)/shard_map/contact/pallas_call | solution.py:319
  83.2 0.7 copy-done.12
  83.9 4.9 %all-to-all-done = f32[128,1,6272]{2,1,0:T(1,128)S(1)} async-done(((f32[128,1,6272]{2,1,0:T(1,128)}), f32[128,1,6272]{2,1,0:T(1,128)S(1)}, u32[]{:S(2)}, u32[]{:S(2)}) %all-to-all-start) | async-done | bytes 3211296 | tf_op jit(solution)/shard_map/all_to_all | solution.py:485
  88.8 1.6 %copy-done.7 = bf16[64,128,32]{2,1,0:T(8,128)(2,1)S(1)} copy-done((bf16[64,128,32]{2,1,0:T(8,128)(2,1)S(1)}, bf16[64,128,32]{2,1,0:T(8,128)(2,1)}, u32[]{:S(2)}) %copy-start.7) | copy-done | bytes 524312
  90.4 1.0 copy-done.11
  91.4 40.6 %fluid.1 = f32[256,128]{1,0:T(8,128)S(1)} custom-call(f32[6272,128]{1,0:T(8,128)S(1)} %bitcast.39, bf16[64,128,32]{2,1,0:T(8,128)(2,1)S(1)} %copy-done.7, bf16[64,16,256]{2,1,0:T(8,128)(2,1)S(1)} %copy-done.11, f32[8,128]{1,0:T(8,128)S(1)} %get-tuple-element.24.after_ref), custom_call_target="tpu_custom_call" | custom-call | tf_op jit(solution)/shard_map/fluid/pallas_call | solution.py:405
  132.0 14.7 %all_to_all.10 = f32[128,1,256]{2,1,0:T(1,128)S(1)} all-to-all(f32[128,1,256]{2,1,0:T(1,128)S(1)} %bitcast.44), channel_id=1, replica_groups=mesh['stream'=16,'span'=8] {'stream','span'}, dimensions={0} | all-to-all | bytes 262144 | tf_op jit(solution)/shard_map/all_to_all | solution.py:485
  146.6 0.0 copy-done.16
  146.7 1.3 combine.1
  (23 shorter events, 0.1 us)
Async XLA Ops:
  0.6 46.1 %copy-start = (f32[8,8,3,128]{3,1,2,0:T(8,128)S(1)}, f32[8,8,3,128]{3,1,2,0:T(8,128)}, u32[]{:S(2)}) copy-start(f32[8,8,3,128]{3,1,2,0:T(8,128)} %param.12) | copy-start | bytes 294916
  2.1 33.1 %copy-start.4 = (f32[3,512,128]{2,1,0:T(8,128)}, f32[3,512,128]{2,1,0:T(8,128)S(1)}, u32[]{:S(2)}) copy-start(f32[3,512,128]{2,1,0:T(8,128)S(1)} %broadcast_add_fusion.world_ref) | copy-start | bytes 2359300
  2.1 35.6 %collective-permute-start.4 = (f32[3,512,128]{2,1,0:T(8,128)S(1)}, f32[3,512,128]{2,1,0:T(8,128)S(1)}, u32[]{:S(2)}, u32[]{:S(2)}) collective-permute-start(f32[3,512,128]{2,1,0:T(8,128)S(1)} %broadcast_add_fusion.world_ref), channel_id=1, source_target_pairs={{0,127},{1,0},{2,1},{3,2},{4,3},{5,4},{6,5},{7,6},{8,7},{9,8},{10,... | collective-permute-start | bytes 2359304 | tf_op jit(solution)/shard_map/ppermute | solution.py:508
  5.2 5.2 %collective-permute-start = (f32[4,1,8,128]{3,2,0,1:T(8,128)S(1)}, f32[4,1,8,128]{3,2,0,1:T(8,128)S(1)}, u32[]{:S(2)}, u32[]{:S(2)}) collective-permute-start(f32[4,1,8,128]{3,2,0,1:T(8,128)S(1)} %get-tuple-element.28), channel_id=1, source_target_pairs={{0,8},{8,16},{16,24},{24,32},{32,40},{40,48},{48,56},{56,64},{64,7... | collective-permute-start | bytes 49160 | tf_op jit(solution)/shard_map/ppermute | solution.py:475
  8.4 4.7 %collective-permute-start.1 = (f32[4,1,8,128]{3,2,0,1:T(8,128)S(1)}, f32[4,1,8,128]{3,2,0,1:T(8,128)S(1)}, u32[]{:S(2)}, u32[]{:S(2)}) collective-permute-start(f32[4,1,8,128]{3,2,0,1:T(8,128)S(1)} %get-tuple-element.29), channel_id=1, source_target_pairs={{8,0},{16,8},{24,16},{32,24},{40,32},{48,40},{56,48},{64,56},{72,6... | collective-permute-start | bytes 49160 | tf_op jit(solution)/shard_map/ppermute | solution.py:477
  14.0 22.9 %collective-permute-start.2 = (f32[4,10,1,128]{3,2,0,1:T(1,128)S(1)}, f32[4,10,1,128]{3,2,0,1:T(1,128)S(1)}, u32[]{:S(2)}, u32[]{:S(2)}) collective-permute-start(f32[4,10,1,128]{3,2,0,1:T(1,128)S(1)} %get-tuple-element.26), channel_id=1, source_target_pairs={{0,1},{1,2},{2,3},{3,4},{4,5},{5,6},{6,7},{8,9},{9,10},{10,11},{11... | collective-permute-start | bytes 61448 | tf_op jit(solution)/shard_map/ppermute | solution.py:475
  18.7 18.2 %collective-permute-start.3 = (f32[4,10,1,128]{3,2,0,1:T(1,128)S(1)}, f32[4,10,1,128]{3,2,0,1:T(1,128)S(1)}, u32[]{:S(2)}, u32[]{:S(2)}) collective-permute-start(f32[4,10,1,128]{3,2,0,1:T(1,128)S(1)} %get-tuple-element.27), channel_id=1, source_target_pairs={{1,0},{2,1},{3,2},{4,3},{5,4},{6,5},{7,6},{9,8},{10,9},{11,10},{12... | collective-permute-start | bytes 61448 | tf_op jit(solution)/shard_map/ppermute | solution.py:477
  25.9 1.1 copy-start.1
  35.3 1.6 %copy-start.3 = (f32[6272,128]{1,0:T(8,128)}, f32[6272,128]{1,0:T(8,128)S(1)}, u32[]{:S(2)}) copy-start(f32[6272,128]{1,0:T(8,128)S(1)} %get-tuple-element.20) | copy-start | bytes 9633796
  37.7 0.9 copy-start.8
  38.6 8.0 %copy-start.18 = (f32[8,8,3,128]{3,1,2,0:T(8,128)S(1)}, f32[8,8,3,128]{3,1,2,0:T(8,128)}, u32[]{:S(2)}) copy-start(f32[8,8,3,128]{3,1,2,0:T(8,128)} %param.11) | copy-start | bytes 294916
  38.6 9.2 %copy-start.14 = (f32[8,8,128]{2,1,0:T(8,128)S(1)}, f32[8,8,128]{2,1,0:T(8,128)}, u32[]{:S(2)}) copy-start(f32[8,8,128]{2,1,0:T(8,128)} %param.13) | copy-start | bytes 98308
  38.6 23.3 %copy-start.17 = (s32[512]{0:T(512)S(1)}, s32[512]{0:T(512)}, u32[]{:S(2)}) copy-start(s32[512]{0:T(512)} %param.21) | copy-start | bytes 6148
  38.6 50.2 %all-to-all-start = ((f32[128,1,6272]{2,1,0:T(1,128)}), f32[128,1,6272]{2,1,0:T(1,128)S(1)}, u32[]{:S(2)}, u32[]{:S(2)}) async-start(f32[128,1,6272]{2,1,0:T(1,128)} %bitcast.42), calls=%async_computation | async-start | bytes 6422528 | tf_op jit(solution)/shard_map/all_to_all | solution.py:485
  59.8 1.4 copy-start.6
  61.1 0.8 copy-start.10
  61.9 1.1 copy-start.2
  63.0 1.1 copy-start.5
  64.2 1.1 copy-start.9
  65.3 0.8 copy-start.15
  66.0 80.6 %copy-start.16 = (f32[512,3]{0,1:T(4,128)S(1)}, f32[512,3]{0,1:T(4,128)}, u32[]{:S(2)}) copy-start(f32[512,3]{0,1:T(4,128)} %param.16) | copy-start | bytes 18436
  83.2 0.7 copy-start.12
  88.8 1.6 %copy-start.7 = (bf16[64,128,32]{2,1,0:T(8,128)(2,1)S(1)}, bf16[64,128,32]{2,1,0:T(8,128)(2,1)}, u32[]{:S(2)}) copy-start(bf16[64,128,32]{2,1,0:T(8,128)(2,1)} %copy-done.6) | copy-start | bytes 1572868
  90.4 1.0 copy-start.11
  91.4 55.2 %copy-start.13 = (f32[512,128]{1,0:T(8,128)S(1)}, f32[512,128]{1,0:T(8,128)}, u32[]{:S(2)}) copy-start(f32[512,128]{1,0:T(8,128)} %copy-done.12) | copy-start | bytes 786436
